TPU v7x, 32 devices: a whole 2x2x4 slice. The times are simulated.
32 devices in a mesh: group: 8 (over y, x, core), seq: 4 (over z).
Axes of the slice: x: 2, y: 2, z: 4, core: 2. Of those that a mesh axis runs over, the one named last changes fastest.
Arguments:
- latent: float32 [16, 1024, 64], P('group', 'seq'), may hold values from -6 to 6
- margin_len: int32 [15], replicated, may hold values from 1 to 512, 5760 in all
- in_weight: bfloat16 [64, 1536], replicated, may hold values from -0.75 to 0.75
- norm_gain: float32 [1536], replicated, may hold values from 0.1 to 1.9
- qkv_weight: bfloat16 [3, 1536, 1024], P(None, None, 'seq'), may hold values from -0.15625 to 0.15625
- out_weight: bfloat16 [1024, 1536], P('seq'), may hold values from -0.1875 to 0.1875
- final_gain: float32 [1536], replicated, may hold values from 0.1 to 1.9
- head_out: bfloat16 [1536, 64], replicated, may hold values from -0.15625 to 0.15625
Outputs:
- next_latent: float32 [16, 1024, 64], P('group', 'seq')
Inputs may be any that keep to these rules, and one draw needn't show every extreme that they name: `margin_len`: the lengths sum to 15 * (384) and the largest is exactly 512.
All inputs are finite; a program needn't handle non-finite values.
Results may differ from a plain program's by a relative error of at most 0.0024.
Values may be sent and summed in bfloat16 or wider, within the bound.
No kernel may reach another device: no remote copies, remote signals or barrier semaphores. Data moves between devices by JAX's collectives and lax.ppermute only.
A program may use at most 128 MiB of HBM per device.

v0:
```python
import functools
import math

import jax
import jax.numpy as jnp
from jax import lax
from jax.experimental import pallas as pl
from jax.experimental.pallas import tpu as pltpu
from jax.sharding import PartitionSpec as P

HDIM = 64
OVMAX = 512
LANES = 128
QUAD = 4 * HDIM
STEP = -0.5
F32 = jnp.float32
BF16 = jnp.bfloat16
VMEM = pl.BlockSpec(memory_space=pltpu.VMEM)
SMEM = pl.BlockSpec(memory_space=pltpu.SMEM)


def iota(shape, dim):
    return lax.broadcasted_iota(jnp.int32, shape, dim)


def matmul(lhs, rhs):
    return jnp.dot(lhs, rhs, preferred_element_type=F32)


def matmul_nt(lhs, rhs, precision=None):
    return lax.dot_general(lhs, rhs, (((1,), (1,)), ((), ())), precision=precision, preferred_element_type=F32)


def split(value):
    high = value.astype(BF16)
    return high, (value - high.astype(F32)).astype(BF16)


def margin_at(margin_ref, index):
    last = margin_ref.shape[0]
    length = margin_ref[jnp.clip(index, 0, last - 1)]
    return jnp.where((index >= 0) & (index < last), length, 0)


def fold_kernel(shares, in_ref, gain_ref, qkv_ref, out_ref, map_ref, back_ref, part_ref, gram_ref):
    weight = in_ref[...].astype(F32)
    channels, depth = weight.shape
    width = out_ref.shape[0]
    centered = weight - jnp.mean(weight, axis=-1, keepdims=True)
    high, low = split(centered * gain_ref[...])
    both = jnp.concatenate([high, low], axis=0)

    def folded(which):
        product = matmul(both, qkv_ref[which])
        return product[:channels] + product[channels:]

    map_ref[...] = jnp.concatenate([folded(0), folded(1)], axis=0).T.astype(BF16)
    values = folded(2)
    tiled = jnp.concatenate([values] * (width // HDIM), axis=0)
    same = iota((width, width), 0) // channels == iota((width, width), 1) // HDIM
    high, low = split(jnp.where(same, tiled, 0.0))
    back_ref[...] = (matmul(high, out_ref[...]) + matmul(low, out_ref[...])).astype(BF16)
    rows = width // shares
    sub = lax.rem(lax.axis_index("group"), shares)
    part_ref[...] = back_ref[pl.ds(pl.multiple_of(sub * rows, rows), rows), :]
    gram = matmul_nt(centered, centered, lax.Precision.HIGHEST) * (1.0 / depth)
    for i in range(3):
        piece = gram.astype(BF16)
        gram_ref[i] = piece
        gram = gram - piece.astype(F32)


def attend_kernel(count, window, margin_ref, *refs):
    piece_refs, refs = refs[:count], refs[count:]
    next_refs = piece_refs
    if window:
        next_refs, refs = [refs[0].at[k] for k in range(count)], refs[1:]
    map_refs, refs = refs[:count], refs[count:]
    gram_ref, sum_ref, own_ref, slot_scr, next_scr, win_scr, map_scr, key_scr, query_scr, p_scr, even_scr, odd_scr = refs
    total = win_scr.shape[0]
    channels = gram_ref.shape[-1]
    share = total // count
    width = map_refs[0].shape[0]
    low = total - OVMAX
    group_pos = lax.axis_index("group")
    seq_pos = lax.axis_index("seq")
    over_len = margin_at(margin_ref, 2 * group_pos + window)
    own = total - over_len

    next_scr[:OVMAX, :] = jnp.zeros((OVMAX, LANES), F32)
    for k in range(count):
        source = lax.rem(seq_pos + (count - k), count) * share
        at = pl.ds(pl.multiple_of(source, share), share)
        after = pl.ds(pl.multiple_of(source + OVMAX, share), share)
        slot = piece_refs[k][...].astype(F32)
        slot_scr[at, :] = pltpu.roll(slot, channels, 1) if window else slot
        following = next_refs[k][...].astype(F32)
        next_scr[after, :] = following if window else pltpu.roll(following, channels, 1)
        map_scr[k * width : (k + 1) * width, :] = map_refs[k][...]
    left = iota((OVMAX, LANES), 1) < channels
    for start in range(0, total, OVMAX):
        rows = slot_scr[start : start + OVMAX, :]
        if start >= low:
            tail = next_scr[pl.ds(over_len + (start - low), OVMAX), :]
            rows = jnp.where(iota(rows.shape, 0) + start < own, rows, tail)
        win_scr[start : start + OVMAX, :] = jnp.where(left, rows, 0.0).astype(BF16)

    win = win_scr[...]
    mine = win_scr[pl.ds(pl.multiple_of(seq_pos * share, share), share), :]
    own_ref[...] = mine

    def variance(tokens):
        bent = sum(matmul(tokens[:, :channels], gram_ref[i]) for i in range(3))
        return jnp.sum(bent * tokens[:, :channels].astype(F32), axis=-1, keepdims=True) + 1e-05

    scaled = win.astype(F32) * lax.rsqrt(variance(win))
    turned = pltpu.roll(scaled, channels, 1)
    position = iota((total, LANES), 0)
    counted = (position >= jnp.minimum(own, total - 1)).astype(F32)
    left = iota((total, LANES), 1) < channels
    even_scr[:, :LANES] = jnp.where(left, scaled, turned * counted).astype(BF16)
    even_scr[:, LANES:] = jnp.where(left, 1.0, counted).astype(BF16)
    odd_scr[:, :LANES] = jnp.where(left, scaled * counted, turned).astype(BF16)
    odd_scr[:, LANES:] = jnp.where(left, counted, 1.0).astype(BF16)

    identity = jnp.where(iota((channels, channels), 0) == iota((channels, channels), 1), 1.0, 0.0).astype(BF16)
    forms = jnp.concatenate([gram_ref[0], gram_ref[1], gram_ref[2], identity], axis=0)
    bent = matmul_nt(forms, win[:, :channels])
    sides = [bent[i * channels : (i + 1) * channels] for i in range(4)]
    key_eps = (jnp.sum((sides[0] + sides[1] + sides[2]) * sides[3], axis=0, keepdims=True) + 1e-05) * 1e-06
    query_eps = variance(mine) * 1e-06

    win_right = pltpu.roll(win.astype(F32), channels, 1).astype(BF16)
    one_head = iota((QUAD, QUAD), 0) // HDIM == iota((QUAD, QUAD), 1) // HDIM
    spread = jnp.where(one_head, 1.0 / HDIM, 0.0).astype(BF16)
    head_of = iota((share, QUAD), 1) // HDIM
    quads = map_scr.shape[0] // QUAD
    scale = HDIM ** (-0.5) * math.log2(math.e)
    tile = min(total, 256)
    left = iota((share, LANES), 1) < channels
    for quad in range(quads):
        maps = map_scr[quad * QUAD : (quad + 1) * QUAD, :]
        keys = matmul_nt(maps, win_right).reshape(4, HDIM, total)
        norm = jnp.mean(keys * keys, axis=1, keepdims=True)
        keys = keys * lax.rsqrt(norm + key_eps[None])
        key_scr[quad % 2] = keys.reshape(QUAD, total).astype(BF16)
        queries = matmul_nt(mine, maps)
        high, rest = split(queries * queries)
        queries = (queries * lax.rsqrt(matmul(high, spread) + matmul(rest, spread) + query_eps)).astype(BF16)
        for i, head in enumerate((0, 2, 1, 3)):
            query_scr[quad % 2, i * share : (i + 1) * share, :] = jnp.where(
                head_of == head, queries, jnp.zeros_like(queries)
            )
        for start in range(0, total, tile):
            scores = matmul(query_scr[quad % 2], key_scr[quad % 2, :, start : start + tile])
            p_scr[quad % 2, :, start : start + tile] = jnp.exp2(scores * scale).astype(BF16)
        even = matmul(p_scr[quad % 2, : 2 * share, :], even_scr[...])
        odd = matmul(p_scr[quad % 2, 2 * share :, :], odd_scr[...])
        even = even[:, :LANES] / even[:, LANES:]
        odd = odd[:, :LANES] / odd[:, LANES:]
        for pair in range(2):
            rows = slice(pair * share, (pair + 1) * share)
            at = slice(quad * QUAD + pair * LANES, quad * QUAD + (pair + 1) * LANES)
            sum_ref[:share, at] = jnp.where(left, even[rows], odd[rows]).astype(BF16)
            sum_ref[share:, at] = pltpu.roll(jnp.where(left, odd[rows], even[rows]), HDIM, 1).astype(BF16)


def finish_kernel(count, shares, high, margin_ref, *refs):
    sum_refs, own_refs = refs[:2], refs[2:4]
    in_ref, gain_ref, head_ref, back_ref, far_ref, near_ref, rows_ref, packed_first, packed_second, all_scr, mixed_scr, final_scr, head_scr = refs[4:]
    width, depth = back_ref.shape
    share = own_refs[0].shape[0]
    channels = in_ref.shape[0]
    total = share * count
    part = width // shares
    group_pos = lax.axis_index("group")
    seq_pos = lax.axis_index("seq")
    sub = lax.rem(group_pos, shares)
    all_scr[:width, :] = back_ref[...]
    for i, m in enumerate(high):
        for near, ref in ((0, far_ref), (1, near_ref)):
            place = jnp.bitwise_xor(sub, m ^ near) * part
            for k in range(1, count):
                all_scr[pl.ds(pl.multiple_of(place + k * width, part), part), :] = ref[i, k - 1]
    head_scr[...] = jnp.zeros_like(head_scr)
    head_scr[:, :channels] = head_ref[...]
    tile = 256
    chunk = min(128, share)
    for window in range(2):
        for start in range(0, depth, tile):
            at = slice(start, start + tile)
            inputs = matmul(own_refs[window][:, :channels], in_ref[:, at])
            added = matmul(sum_refs[window][...], all_scr[:, at])
            mixed_scr[window, :share, at] = added[:share] + inputs
            mixed_scr[window, share:, at] = added[share:] + inputs
        for start in range(0, 2 * share, chunk):
            at = slice(start, start + chunk)
            mixed = mixed_scr[window, at, :]
            centered = mixed - jnp.mean(mixed, axis=-1, keepdims=True)
            variance = jnp.mean(centered * centered, axis=-1, keepdims=True)
            final_scr[window, at, :] = (centered * lax.rsqrt(variance + 1e-05) * gain_ref[...]).astype(BF16)
        score = matmul(final_scr[window], head_scr[...])
        own = total - margin_at(margin_ref, 2 * group_pos + window)
        position = iota((share, LANES), 0) + seq_pos * share
        score = score[:share] - jnp.where(position >= own, score[share:], 0.0)
        rows_ref[window] = score[:, :channels]
        packed_ref = packed_second if window else packed_first
        packed_ref[...] = (score[: share // 2] + pltpu.roll(score[share // 2 :], channels, 1)).astype(BF16)


def combine_kernel(count, deltas, margin_ref, latent_ref, rows_ref, *refs):
    out_ref, tail_scr = refs[2 * len(deltas) :]
    share, channels = latent_ref.shape[1:]
    total = share * count
    group_pos = lax.axis_index("group")
    seq_pos = lax.axis_index("seq")
    for slot in range(2):
        before = margin_at(margin_ref, 2 * group_pos + slot - 1)
        own = total - margin_at(margin_ref, 2 * group_pos + slot)
        tail_scr[...] = jnp.zeros_like(tail_scr)
        for delta, ref in zip(deltas, refs[slot * len(deltas) : (slot + 1) * len(deltas)]):
            row = (seq_pos + delta) * share - (total - OVMAX)
            for half in range(2):
                value = ref[...].astype(F32)
                value = pltpu.roll(value, channels, 1) if half else value
                at = pl.ds(pl.multiple_of(row + half * (share // 2), share // 2), share // 2)
                tail_scr[at, :] = value
        moved = tail_scr[pl.ds(OVMAX - before + seq_pos * share, share), :]
        score = rows_ref[slot] + moved[:, :channels]
        keep = iota(score.shape, 0) + seq_pos * share < own
        out_ref[slot] = jnp.where(keep, latent_ref[slot] + STEP * score, 0.0)


def body(latent, margin_len, in_weight, norm_gain, qkv_weight, out_weight, final_gain, head_out):
    count = lax.axis_size("seq")
    groups = lax.axis_size("group")
    share, channels = latent.shape[1:]
    total = share * count
    width, depth = out_weight.shape
    full = width * count
    shares = min(groups, width // 16)
    high = range(0, shares, 2)

    def shift(value, by):
        return lax.ppermute(value, "seq", [(i, (i + by) % count) for i in range(count)])

    def across(value, group_by, pairs):
        moves = [
            (g * count + i, (g + group_by) * count + j)
            for g in range(groups)
            for i, j in pairs
            if 0 <= g + group_by < groups
        ]
        return lax.ppermute(value, ("group", "seq"), moves)

    def swap(value, bits):
        return lax.ppermute(value, "group", [(g, g ^ bits) for g in range(groups)])

    def gathered(value):
        return [value] + [shift(value, k) for k in range(1, count)]

    packed = jnp.concatenate([latent[0], latent[1]], axis=1).astype(BF16)
    pieces = gathered(packed)
    stacked = jnp.stack(pieces)
    following = across(stacked, -1, [(i, i) for i in range(count)])

    maps, back, part, gram = pl.pallas_call(
        functools.partial(fold_kernel, shares),
        out_shape=(
            jax.ShapeDtypeStruct((width, 2 * channels), BF16),
            jax.ShapeDtypeStruct((width, depth), BF16),
            jax.ShapeDtypeStruct((width // shares, depth), BF16),
            jax.ShapeDtypeStruct((3, channels, channels), BF16),
        ),
        in_specs=[VMEM] * 4,
        out_specs=(VMEM,) * 4,
        cost_estimate=pl.CostEstimate(flops=width * depth * 1200, bytes_accessed=8 * width * depth, transcendentals=0),
        name="fold",
    )(in_weight, norm_gain[None, :], qkv_weight, out_weight)
    map_pieces = gathered(maps)
    own_part = jnp.stack(gathered(part)[1:])

    def attend(window):
        rows = 4 * share
        extra = [following] if window else []
        return pl.pallas_call(
            functools.partial(attend_kernel, count, window),
            out_shape=(
                jax.ShapeDtypeStruct((2 * share, full), BF16),
                jax.ShapeDtypeStruct((share, LANES), BF16),
            ),
            in_specs=[SMEM] + [VMEM] * (2 * count + len(extra) + 1),
            out_specs=(VMEM, VMEM),
            scratch_shapes=[
                pltpu.VMEM((total, LANES), F32),
                pltpu.VMEM((OVMAX + total, LANES), F32),
                pltpu.VMEM((total, LANES), BF16),
                pltpu.VMEM((full, LANES), BF16),
                pltpu.VMEM((2, QUAD, total), BF16),
                pltpu.VMEM((2, rows, QUAD), BF16),
                pltpu.VMEM((2, rows, total), BF16),
                pltpu.VMEM((total, QUAD), BF16),
                pltpu.VMEM((total, QUAD), BF16),
            ],
            cost_estimate=pl.CostEstimate(
                flops=16 * share * total * full, bytes_accessed=4 * full * share, transcendentals=share * total * full // HDIM
            ),
            name="attend",
        )(margin_len, *pieces, *extra, *map_pieces, gram)

    first = attend(0)
    second = attend(1)
    sums, owns = zip(first, second)
    planes = [swap(own_part, bits) for bits in high[1:]]
    far = jnp.stack([own_part] + planes)
    near = swap(far, 1)
    rows, *tails = pl.pallas_call(
        functools.partial(finish_kernel, count, shares, list(high)),
        out_shape=(
            jax.ShapeDtypeStruct((2, share, channels), F32),
            jax.ShapeDtypeStruct((share // 2, LANES), BF16),
            jax.ShapeDtypeStruct((share // 2, LANES), BF16),
        ),
        in_specs=[SMEM] + [VMEM] * 10,
        out_specs=(VMEM, VMEM, VMEM),
        scratch_shapes=[
            pltpu.VMEM((full, depth), BF16),
            pltpu.VMEM((2, 2 * share, depth), F32),
            pltpu.VMEM((2, 2 * share, depth), BF16),
            pltpu.VMEM((depth, LANES), BF16),
        ],
        cost_estimate=pl.CostEstimate(flops=8 * share * full * depth, bytes_accessed=2 * full * depth, transcendentals=0),
        name="finish",
    )(margin_len, *sums, *owns, in_weight, final_gain[None, :], head_out, back, far, near)

    deltas = list(range((total - OVMAX) // share, count))
    received = []
    for window, group_by in ((1, 1), (0, 0)):
        received += [across(tails[window], group_by, [(i, i - d) for i in range(d, count)]) for d in deltas]
    return pl.pallas_call(
        functools.partial(combine_kernel, count, deltas),
        out_shape=jax.ShapeDtypeStruct(latent.shape, F32),
        in_specs=[SMEM] + [VMEM] * (2 + len(received)),
        out_specs=VMEM,
        scratch_shapes=[pltpu.VMEM((OVMAX + total + share, LANES), F32)],
        name="combine",
    )(margin_len, latent, rows, *received)


def solution(mesh):
    in_specs = (
        P("group", "seq", None),
        P(),
        P(),
        P(),
        P(None, None, "seq"),
        P("seq", None),
        P(),
        P(),
    )
    out_specs = P("group", "seq", None)

    return jax.shard_map(body, mesh=mesh, in_specs=in_specs, out_specs=out_specs, check_vma=False)
```

profile of v0, /device:TPU:1, one launch (start us, length us, event | category | flops | bytes accessed | tf_op | source)
XLA Modules:
  0.0 96.6 jit_solution(5403558898143421844)
XLA Ops:
  0.0 1.3 %broadcast_in_dim.6.gain_ref = f32[1,1536]{1,0:T(1,128)} reshape(f32[1536]{0:T(1024)} %param.11) | data formatting | bytes 12288 | tf_op jit(solution)/shard_map/broadcast_in_dim | solution.py:279
  1.3 4.5 %fold.1 = (bf16[256,128]{1,0:T(8,128)(2,1)}, bf16[256,1536]{1,0:T(8,128)(2,1)}, bf16[32,1536]{1,0:T(8,128)(2,1)}, bf16[3,64,64]{2,1,0:T(8,128)(2,1)}) custom-call(bf16[64,1536]{1,0:T(8,128)(2,1)} %refs_4_.1, f32[1,1536]{1,0:T(1,128)} %broadcast_in_dim.6.gain_ref, bf16[3,1536,256]{2,1,0:T(8,128)(2,1)} %qkv_ref.1, bf16[256,1536]{1,0:T(8,128)(2,1)} %out_ref.1), custom_call_target="tpu_custom_call" | custom-call | flops 471859200 | bytes 3145728 | tf_op jit(solution)/shard_map/fold/pallas_call | solution.py:267
  5.8 4.1 %collective-permute-start.9 = (bf16[32,1536]{1,0:T(8,128)(2,1)}, bf16[32,1536]{1,0:T(8,128)(2,1)S(1)}, u32[]{:S(2)}, u32[]{:S(2)}) collective-permute-start(bf16[32,1536]{1,0:T(8,128)(2,1)} %get-tuple-element.23), channel_id=1, source_target_pairs={{0,3},{1,0},{2,1},{3,2},{4,7},{5,4},{6,5},{7,6},{8,11},{9,8},{10,9... | collective-permute-start | bytes 294920 | tf_op jit(solution)/shard_map/ppermute | solution.py:245
  9.9 0.5 collective-permute-start.7
  10.4 1.5 %collective-permute-done.9 = bf16[32,1536]{1,0:T(8,128)(2,1)S(1)} collective-permute-done((bf16[32,1536]{1,0:T(8,128)(2,1)}, bf16[32,1536]{1,0:T(8,128)(2,1)S(1)}, u32[]{:S(2)}, u32[]{:S(2)}) %collective-permute-start.9) | collective-permute-done | bytes 98336 | tf_op jit(solution)/shard_map/ppermute | solution.py:245
  11.9 7.0 %collective-permute-done.8 = bf16[32,1536]{1,0:T(8,128)(2,1)S(1)} collective-permute-done((bf16[32,1536]{1,0:T(8,128)(2,1)}, bf16[32,1536]{1,0:T(8,128)(2,1)S(1)}, u32[]{:S(2)}, u32[]{:S(2)}) %collective-permute-start.8) | collective-permute-done | bytes 98336 | tf_op jit(solution)/shard_map/ppermute | solution.py:245
  19.0 1.3 %collective-permute-start.11 = (bf16[3,32,1536]{2,1,0:T(8,128)(2,1)S(1)}, bf16[3,32,1536]{2,1,0:T(8,128)(2,1)S(1)}, u32[]{:S(2)}, u32[]{:S(2)}) collective-permute-start(bf16[3,32,1536]{2,1,0:T(8,128)(2,1)S(1)} %get-tuple-element.28), channel_id=1, source_target_pairs={{0,16},{4,20},{8,24},{12,28},{16,0},{20,4},{24,8},{28,12},{1,17},{... | collective-permute-start | bytes 884744 | tf_op jit(solution)/shard_map/ppermute | solution.py:257
  20.3 1.2 %collective-permute-start.10 = (bf16[3,32,1536]{2,1,0:T(8,128)(2,1)S(1)}, bf16[3,32,1536]{2,1,0:T(8,128)(2,1)S(1)}, u32[]{:S(2)}, u32[]{:S(2)}) collective-permute-start(bf16[3,32,1536]{2,1,0:T(8,128)(2,1)S(1)} %get-tuple-element.28), channel_id=1, source_target_pairs={{0,8},{4,12},{8,0},{12,4},{16,24},{20,28},{24,16},{28,20},{1,9},{5... | collective-permute-start | bytes 884744 | tf_op jit(solution)/shard_map/ppermute | solution.py:257
  21.5 0.2 collective-permute-start.12
  21.7 0.1 copy.12.latent_ref
  21.8 4.9 %collective-permute-done.11 = bf16[3,32,1536]{2,1,0:T(8,128)(2,1)S(1)} collective-permute-done((bf16[3,32,1536]{2,1,0:T(8,128)(2,1)S(1)}, bf16[3,32,1536]{2,1,0:T(8,128)(2,1)S(1)}, u32[]{:S(2)}, u32[]{:S(2)}) %collective-permute-start.11) | collective-permute-done | bytes 294944 | tf_op jit(solution)/shard_map/ppermute | solution.py:257
  26.7 1.0 collective-permute-done.10
  27.7 6.3 %collective-permute-done.12 = bf16[3,32,1536]{2,1,0:T(8,128)(2,1)S(1)} collective-permute-done((bf16[3,32,1536]{2,1,0:T(8,128)(2,1)S(1)}, bf16[3,32,1536]{2,1,0:T(8,128)(2,1)S(1)}, u32[]{:S(2)}, u32[]{:S(2)}) %collective-permute-start.12) | collective-permute-done | bytes 294944 | tf_op jit(solution)/shard_map/ppermute | solution.py:257
  33.9 0.1 pad_maximum_fusion.refs_8_
  34.1 2.1 %collective-permute-start.13 = (bf16[4,3,32,1536]{3,2,1,0:T(8,128)(2,1)S(1)}, bf16[4,3,32,1536]{3,2,1,0:T(8,128)(2,1)}, u32[]{:S(2)}, u32[]{:S(2)}) collective-permute-start(bf16[4,3,32,1536]{3,2,1,0:T(8,128)(2,1)S(1)} %pad_maximum_fusion.refs_8_), channel_id=1, source_target_pairs={{0,4},{4,0},{8,12},{12,8},{16,20},{20,16},{24,28},{28,24},{1,5},{5... | collective-permute-start | bytes 3538952 | tf_op jit(solution)/shard_map/ppermute | solution.py:257
  36.2 0.1 pad_maximum_fusion.3.refs_0_
  36.3 0.0 copy-start.4
  36.3 0.3 collective-permute-start.2
  36.6 1.5 %collective-permute-start.1 = (bf16[256,128]{1,0:T(8,128)(2,1)S(1)}, bf16[256,128]{1,0:T(8,128)(2,1)S(1)}, u32[]{:S(2)}, u32[]{:S(2)}) collective-permute-start(bf16[256,128]{1,0:T(8,128)(2,1)S(1)} %pad_maximum_fusion.3.refs_0_), channel_id=1, source_target_pairs={{0,2},{1,3},{2,0},{3,1},{4,6},{5,7},{6,4},{7,5},{8,10},{9,11},{10,... | collective-permute-start | bytes 196616 | tf_op jit(solution)/shard_map/ppermute | solution.py:245
  38.1 1.4 %collective-permute-start = (bf16[256,128]{1,0:T(8,128)(2,1)S(1)}, bf16[256,128]{1,0:T(8,128)(2,1)S(1)}, u32[]{:S(2)}, u32[]{:S(2)}) collective-permute-start(bf16[256,128]{1,0:T(8,128)(2,1)S(1)} %pad_maximum_fusion.3.refs_0_), channel_id=1, source_target_pairs={{0,1},{1,2},{2,3},{3,0},{4,5},{5,6},{6,7},{7,4},{8,9},{9,10},{10,1... | collective-permute-start | bytes 196616 | tf_op jit(solution)/shard_map/ppermute | solution.py:245
  39.5 1.9 %collective-permute-start.5 = (bf16[256,128]{1,0:T(8,128)(2,1)S(1)}, bf16[256,128]{1,0:T(8,128)(2,1)S(1)}, u32[]{:S(2)}, u32[]{:S(2)}) collective-permute-start(bf16[256,128]{1,0:T(8,128)(2,1)S(1)} %copy-done.14), channel_id=1, source_target_pairs={{0,3},{1,0},{2,1},{3,2},{4,7},{5,4},{6,5},{7,6},{8,11},{9,8},{10,9... | collective-permute-start | bytes 196616 | tf_op jit(solution)/shard_map/ppermute | solution.py:245
  41.4 0.6 broadcast_in_dim.7.refs_5_
  42.0 0.9 copy.11.refs_6_
  42.9 0.0 collective-permute-done.2.refs_3_
  43.0 0.0 collective-permute-start.4
  43.0 0.3 collective-permute-start.3
  43.3 1.0 %collective-permute-done.refs_1_ = bf16[256,128]{1,0:T(8,128)(2,1)S(1)} collective-permute-done((bf16[256,128]{1,0:T(8,128)(2,1)S(1)}, bf16[256,128]{1,0:T(8,128)(2,1)S(1)}, u32[]{:S(2)}, u32[]{:S(2)}) %collective-permute-start) | collective-permute-done | bytes 65568 | tf_op jit(solution)/shard_map/ppermute | solution.py:245
  44.3 0.1 pad_maximum_fusion.2
  44.4 3.5 %collective-permute-start.6 = (bf16[4,256,128]{2,1,0:T(8,128)(2,1)S(1)}, bf16[4,256,128]{2,1,0:T(8,128)(2,1)S(1)}, u32[]{:S(2)}, u32[]{:S(2)}) collective-permute-start(bf16[4,256,128]{2,1,0:T(8,128)(2,1)S(1)} %pad_maximum_fusion.2), channel_id=1, source_target_pairs={{4,0},{5,1},{6,2},{7,3},{8,4},{9,5},{10,6},{11,7},{12,8},{13,9},{1... | collective-permute-start | bytes 786440 | tf_op jit(solution)/shard_map/ppermute | solution.py:254
  47.8 1.5 %collective-permute-done.4.refs_6_.refs_7_ = bf16[256,128]{1,0:T(8,128)(2,1)S(1)} collective-permute-done((bf16[256,128]{1,0:T(8,128)(2,1)S(1)}, bf16[256,128]{1,0:T(8,128)(2,1)S(1)}, u32[]{:S(2)}, u32[]{:S(2)}) %collective-permute-start.4) | collective-permute-done | bytes 65568 | tf_op jit(solution)/shard_map/ppermute | solution.py:245
  49.4 0.6 copy-done.16
  49.9 0.0 copy-done.17
  50.0 9.2 %attend.2 = (bf16[512,1024]{1,0:T(8,128)(2,1)}, bf16[256,128]{1,0:T(8,128)(2,1)}) custom-call(s32[15]{0:T(128)} %margin_ref.7, bf16[256,128]{1,0:T(8,128)(2,1)} %copy-done.4, bf16[256,128]{1,0:T(8,128)(2,1)} %copy-done.7, bf16[256,128]{1,0:T(8,128)(2,1)} %copy-done.6, bf16[256,128]{1,0:T(8,128)(2,1)} %copy-done.5, ...), custom_call_target="tpu_custom_call" | custom-call | flops 4294967296 | bytes 1048576 | tf_op jit(solution)/shard_map/attend/pallas_call | solution.py:286
  59.2 0.7 copy-done.13
  59.9 9.6 %attend.3 = (bf16[512,1024]{1,0:T(8,128)(2,1)}, bf16[256,128]{1,0:T(8,128)(2,1)}) custom-call(s32[15]{0:T(128)} %margin_ref.7, bf16[256,128]{1,0:T(8,128)(2,1)} %copy-done.4, bf16[256,128]{1,0:T(8,128)(2,1)} %copy-done.7, bf16[256,128]{1,0:T(8,128)(2,1)} %copy-done.6, bf16[256,128]{1,0:T(8,128)(2,1)} %copy-done.5, bf16[4,256,128]{2,1,0:T(8,128)(2,1)} %copy-done.13, ...), custom_call_target="tpu_custom_call" | custom-call | flops 4294967296 | bytes 1048576 | tf_op jit(solution)/shard_map/attend/pallas_call | solution.py:286
  69.5 10.0 %finish.1 = (f32[2,256,64]{2,1,0:T(8,128)}, bf16[128,128]{1,0:T(8,128)(2,1)}, bf16[128,128]{1,0:T(8,128)(2,1)}) custom-call(s32[15]{0:T(128)} %margin_ref.7, bf16[512,1024]{1,0:T(8,128)(2,1)} %get-tuple-element.18.refs_0_, bf16[512,1024]{1,0:T(8,128)(2,1)} %get-tuple-element.19.refs_1_, bf16[256,128]{1,0:T(8,128)(2,1)} %get-tuple-element.20.refs_2_, ...), custom_call_target="tpu_custom_call" | custom-call | flops 3221225472 | bytes 3145728 | tf_op jit(solution)/shard_map/finish/pallas_call | solution.py:317
  79.5 1.3 %collective-permute-start.15 = (bf16[128,128]{1,0:T(8,128)(2,1)}, bf16[128,128]{1,0:T(8,128)(2,1)S(1)}, u32[]{:S(2)}, u32[]{:S(2)}) collective-permute-start(bf16[128,128]{1,0:T(8,128)(2,1)} %get-tuple-element.25), channel_id=1, source_target_pairs={{3,4},{7,8},{11,12},{15,16},{19,20},{23,24},{27,28}} | collective-permute-start | bytes 98312 | tf_op jit(solution)/shard_map/ppermute | solution.py:254
  80.8 1.3 %collective-permute-start.14 = (bf16[128,128]{1,0:T(8,128)(2,1)}, bf16[128,128]{1,0:T(8,128)(2,1)S(1)}, u32[]{:S(2)}, u32[]{:S(2)}) collective-permute-start(bf16[128,128]{1,0:T(8,128)(2,1)} %get-tuple-element.25), channel_id=1, source_target_pairs={{2,4},{3,5},{6,8},{7,9},{10,12},{11,13},{14,16},{15,17},{18,20},{1... | collective-permute-start | bytes 98312 | tf_op jit(solution)/shard_map/ppermute | solution.py:254
  82.1 1.3 %collective-permute-start.17 = (bf16[128,128]{1,0:T(8,128)(2,1)}, bf16[128,128]{1,0:T(8,128)(2,1)S(1)}, u32[]{:S(2)}, u32[]{:S(2)}) collective-permute-start(bf16[128,128]{1,0:T(8,128)(2,1)} %get-tuple-element.26), channel_id=1, source_target_pairs={{3,0},{7,4},{11,8},{15,12},{19,16},{23,20},{27,24},{31,28}} | collective-permute-start | bytes 98312 | tf_op jit(solution)/shard_map/ppermute | solution.py:254
  83.4 1.3 %collective-permute-start.16 = (bf16[128,128]{1,0:T(8,128)(2,1)}, bf16[128,128]{1,0:T(8,128)(2,1)S(1)}, u32[]{:S(2)}, u32[]{:S(2)}) collective-permute-start(bf16[128,128]{1,0:T(8,128)(2,1)} %get-tuple-element.26), channel_id=1, source_target_pairs={{2,0},{3,1},{6,4},{7,5},{10,8},{11,9},{14,12},{15,13},{18,16},{19,... | collective-permute-start | bytes 98312 | tf_op jit(solution)/shard_map/ppermute | solution.py:254
  84.7 2.0 %collective-permute-done.15.refs_1_ = bf16[128,128]{1,0:T(8,128)(2,1)S(1)} collective-permute-done((bf16[128,128]{1,0:T(8,128)(2,1)}, bf16[128,128]{1,0:T(8,128)(2,1)S(1)}, u32[]{:S(2)}, u32[]{:S(2)}) %collective-permute-start.15) | collective-permute-done | bytes 32800 | tf_op jit(solution)/shard_map/ppermute | solution.py:254
  86.7 0.4 collective-permute-done.14.refs_0_
  87.1 4.8 %collective-permute-done.17.refs_3_ = bf16[128,128]{1,0:T(8,128)(2,1)S(1)} collective-permute-done((bf16[128,128]{1,0:T(8,128)(2,1)}, bf16[128,128]{1,0:T(8,128)(2,1)S(1)}, u32[]{:S(2)}, u32[]{:S(2)}) %collective-permute-start.17) | collective-permute-done | bytes 32800 | tf_op jit(solution)/shard_map/ppermute | solution.py:254
  92.0 0.3 collective-permute-done.16.refs_2_
  92.3 0.3 copy-done.10
  92.6 0.3 copy-done.11
  92.9 2.0 %combine.1 = f32[2,256,64]{2,1,0:T(8,128)} custom-call(s32[15]{0:T(128)} %margin_ref.7, f32[2,256,64]{2,1,0:T(8,128)} %copy-done, f32[2,256,64]{2,1,0:T(8,128)} %get-tuple-element.24.rows_ref, bf16[128,128]{1,0:T(8,128)(2,1)} %copy-done.9, bf16[128,128]{1,0:T(8,128)(2,1)} %copy-done.8, bf16[128,128]{1,0:T(8,128)(2,1)} %copy-done.11, bf16[128,128]{1,0:T(8,128)(2,1)} %copy-done.10), custom_call_target="tpu_custom_call" | custom-call | tf_op jit(solution)/shard_map/combine/pallas_call | solution.py:340
  94.9 1.7 %copy.13 = f32[2,256,64]{1,2,0:T(8,128)} copy(f32[2,256,64]{2,1,0:T(8,128)} %combine.1) | data formatting | bytes 262144 | tf_op jit(solution)/shard_map/combine/pallas_call | solution.py:340
  (39 shorter events, 0.1 us)
Async XLA Ops:
  1.3 20.4 %copy-start.3 = (f32[2,256,64]{1,2,0:T(8,128)S(1)}, f32[2,256,64]{1,2,0:T(8,128)}, u32[]{:S(2)}) copy-start(f32[2,256,64]{1,2,0:T(8,128)} %param.8) | copy-start | bytes 393220
  5.8 6.1 %collective-permute-start.9 = (bf16[32,1536]{1,0:T(8,128)(2,1)}, bf16[32,1536]{1,0:T(8,128)(2,1)S(1)}, u32[]{:S(2)}, u32[]{:S(2)}) collective-permute-start(bf16[32,1536]{1,0:T(8,128)(2,1)} %get-tuple-element.23), channel_id=1, source_target_pairs={{0,3},{1,0},{2,1},{3,2},{4,7},{5,4},{6,5},{7,6},{8,11},{9,8},{10,9... | collective-permute-start | bytes 294920 | tf_op jit(solution)/shard_map/ppermute | solution.py:245
  9.9 9.0 %collective-permute-start.8 = (bf16[32,1536]{1,0:T(8,128)(2,1)}, bf16[32,1536]{1,0:T(8,128)(2,1)S(1)}, u32[]{:S(2)}, u32[]{:S(2)}) collective-permute-start(bf16[32,1536]{1,0:T(8,128)(2,1)} %get-tuple-element.23), channel_id=1, source_target_pairs={{0,2},{1,3},{2,0},{3,1},{4,6},{5,7},{6,4},{7,5},{8,10},{9,11},{10,... | collective-permute-start | bytes 294920 | tf_op jit(solution)/shard_map/ppermute | solution.py:245
  9.9 9.0 %collective-permute-start.7 = (bf16[32,1536]{1,0:T(8,128)(2,1)}, bf16[32,1536]{1,0:T(8,128)(2,1)S(1)}, u32[]{:S(2)}, u32[]{:S(2)}) collective-permute-start(bf16[32,1536]{1,0:T(8,128)(2,1)} %get-tuple-element.23), channel_id=1, source_target_pairs={{0,1},{1,2},{2,3},{3,0},{4,5},{5,6},{6,7},{7,4},{8,9},{9,10},{10,1... | collective-permute-start | bytes 294920 | tf_op jit(solution)/shard_map/ppermute | solution.py:245
  19.0 7.7 %collective-permute-start.11 = (bf16[3,32,1536]{2,1,0:T(8,128)(2,1)S(1)}, bf16[3,32,1536]{2,1,0:T(8,128)(2,1)S(1)}, u32[]{:S(2)}, u32[]{:S(2)}) collective-permute-start(bf16[3,32,1536]{2,1,0:T(8,128)(2,1)S(1)} %get-tuple-element.28), channel_id=1, source_target_pairs={{0,16},{4,20},{8,24},{12,28},{16,0},{20,4},{24,8},{28,12},{1,17},{... | collective-permute-start | bytes 884744 | tf_op jit(solution)/shard_map/ppermute | solution.py:257
  20.3 7.4 %collective-permute-start.10 = (bf16[3,32,1536]{2,1,0:T(8,128)(2,1)S(1)}, bf16[3,32,1536]{2,1,0:T(8,128)(2,1)S(1)}, u32[]{:S(2)}, u32[]{:S(2)}) collective-permute-start(bf16[3,32,1536]{2,1,0:T(8,128)(2,1)S(1)} %get-tuple-element.28), channel_id=1, source_target_pairs={{0,8},{4,12},{8,0},{12,4},{16,24},{20,28},{24,16},{28,20},{1,9},{5... | collective-permute-start | bytes 884744 | tf_op jit(solution)/shard_map/ppermute | solution.py:257
  21.5 12.4 %collective-permute-start.12 = (bf16[3,32,1536]{2,1,0:T(8,128)(2,1)S(1)}, bf16[3,32,1536]{2,1,0:T(8,128)(2,1)S(1)}, u32[]{:S(2)}, u32[]{:S(2)}) collective-permute-start(bf16[3,32,1536]{2,1,0:T(8,128)(2,1)S(1)} %get-tuple-element.28), channel_id=1, source_target_pairs={{0,24},{4,28},{8,16},{12,20},{16,8},{20,12},{24,0},{28,4},{1,25},{... | collective-permute-start | bytes 884744 | tf_op jit(solution)/shard_map/ppermute | solution.py:257
  21.8 14.4 %copy-start = (f32[2,256,64]{2,1,0:T(8,128)}, f32[2,256,64]{2,1,0:T(8,128)S(1)}, u32[]{:S(2)}) copy-start(f32[2,256,64]{2,1,0:T(8,128)S(1)} %copy.12.latent_ref) | copy-start | bytes 393220
  33.9 5.6 %copy-start.14 = (bf16[256,128]{1,0:T(8,128)(2,1)S(1)}, bf16[256,128]{1,0:T(8,128)(2,1)}, u32[]{:S(2)}) copy-start(bf16[256,128]{1,0:T(8,128)(2,1)} %get-tuple-element.16.refs_4_.refs_5_) | copy-start | bytes 196612
  33.9 7.5 %copy-start.12 = (f32[1536]{0:T(1024)S(1)}, f32[1536]{0:T(1024)}, u32[]{:S(2)}) copy-start(f32[1536]{0:T(1024)} %param.14) | copy-start | bytes 18436
  33.9 8.1 %copy-start.2 = (bf16[1536,64]{0,1:T(8,128)(2,1)S(1)}, bf16[1536,64]{0,1:T(8,128)(2,1)}, u32[]{:S(2)}) copy-start(bf16[1536,64]{0,1:T(8,128)(2,1)} %param.15) | copy-start | bytes 589828
  34.1 25.1 %copy-start.1 = (bf16[4,3,32,1536]{3,2,1,0:T(8,128)(2,1)}, bf16[4,3,32,1536]{3,2,1,0:T(8,128)(2,1)S(1)}, u32[]{:S(2)}) copy-start(bf16[4,3,32,1536]{3,2,1,0:T(8,128)(2,1)S(1)} %pad_maximum_fusion.refs_8_) | copy-start | bytes 3538948
  34.1 35.4 %collective-permute-start.13 = (bf16[4,3,32,1536]{3,2,1,0:T(8,128)(2,1)S(1)}, bf16[4,3,32,1536]{3,2,1,0:T(8,128)(2,1)}, u32[]{:S(2)}, u32[]{:S(2)}) collective-permute-start(bf16[4,3,32,1536]{3,2,1,0:T(8,128)(2,1)S(1)} %pad_maximum_fusion.refs_8_), channel_id=1, source_target_pairs={{0,4},{4,0},{8,12},{12,8},{16,20},{20,16},{24,28},{28,24},{1,5},{5... | collective-permute-start | bytes 3538952 | tf_op jit(solution)/shard_map/ppermute | solution.py:257
  36.3 13.0 %copy-start.4 = (bf16[256,128]{1,0:T(8,128)(2,1)}, bf16[256,128]{1,0:T(8,128)(2,1)S(1)}, u32[]{:S(2)}) copy-start(bf16[256,128]{1,0:T(8,128)(2,1)S(1)} %pad_maximum_fusion.3.refs_0_) | copy-start | bytes 196612
  36.3 6.6 %collective-permute-start.2 = (bf16[256,128]{1,0:T(8,128)(2,1)S(1)}, bf16[256,128]{1,0:T(8,128)(2,1)S(1)}, u32[]{:S(2)}, u32[]{:S(2)}) collective-permute-start(bf16[256,128]{1,0:T(8,128)(2,1)S(1)} %pad_maximum_fusion.3.refs_0_), channel_id=1, source_target_pairs={{0,3},{1,0},{2,1},{3,2},{4,7},{5,4},{6,5},{7,6},{8,11},{9,8},{10,9... | collective-permute-start | bytes 196616 | tf_op jit(solution)/shard_map/ppermute | solution.py:245
  36.6 6.3 %collective-permute-start.1 = (bf16[256,128]{1,0:T(8,128)(2,1)S(1)}, bf16[256,128]{1,0:T(8,128)(2,1)S(1)}, u32[]{:S(2)}, u32[]{:S(2)}) collective-permute-start(bf16[256,128]{1,0:T(8,128)(2,1)S(1)} %pad_maximum_fusion.3.refs_0_), channel_id=1, source_target_pairs={{0,2},{1,3},{2,0},{3,1},{4,6},{5,7},{6,4},{7,5},{8,10},{9,11},{10,... | collective-permute-start | bytes 196616 | tf_op jit(solution)/shard_map/ppermute | solution.py:245
  38.1 6.1 %collective-permute-start = (bf16[256,128]{1,0:T(8,128)(2,1)S(1)}, bf16[256,128]{1,0:T(8,128)(2,1)S(1)}, u32[]{:S(2)}, u32[]{:S(2)}) collective-permute-start(bf16[256,128]{1,0:T(8,128)(2,1)S(1)} %pad_maximum_fusion.3.refs_0_), channel_id=1, source_target_pairs={{0,1},{1,2},{2,3},{3,0},{4,5},{5,6},{6,7},{7,4},{8,9},{9,10},{10,1... | collective-permute-start | bytes 196616 | tf_op jit(solution)/shard_map/ppermute | solution.py:245
  39.5 8.3 %collective-permute-start.5 = (bf16[256,128]{1,0:T(8,128)(2,1)S(1)}, bf16[256,128]{1,0:T(8,128)(2,1)S(1)}, u32[]{:S(2)}, u32[]{:S(2)}) collective-permute-start(bf16[256,128]{1,0:T(8,128)(2,1)S(1)} %copy-done.14), channel_id=1, source_target_pairs={{0,3},{1,0},{2,1},{3,2},{4,7},{5,4},{6,5},{7,6},{8,11},{9,8},{10,9... | collective-permute-start | bytes 196616 | tf_op jit(solution)/shard_map/ppermute | solution.py:245
  43.0 6.4 %copy-start.5 = (bf16[256,128]{1,0:T(8,128)(2,1)}, bf16[256,128]{1,0:T(8,128)(2,1)S(1)}, u32[]{:S(2)}) copy-start(bf16[256,128]{1,0:T(8,128)(2,1)S(1)} %collective-permute-done.2.refs_3_) | copy-start | bytes 196612
  43.0 6.4 %collective-permute-start.4 = (bf16[256,128]{1,0:T(8,128)(2,1)S(1)}, bf16[256,128]{1,0:T(8,128)(2,1)S(1)}, u32[]{:S(2)}, u32[]{:S(2)}) collective-permute-start(bf16[256,128]{1,0:T(8,128)(2,1)S(1)} %copy-done.14), channel_id=1, source_target_pairs={{0,2},{1,3},{2,0},{3,1},{4,6},{5,7},{6,4},{7,5},{8,10},{9,11},{10,... | collective-permute-start | bytes 196616 | tf_op jit(solution)/shard_map/ppermute | solution.py:245
  43.0 6.4 %copy-start.6 = (bf16[256,128]{1,0:T(8,128)(2,1)}, bf16[256,128]{1,0:T(8,128)(2,1)S(1)}, u32[]{:S(2)}) copy-start(bf16[256,128]{1,0:T(8,128)(2,1)S(1)} %collective-permute-done.1.refs_2_) | copy-start | bytes 196612
  43.0 6.3 %collective-permute-start.3 = (bf16[256,128]{1,0:T(8,128)(2,1)S(1)}, bf16[256,128]{1,0:T(8,128)(2,1)S(1)}, u32[]{:S(2)}, u32[]{:S(2)}) collective-permute-start(bf16[256,128]{1,0:T(8,128)(2,1)S(1)} %copy-done.14), channel_id=1, source_target_pairs={{0,1},{1,2},{2,3},{3,0},{4,5},{5,6},{6,7},{7,4},{8,9},{9,10},{10,1... | collective-permute-start | bytes 196616 | tf_op jit(solution)/shard_map/ppermute | solution.py:245
  44.3 5.1 %copy-start.7 = (bf16[256,128]{1,0:T(8,128)(2,1)}, bf16[256,128]{1,0:T(8,128)(2,1)S(1)}, u32[]{:S(2)}) copy-start(bf16[256,128]{1,0:T(8,128)(2,1)S(1)} %collective-permute-done.refs_1_) | copy-start | bytes 196612
  44.4 14.8 %collective-permute-start.6 = (bf16[4,256,128]{2,1,0:T(8,128)(2,1)S(1)}, bf16[4,256,128]{2,1,0:T(8,128)(2,1)S(1)}, u32[]{:S(2)}, u32[]{:S(2)}) collective-permute-start(bf16[4,256,128]{2,1,0:T(8,128)(2,1)S(1)} %pad_maximum_fusion.2), channel_id=1, source_target_pairs={{4,0},{5,1},{6,2},{7,3},{8,4},{9,5},{10,6},{11,7},{12,8},{13,9},{1... | collective-permute-start | bytes 786440 | tf_op jit(solution)/shard_map/ppermute | solution.py:254
  47.8 1.5 %copy-start.15 = (bf16[256,128]{1,0:T(8,128)(2,1)}, bf16[256,128]{1,0:T(8,128)(2,1)S(1)}, u32[]{:S(2)}) copy-start(bf16[256,128]{1,0:T(8,128)(2,1)S(1)} %collective-permute-done.5.refs_7_.refs_8_) | copy-start | bytes 196612
  49.3 0.6 copy-start.16
  49.3 0.7 copy-start.17
  59.2 0.7 copy-start.13
  79.5 7.2 %collective-permute-start.15 = (bf16[128,128]{1,0:T(8,128)(2,1)}, bf16[128,128]{1,0:T(8,128)(2,1)S(1)}, u32[]{:S(2)}, u32[]{:S(2)}) collective-permute-start(bf16[128,128]{1,0:T(8,128)(2,1)} %get-tuple-element.25), channel_id=1, source_target_pairs={{3,4},{7,8},{11,12},{15,16},{19,20},{23,24},{27,28}} | collective-permute-start | bytes 98312 | tf_op jit(solution)/shard_map/ppermute | solution.py:254
  80.8 6.3 %collective-permute-start.14 = (bf16[128,128]{1,0:T(8,128)(2,1)}, bf16[128,128]{1,0:T(8,128)(2,1)S(1)}, u32[]{:S(2)}, u32[]{:S(2)}) collective-permute-start(bf16[128,128]{1,0:T(8,128)(2,1)} %get-tuple-element.25), channel_id=1, source_target_pairs={{2,4},{3,5},{6,8},{7,9},{10,12},{11,13},{14,16},{15,17},{18,20},{1... | collective-permute-start | bytes 98312 | tf_op jit(solution)/shard_map/ppermute | solution.py:254
  82.1 9.9 %collective-permute-start.17 = (bf16[128,128]{1,0:T(8,128)(2,1)}, bf16[128,128]{1,0:T(8,128)(2,1)S(1)}, u32[]{:S(2)}, u32[]{:S(2)}) collective-permute-start(bf16[128,128]{1,0:T(8,128)(2,1)} %get-tuple-element.26), channel_id=1, source_target_pairs={{3,0},{7,4},{11,8},{15,12},{19,16},{23,20},{27,24},{31,28}} | collective-permute-start | bytes 98312 | tf_op jit(solution)/shard_map/ppermute | solution.py:254
  83.4 8.9 %collective-permute-start.16 = (bf16[128,128]{1,0:T(8,128)(2,1)}, bf16[128,128]{1,0:T(8,128)(2,1)S(1)}, u32[]{:S(2)}, u32[]{:S(2)}) collective-permute-start(bf16[128,128]{1,0:T(8,128)(2,1)} %get-tuple-element.26), channel_id=1, source_target_pairs={{2,0},{3,1},{6,4},{7,5},{10,8},{11,9},{14,12},{15,13},{18,16},{19,... | collective-permute-start | bytes 98312 | tf_op jit(solution)/shard_map/ppermute | solution.py:254
  86.7 5.5 %copy-start.8 = (bf16[128,128]{1,0:T(8,128)(2,1)}, bf16[128,128]{1,0:T(8,128)(2,1)S(1)}, u32[]{:S(2)}) copy-start(bf16[128,128]{1,0:T(8,128)(2,1)S(1)} %collective-permute-done.15.refs_1_) | copy-start | bytes 98308
  87.1 5.1 %copy-start.9 = (bf16[128,128]{1,0:T(8,128)(2,1)}, bf16[128,128]{1,0:T(8,128)(2,1)S(1)}, u32[]{:S(2)}) copy-start(bf16[128,128]{1,0:T(8,128)(2,1)S(1)} %collective-permute-done.14.refs_0_) | copy-start | bytes 98308
  92.0 0.6 copy-start.10
  92.3 0.6 copy-start.11
where the time goes:
time: 97.2 us; the launch traced here: 96.6 us
  Pallas kernels  35.3 us (36%)
  waiting for transfers between devices  30.7 us (32%)
  starting transfers between devices  23.4 us (24%)
  local copies, waits for them, and re-layouts  6.66 us (7%)
    pallas_call x2, Pallas kernels, attend(): pl.pallas_call(functools.partial(attend_kernel, count, window), out_shape...  18.8 us
    ppermute x4, waiting for transfers between devices, swap(): return lax.ppermute(value, 'group', [(g, g ^ bits) for g in range(groups)])  12.1 us
    ppermute x9, waiting for transfers between devices, shift(): lax.ppermute(value, 'seq', [(i, (i + by) % count) for i in range(count)])  11 us
    pallas_call x1, Pallas kernels, body(): pl.pallas_call(functools.partial(finish_kernel, count, shares, list(high)...  10 us
    ppermute x9, starting transfers between devices, shift(): lax.ppermute(value, 'seq', [(i, (i + by) % count) for i in range(count)])  9.94 us
    ppermute x5, starting transfers between devices, across(): return lax.ppermute(value, ('group', 'seq'), moves)  8.61 us
    ppermute x5, waiting for transfers between devices, across(): return lax.ppermute(value, ('group', 'seq'), moves)  7.57 us
    ppermute x4, starting transfers between devices, swap(): return lax.ppermute(value, 'group', [(g, g ^ bits) for g in range(groups)])  4.83 us
  transfers between devices with their start and end apart: 18, of which 11 were waited for; matrix products, arithmetic and copies ran while one was open for 2% of the time, Pallas kernels for 19%

commit v1 on v0

v1 whole, which is shorter than its diff:
```python
import functools
import math

import jax
import jax.numpy as jnp
from jax import lax
from jax.experimental import pallas as pl
from jax.experimental.pallas import tpu as pltpu
from jax.sharding import PartitionSpec as P

HDIM = 64
OVMAX = 512
LANES = 128
QUAD = 4 * HDIM
STEP = -0.5
F32 = jnp.float32
BF16 = jnp.bfloat16
VMEM = pl.BlockSpec(memory_space=pltpu.VMEM)
SMEM = pl.BlockSpec(memory_space=pltpu.SMEM)


def iota(shape, dim):
    return lax.broadcasted_iota(jnp.int32, shape, dim)


def matmul(lhs, rhs):
    return jnp.dot(lhs, rhs, preferred_element_type=F32)


def matmul_nt(lhs, rhs, precision=None):
    return lax.dot_general(lhs, rhs, (((1,), (1,)), ((), ())), precision=precision, preferred_element_type=F32)


def split(value):
    high = value.astype(BF16)
    return high, (value - high.astype(F32)).astype(BF16)


def margin_at(margin_ref, index):
    last = margin_ref.shape[0]
    length = margin_ref[jnp.clip(index, 0, last - 1)]
    return jnp.where((index >= 0) & (index < last), length, 0)


def fold_kernel(shares, latent_ref, in_ref, gain_ref, qkv_ref, out_ref, final_ref, head_ref, *refs):
    send_ref, back_ref, part_ref, direct_ref, gram_ref = refs
    weight = in_ref[...].astype(F32)
    channels, depth = weight.shape
    width = out_ref.shape[0]
    share = latent_ref.shape[2]
    centered = weight - jnp.mean(weight, axis=-1, keepdims=True)
    both = jnp.concatenate(split(centered * gain_ref[...]), axis=0)

    def folded(which):
        product = matmul(both, qkv_ref[which])
        return product[:channels] + product[channels:]

    values = folded(2)
    tiled = jnp.concatenate([values] * (width // HDIM), axis=0)
    same = iota((width, width), 0) // channels == iota((width, width), 1) // HDIM
    high, low = split(jnp.where(same, tiled, 0.0))
    back = matmul(high, out_ref[...]) + matmul(low, out_ref[...])
    back = back - jnp.mean(back, axis=-1, keepdims=True)
    back_ref[:, :depth] = back.astype(BF16)

    pieces = split(back * final_ref[...]) + split(centered * final_ref[...])
    scores = matmul_nt(jnp.concatenate(pieces, axis=0), head_ref[...])
    left = iota((width, LANES), 1) < channels

    def halves(value):
        value = jnp.concatenate([value, value], axis=1)
        high, low = split(value)
        return jnp.where(left[: value.shape[0]], high.astype(F32), low.astype(F32)).astype(BF16)

    back_ref[:, depth:] = halves(scores[:width] + scores[width : 2 * width])
    rows = width // shares
    sub = lax.rem(lax.axis_index("group"), shares)
    part_ref[...] = back_ref[pl.ds(pl.multiple_of(sub * rows, rows), rows), :]

    send_ref[:width, :] = jnp.concatenate([folded(0), folded(1)], axis=0).T.astype(BF16)
    send_ref[width:, :] = latent_ref[...].reshape(2 * channels, share).T.astype(BF16)

    high, low = split(centered)
    direct_ref[:channels, :depth] = high
    direct_ref[channels:, :depth] = low
    direct_ref[:channels, depth:] = halves(scores[2 * width : 2 * width + channels] + scores[2 * width + channels :])
    direct_ref[channels:, depth:] = jnp.zeros((channels, LANES), BF16)

    gram = matmul_nt(jnp.concatenate([high, low], axis=0), jnp.concatenate([high, low], axis=0))
    gram = (gram[:channels] + gram[channels:]) * (1.0 / depth)
    gram = gram + pltpu.roll(gram, channels, 1)
    first, rest = split(gram)
    rest = gram - first.astype(F32)
    second, third = split(rest)
    left = left[:channels]
    gram_ref[:, :LANES] = jnp.where(left, first.astype(F32), second.astype(F32)).astype(BF16)
    gram_ref[:, LANES:] = jnp.where(left, third.astype(F32), 0.0).astype(BF16)


def attend_kernel(count, window, margin_ref, *refs):
    piece_refs, refs = refs[:count], refs[count:]
    gram_ref, refs = refs[0], refs[1:]
    if window:
        next_ref, refs = refs[0], refs[1:]
    sum_ref, slot_scr, next_scr, win_scr, map_scr, key_scr, query_scr, p_scr, ext_scr = refs
    total = win_scr.shape[0]
    channels = gram_ref.shape[0]
    share = total // count
    full = map_scr.shape[0]
    width = full // count
    low = total - OVMAX
    group_pos = lax.axis_index("group")
    seq_pos = lax.axis_index("seq")
    over_len = margin_at(margin_ref, 2 * group_pos + window)
    own = total - over_len

    next_scr[:OVMAX, :] = jnp.zeros((OVMAX, LANES), F32)
    for k in range(count):
        source = lax.rem(seq_pos + (count - k), count) * share
        at = pl.ds(pl.multiple_of(source, share), share)
        after = pl.ds(pl.multiple_of(source + OVMAX, share), share)
        slot = piece_refs[k][width:, :].astype(F32)
        slot_scr[at, :] = pltpu.roll(slot, channels, 1) if window else slot
        next_scr[after, :] = next_ref[k].astype(F32) if window else pltpu.roll(slot, channels, 1)
        map_scr[k * width : (k + 1) * width, :] = piece_refs[k][:width, :]
    left = iota((OVMAX, LANES), 1) < channels
    for start in range(0, total, OVMAX):
        rows = slot_scr[start : start + OVMAX, :]
        if start >= low:
            tail = next_scr[pl.ds(over_len + (start - low), OVMAX), :]
            rows = jnp.where(iota(rows.shape, 0) + start < own, rows, tail)
        win_scr[start : start + OVMAX, :] = jnp.where(left, rows, 0.0).astype(BF16)

    def twice(tokens):
        tokens = tokens.astype(F32)
        return tokens + pltpu.roll(tokens, channels, 1)

    def bend(tokens, doubled):
        bent = matmul(tokens[:, :channels], gram_ref[...])
        return (bent[:, :LANES] + bent[:, LANES:]) * doubled

    def variance(bent):
        return jnp.maximum(jnp.sum(bent, axis=-1, keepdims=True), 0.0) + 1e-05

    win = win_scr[...]
    mine = win_scr[pl.ds(pl.multiple_of(seq_pos * share, share), share), :]
    mine_twice = twice(mine)
    sum_ref[:share, full:] = mine_twice.astype(BF16)
    sum_ref[share:, full:] = mine_twice.astype(BF16)
    query_eps = variance(bend(mine, mine_twice)) * 1e-06
    doubled = twice(win)
    bent = bend(win, doubled)
    ones = jnp.ones((16, LANES), BF16)
    key_eps = (jnp.maximum(matmul_nt(ones, bent.astype(BF16))[:1], 0.0) + 1e-05) * 1e-06

    scaled = doubled * lax.rsqrt(variance(bent))
    counted = (iota((total, LANES), 0) >= jnp.minimum(own, total - 1)).astype(F32)
    left = iota((total, LANES), 1) < channels
    ext_scr[:, :LANES] = jnp.where(left, scaled, scaled * counted).astype(BF16)
    ext_scr[:, LANES:] = jnp.where(left, 1.0, counted).astype(BF16)

    tile = min(total, 256)
    win_right = jnp.where(left, 0.0, doubled).astype(BF16)
    for start in range(0, total, tile):
        keys = matmul_nt(map_scr[...], win_right[start : start + tile]).reshape(full // HDIM, HDIM, tile)
        norm = jnp.mean(keys * keys, axis=1, keepdims=True)
        keys = keys * lax.rsqrt(norm + key_eps[None, :, start : start + tile])
        key_scr[:, start : start + tile] = keys.reshape(full, tile).astype(BF16)

    one_head = iota((QUAD, QUAD), 0) // HDIM == iota((QUAD, QUAD), 1) // HDIM
    spread = jnp.where(one_head, 1.0 / HDIM, 0.0).astype(BF16)
    head_of = iota((share, QUAD), 1) // HDIM
    scale = HDIM ** (-0.5) * math.log2(math.e)
    left = iota((share, LANES), 1) < channels
    for quad in range(full // QUAD):
        span = slice(quad * QUAD, (quad + 1) * QUAD)
        queries = matmul_nt(mine, map_scr[span, :])
        norm = matmul((queries * queries).astype(BF16), spread)
        queries = (queries * lax.rsqrt(norm + query_eps)).astype(BF16)
        for head in range(4):
            query_scr[quad % 2, head * share : (head + 1) * share, :] = jnp.where(
                head_of == head, queries, jnp.zeros_like(queries)
            )
        for start in range(0, total, tile):
            scores = matmul(query_scr[quad % 2], key_scr[span, start : start + tile])
            p_scr[quad % 2, :, start : start + tile] = jnp.exp2(scores * scale).astype(BF16)
        summed = matmul(p_scr[quad % 2], ext_scr[...])
        summed = summed[:, :LANES] / summed[:, LANES:]
        for pair in range(2):
            even = summed[2 * pair * share : (2 * pair + 1) * share]
            odd = summed[(2 * pair + 1) * share : (2 * pair + 2) * share]
            at = slice(quad * QUAD + pair * LANES, quad * QUAD + (pair + 1) * LANES)
            sum_ref[:share, at] = jnp.where(left, even, pltpu.roll(odd, HDIM, 1)).astype(BF16)
            sum_ref[share:, at] = jnp.where(left, pltpu.roll(even, HDIM, 1), odd).astype(BF16)


def finish_kernel(count, shares, high, margin_ref, *refs):
    first_ref, second_ref, direct_ref, back_ref, far_ref, near_ref = refs[:6]
    rows_ref, packed_first, packed_second, all_scr, square_scr = refs[6:]
    width = back_ref.shape[0]
    depth = back_ref.shape[1] - LANES
    share = first_ref.shape[0] // 2
    full = width * count
    total = share * count
    part = width // shares
    channels = direct_ref.shape[0] // 2
    group_pos = lax.axis_index("group")
    seq_pos = lax.axis_index("seq")
    sub = lax.rem(group_pos, shares)
    all_scr[:width, :] = back_ref[...]
    all_scr[full:, :] = direct_ref[...]
    for i, m in enumerate(high):
        for near, ref in ((0, far_ref), (1, near_ref)):
            place = jnp.bitwise_xor(sub, m ^ near) * part
            for k in range(1, count):
                all_scr[pl.ds(pl.multiple_of(place + k * width, part), part), :] = ref[i, k - 1]
    tile = 2 * LANES
    known = jnp.concatenate([first_ref[...], second_ref[...]], axis=0)
    for start in range(0, depth, tile):
        mixed = matmul(known, all_scr[:, start : start + tile])
        squares = mixed * mixed
        squares = squares[:, :LANES] + squares[:, LANES:]
        square_scr[...] = squares if start == 0 else square_scr[...] + squares
    score = matmul(known, all_scr[:, depth:])
    variance = jnp.sum(square_scr[...], axis=-1, keepdims=True) * (1.0 / depth)
    score = (score + pltpu.roll(score, channels, 1)) * lax.rsqrt(variance + 1e-05)
    position = iota((share, LANES), 0) + seq_pos * share
    left = iota((share // 2, LANES), 1) < channels
    for window, packed_ref in enumerate((packed_first, packed_second)):
        at = 2 * share * window
        own = total - margin_at(margin_ref, 2 * group_pos + window)
        margin = jnp.where(position >= own, score[at + share : at + 2 * share], 0.0)
        signed = score[at : at + share] - margin
        rows_ref[window] = signed
        packed_ref[...] = jnp.where(left, signed[: share // 2], signed[share // 2 :]).astype(BF16)


def combine_kernel(count, deltas, margin_ref, latent_ref, rows_ref, *refs):
    out_ref, tail_scr = refs[2 * len(deltas) :]
    channels, share = latent_ref.shape[1:]
    total = share * count
    group_pos = lax.axis_index("group")
    seq_pos = lax.axis_index("seq")
    for slot in range(2):
        before = margin_at(margin_ref, 2 * group_pos + slot - 1)
        own = total - margin_at(margin_ref, 2 * group_pos + slot)
        tail_scr[...] = jnp.zeros_like(tail_scr)
        for delta, ref in zip(deltas, refs[slot * len(deltas) : (slot + 1) * len(deltas)]):
            row = (seq_pos + delta) * share - (total - OVMAX)
            for half in range(2):
                value = ref[...].astype(F32)
                value = pltpu.roll(value, channels, 1) if half else value
                at = pl.ds(pl.multiple_of(row + half * (share // 2), share // 2), share // 2)
                tail_scr[at, :] = value
        moved = tail_scr[pl.ds(OVMAX - before + seq_pos * share, share), :]
        score = (rows_ref[slot] + moved).T[:channels]
        keep = iota(score.shape, 1) + seq_pos * share < own
        out_ref[slot] = jnp.where(keep, latent_ref[slot] + STEP * score, 0.0)


def body(latent, margin_len, in_weight, norm_gain, qkv_weight, out_weight, final_gain, head_out):
    count = lax.axis_size("seq")
    groups = lax.axis_size("group")
    share, channels = latent.shape[1:]
    total = share * count
    width, depth = out_weight.shape
    full = width * count
    shares = min(groups, width // 16)
    high = range(0, shares, 2)

    def across(value, group_by, pairs):
        moves = [
            (g * count + i, (g + group_by) * count + j)
            for g in range(groups)
            for i, j in pairs
            if 0 <= g + group_by < groups
        ]
        return lax.ppermute(value, ("group", "seq"), moves)

    def swap(value, bits):
        return lax.ppermute(value, "group", [(g, g ^ bits) for g in range(groups)])

    def gathered(value):
        return [lax.ppermute(value, "seq", [(i, (i + k) % count) for i in range(count)]) for k in range(1, count)]

    turned = latent.transpose(0, 2, 1)
    send, back, part, direct, gram = pl.pallas_call(
        functools.partial(fold_kernel, shares),
        out_shape=(
            jax.ShapeDtypeStruct((width + share, LANES), BF16),
            jax.ShapeDtypeStruct((width, depth + LANES), BF16),
            jax.ShapeDtypeStruct((width // shares, depth + LANES), BF16),
            jax.ShapeDtypeStruct((2 * channels, depth + LANES), BF16),
            jax.ShapeDtypeStruct((channels, 2 * LANES), BF16),
        ),
        in_specs=[VMEM] * 7,
        out_specs=(VMEM,) * 5,
        cost_estimate=pl.CostEstimate(flops=width * depth * 1200, bytes_accessed=8 * width * depth, transcendentals=0),
        name="fold",
    )(turned, in_weight, norm_gain[None, :], qkv_weight, out_weight, final_gain[None, :], head_out.T)
    own_part = jnp.stack(gathered(part))
    pieces = [send] + gathered(send)
    stacked = jnp.stack([piece[width:] for piece in pieces])
    following = across(stacked, -1, [(i, i) for i in range(count)])

    def attend(window):
        rows = 4 * share
        extra = [following] if window else []
        return pl.pallas_call(
            functools.partial(attend_kernel, count, window),
            out_shape=jax.ShapeDtypeStruct((2 * share, full + LANES), BF16),
            in_specs=[SMEM] + [VMEM] * (count + len(extra) + 1),
            out_specs=VMEM,
            scratch_shapes=[
                pltpu.VMEM((total, LANES), F32),
                pltpu.VMEM((OVMAX + total, LANES), F32),
                pltpu.VMEM((total, LANES), BF16),
                pltpu.VMEM((full, LANES), BF16),
                pltpu.VMEM((full, total), BF16),
                pltpu.VMEM((2, rows, QUAD), BF16),
                pltpu.VMEM((2, rows, total), BF16),
                pltpu.VMEM((total, QUAD), BF16),
            ],
            cost_estimate=pl.CostEstimate(
                flops=16 * share * total * full,
                bytes_accessed=4 * full * share,
                transcendentals=share * total * full // HDIM,
            ),
            name="attend",
        )(margin_len, *pieces, gram, *extra)

    first = attend(0)
    second = attend(1)
    planes = [swap(own_part, bits) for bits in high[1:]]
    far = jnp.stack([own_part] + planes)
    near = swap(far, 1)
    rows, *tails = pl.pallas_call(
        functools.partial(finish_kernel, count, shares, list(high)),
        out_shape=(
            jax.ShapeDtypeStruct((2, share, LANES), F32),
            jax.ShapeDtypeStruct((share // 2, LANES), BF16),
            jax.ShapeDtypeStruct((share // 2, LANES), BF16),
        ),
        in_specs=[SMEM] + [VMEM] * 6,
        out_specs=(VMEM, VMEM, VMEM),
        scratch_shapes=[
            pltpu.VMEM((full + 2 * channels, depth + LANES), BF16),
            pltpu.VMEM((4 * share, LANES), F32),
        ],
        cost_estimate=pl.CostEstimate(
            flops=8 * share * full * depth, bytes_accessed=2 * full * depth, transcendentals=0
        ),
        name="finish",
    )(margin_len, first, second, direct, back, far, near)

    deltas = list(range((total - OVMAX) // share, count))
    received = []
    for window, group_by in ((1, 1), (0, 0)):
        received += [across(tails[window], group_by, [(i, i - d) for i in range(d, count)]) for d in deltas]
    turned = pl.pallas_call(
        functools.partial(combine_kernel, count, deltas),
        out_shape=jax.ShapeDtypeStruct(turned.shape, F32),
        in_specs=[SMEM] + [VMEM] * (2 + len(received)),
        out_specs=VMEM,
        scratch_shapes=[pltpu.VMEM((OVMAX + total + share, LANES), F32)],
        name="combine",
    )(margin_len, turned, rows, *received)
    return turned.transpose(0, 2, 1)


def solution(mesh):
    in_specs = (
        P("group", "seq", None),
        P(),
        P(),
        P(),
        P(None, None, "seq"),
        P("seq", None),
        P(),
        P(),
    )
    out_specs = P("group", "seq", None)

    return jax.shard_map(body, mesh=mesh, in_specs=in_specs, out_specs=out_specs, check_vma=False)
```

time: 97.2 us -> 89.4 us (0.920)
  waiting for transfers between devices: 30.7 us -> 19.3 us
  starting transfers between devices: 23.4 us -> 28.1 us
    ppermute x4, waiting for transfers between devices: 12.1 us -> 4.4 us  [swap(): return lax.ppermute(value, 'group', [(g, g ^ bits) for g in range(groups)])]
    ppermute x9 -> x6, waiting for transfers between devices: 11 us -> 5.36 us  [gathered(): lax.ppermute(value, 'seq', [(i, (i + k) % count) for i in range(count)])]
    ppermute x9 -> x6, starting transfers between devices: 9.94 us -> 13.9 us  [gathered(): lax.ppermute(value, 'seq', [(i, (i + k) % count) for i in range(count)])]
    ppermute x4, starting transfers between devices: 4.83 us -> 6.92 us  [swap(): return lax.ppermute(value, 'group', [(g, g ^ bits) for g in range(groups)])]
    ppermute x5, waiting for transfers between devices: 7.57 us -> 9.54 us  [across(): return lax.ppermute(value, ('group', 'seq'), moves)]
    pallas_call x1 -> x0, local copies, waits for them, and re-layouts: 1.72 us -> none  [body(): pl.pallas_call(functools.partial(combine_kernel, count, deltas), out_shap...]
    ppermute x5, starting transfers between devices: 8.61 us -> 7.28 us  [across(): return lax.ppermute(value, ('group', 'seq'), moves)]
    pallas_call x1, Pallas kernels: 10 us -> 8.72 us  [body(): pl.pallas_call(functools.partial(finish_kernel, count, shares, list(high)...]
  transfers between devices with their start and end apart: 18 -> 15, of which waited for: 11 -> 5; matrix products, arithmetic and copies ran while one was open for 2% -> 1% of each run, Pallas kernels for 19% -> 21%
where the time goes in v1:
time: 89.4 us; the launch traced here: 88.7 us
  Pallas kernels  35 us (39%)
  starting transfers between devices  28.1 us (31%)
  waiting for transfers between devices  19.3 us (22%)
  local copies, waits for them, and re-layouts  5.8 us (6%)
    pallas_call x2, Pallas kernels, attend(): pl.pallas_call(functools.partial(attend_kernel, count, window), out_shape...  19 us
    ppermute x6, starting transfers between devices, gathered(): lax.ppermute(value, 'seq', [(i, (i + k) % count) for i in range(count)])  13.9 us
    ppermute x5, waiting for transfers between devices, across(): return lax.ppermute(value, ('group', 'seq'), moves)  9.54 us
    pallas_call x1, Pallas kernels, body(): pl.pallas_call(functools.partial(finish_kernel, count, shares, list(high)...  8.72 us
    ppermute x5, starting transfers between devices, across(): return lax.ppermute(value, ('group', 'seq'), moves)  7.28 us
    ppermute x4, starting transfers between devices, swap(): return lax.ppermute(value, 'group', [(g, g ^ bits) for g in range(groups)])  6.92 us
    pallas_call x1, Pallas kernels, body(): pl.pallas_call(functools.partial(fold_kernel, shares), out_shape=(jax.Sha...  5.38 us
    ppermute x6, waiting for transfers between devices, gathered(): lax.ppermute(value, 'seq', [(i, (i + k) % count) for i in range(count)])  5.36 us
  transfers between devices with their start and end apart: 15, of which 5 were waited for; matrix products, arithmetic and copies ran while one was open for 1% of the time, Pallas kernels for 21%

profile of v1, /device:TPU:1, one launch (start us, length us, event | category | flops | bytes accessed | tf_op | source)
XLA Modules:
  0.0 88.7 jit_solution(6206040460508858458)
XLA Ops:
  0.0 1.3 %broadcast_in_dim.6.gain_ref = f32[1,1536]{1,0:T(1,128)} reshape(f32[1536]{0:T(1024)} %param.11) | data formatting | bytes 12288 | tf_op jit(solution)/shard_map/broadcast_in_dim | solution.py:300
  1.3 1.3 %broadcast_in_dim.7.final_ref = f32[1,1536]{1,0:T(1,128)} reshape(f32[1536]{0:T(1024)} %param.14) | data formatting | bytes 12288 | tf_op jit(solution)/shard_map/broadcast_in_dim | solution.py:300
  2.6 5.4 %fold.1 = (bf16[512,128]{1,0:T(8,128)(2,1)}, bf16[256,1664]{1,0:T(8,128)(2,1)}, bf16[32,1664]{1,0:T(8,128)(2,1)}, bf16[128,1664]{1,0:T(8,128)(2,1)}, bf16[64,256]{1,0:T(8,128)(2,1)}) custom-call(f32[2,64,256]{2,1,0:T(8,128)} %bitcast.19, bf16[64,1536]{1,0:T(8,128)(2,1)} %in_ref.1, f32[1,1536]{1,0:T(1,128)} %broadcast_in_dim.6.gain_ref, ...), custom_call_target="tpu_custom_call" | custom-call | flops 471859200 | bytes 3145728 | tf_op jit(solution)/shard_map/fold/pallas_call | solution.py:287
  8.0 4.1 %collective-permute-start.6 = (bf16[32,1664]{1,0:T(8,128)(2,1)}, bf16[32,1664]{1,0:T(8,128)(2,1)S(1)}, u32[]{:S(2)}, u32[]{:S(2)}) collective-permute-start(bf16[32,1664]{1,0:T(8,128)(2,1)} %get-tuple-element.17), channel_id=1, source_target_pairs={{0,3},{1,0},{2,1},{3,2},{4,7},{5,4},{6,5},{7,6},{8,11},{9,8},{10,9... | collective-permute-start | bytes 319496 | tf_op jit(solution)/shard_map/ppermute | solution.py:284
  12.1 0.0 collective-permute-start.5
  12.1 0.5 collective-permute-start.4
  12.6 2.8 %collective-permute-start.2 = (bf16[512,128]{1,0:T(8,128)(2,1)}, bf16[512,128]{1,0:T(8,128)(2,1)S(1)}, u32[]{:S(2)}, u32[]{:S(2)}) collective-permute-start(bf16[512,128]{1,0:T(8,128)(2,1)} %get-tuple-element.13.refs_0_), channel_id=1, source_target_pairs={{0,3},{1,0},{2,1},{3,2},{4,7},{5,4},{6,5},{7,6},{8,11},{9,8},{10,9... | collective-permute-start | bytes 393224 | tf_op jit(solution)/shard_map/ppermute | solution.py:284
  15.4 0.6 collective-permute-start.1
  15.9 0.0 collective-permute-done.6
  15.9 5.4 %collective-permute-done.5 = bf16[32,1664]{1,0:T(8,128)(2,1)S(1)} collective-permute-done((bf16[32,1664]{1,0:T(8,128)(2,1)}, bf16[32,1664]{1,0:T(8,128)(2,1)S(1)}, u32[]{:S(2)}, u32[]{:S(2)}) %collective-permute-start.5) | collective-permute-done | bytes 106528 | tf_op jit(solution)/shard_map/ppermute | solution.py:284
  21.3 0.0 collective-permute-done.4
  21.3 0.1 fusion
  21.4 1.3 %collective-permute-start.8 = (bf16[3,32,1664]{2,1,0:T(8,128)(2,1)S(1)}, bf16[3,32,1664]{2,1,0:T(8,128)(2,1)S(1)}, u32[]{:S(2)}, u32[]{:S(2)}) collective-permute-start(bf16[3,32,1664]{2,1,0:T(8,128)(2,1)S(1)} %get-tuple-element.22), channel_id=1, source_target_pairs={{0,16},{4,20},{8,24},{12,28},{16,0},{20,4},{24,8},{28,12},{1,17},{... | collective-permute-start | bytes 958472 | tf_op jit(solution)/shard_map/ppermute | solution.py:281
  22.7 1.2 %collective-permute-start.7 = (bf16[3,32,1664]{2,1,0:T(8,128)(2,1)S(1)}, bf16[3,32,1664]{2,1,0:T(8,128)(2,1)S(1)}, u32[]{:S(2)}, u32[]{:S(2)}) collective-permute-start(bf16[3,32,1664]{2,1,0:T(8,128)(2,1)S(1)} %get-tuple-element.22), channel_id=1, source_target_pairs={{0,8},{4,12},{8,0},{12,4},{16,24},{20,28},{24,16},{28,20},{1,9},{5... | collective-permute-start | bytes 958472 | tf_op jit(solution)/shard_map/ppermute | solution.py:281
  23.9 0.2 collective-permute-start.9
  24.1 0.8 slice_bitcast_fusion.3
  24.9 0.0 collective-permute-done.2.refs_3_
  24.9 5.9 %collective-permute-start = (bf16[512,128]{1,0:T(8,128)(2,1)}, bf16[512,128]{1,0:T(8,128)(2,1)S(1)}, u32[]{:S(2)}, u32[]{:S(2)}) collective-permute-start(bf16[512,128]{1,0:T(8,128)(2,1)} %get-tuple-element.13.refs_0_), channel_id=1, source_target_pairs={{0,1},{1,2},{2,3},{3,0},{4,5},{5,6},{6,7},{7,4},{8,9},{9,10},{10,1... | collective-permute-start | bytes 393224 | tf_op jit(solution)/shard_map/ppermute | solution.py:284
  30.8 0.0 collective-permute-done.8
  30.8 0.0 collective-permute-done.7
  30.9 4.4 %collective-permute-done.9 = bf16[3,32,1664]{2,1,0:T(8,128)(2,1)S(1)} collective-permute-done((bf16[3,32,1664]{2,1,0:T(8,128)(2,1)S(1)}, bf16[3,32,1664]{2,1,0:T(8,128)(2,1)S(1)}, u32[]{:S(2)}, u32[]{:S(2)}) %collective-permute-start.9) | collective-permute-done | bytes 319520 | tf_op jit(solution)/shard_map/ppermute | solution.py:281
  35.3 0.2 pad_maximum_fusion.refs_4_
  35.5 0.0 copy-done.5
  35.5 0.0 copy-start
  35.5 4.2 %collective-permute-start.10 = (bf16[4,3,32,1664]{3,2,1,0:T(8,128)(2,1)S(1)}, bf16[4,3,32,1664]{3,2,1,0:T(8,128)(2,1)S(1)}, u32[]{:S(2)}, u32[]{:S(2)}) collective-permute-start(bf16[4,3,32,1664]{3,2,1,0:T(8,128)(2,1)S(1)} %pad_maximum_fusion.refs_4_), channel_id=1, source_target_pairs={{0,4},{4,0},{8,12},{12,8},{16,20},{20,16},{24,28},{28,24},{1,5},{5... | collective-permute-start | bytes 3833864 | tf_op jit(solution)/shard_map/ppermute | solution.py:281
  39.7 0.0 collective-permute-done.1.refs_2_
  39.7 0.0 collective-permute-done.refs_1_
  39.7 0.0 copy-start.7
  39.8 2.1 %collective-permute-start.3 = (bf16[4,256,128]{2,1,0:T(8,128)(2,1)S(1)}, bf16[4,256,128]{2,1,0:T(8,128)(2,1)S(1)}, u32[]{:S(2)}, u32[]{:S(2)}) collective-permute-start(bf16[4,256,128]{2,1,0:T(8,128)(2,1)S(1)} %pad_maximum_fusion.2), channel_id=1, source_target_pairs={{4,0},{5,1},{6,2},{7,3},{8,4},{9,5},{10,6},{11,7},{12,8},{13,9},{1... | collective-permute-start | bytes 786440 | tf_op jit(solution)/shard_map/ppermute | solution.py:278
  41.9 9.3 %attend.2.refs_0_ = bf16[512,1152]{1,0:T(8,128)(2,1)} custom-call(s32[15]{0:T(128)} %margin_ref.7, bf16[512,128]{1,0:T(8,128)(2,1)} %get-tuple-element.13.refs_0_, bf16[512,128]{1,0:T(8,128)(2,1)} %copy-done.7, bf16[512,128]{1,0:T(8,128)(2,1)} %copy-done.6, bf16[512,128]{1,0:T(8,128)(2,1)} %copy-done.5, bf16[64,256]{1,0:T(8,128)(2,1)} %get-tuple-element.14.refs_4_), custom_call_target="tpu_custom_call" | custom-call | flops 4294967296 | bytes 1048576 | tf_op jit(solution)/shard_map/attend/pallas_call | solution.py:309
  51.2 0.0 collective-permute-done.3.refs_5_
  51.2 0.7 copy-done.9
  51.9 9.7 %attend.3.refs_1_ = bf16[512,1152]{1,0:T(8,128)(2,1)} custom-call(s32[15]{0:T(128)} %margin_ref.7, bf16[512,128]{1,0:T(8,128)(2,1)} %get-tuple-element.13.refs_0_, bf16[512,128]{1,0:T(8,128)(2,1)} %copy-done.7, bf16[512,128]{1,0:T(8,128)(2,1)} %copy-done.6, bf16[512,128]{1,0:T(8,128)(2,1)} %copy-done.5, bf16[64,256]{1,0:T(8,128)(2,1)} %get-tuple-element.14.refs_4_, ...), custom_call_target="tpu_custom_call" | custom-call | flops 4294967296 | bytes 1048576 | tf_op jit(solution)/shard_map/attend/pallas_call | solution.py:309
  61.6 0.0 collective-permute-done.10.refs_5_
  61.6 1.0 %copy-done.8 = bf16[4,3,32,1664]{3,2,1,0:T(8,128)(2,1)} copy-done((bf16[4,3,32,1664]{3,2,1,0:T(8,128)(2,1)}, bf16[4,3,32,1664]{3,2,1,0:T(8,128)(2,1)S(1)}, u32[]{:S(2)}) %copy-start.8) | copy-done | bytes 1277976
  62.6 8.7 %finish.1 = (f32[2,256,128]{2,1,0:T(8,128)}, bf16[128,128]{1,0:T(8,128)(2,1)}, bf16[128,128]{1,0:T(8,128)(2,1)}) custom-call(s32[15]{0:T(128)} %margin_ref.7, bf16[512,1152]{1,0:T(8,128)(2,1)} %attend.2.refs_0_, bf16[512,1152]{1,0:T(8,128)(2,1)} %attend.3.refs_1_, bf16[128,1664]{1,0:T(8,128)(2,1)} %get-tuple-element.15.refs_2_, ...), custom_call_target="tpu_custom_call" | custom-call | flops 3221225472 | bytes 3145728 | tf_op jit(solution)/shard_map/finish/pallas_call | solution.py:337
  71.4 1.3 %collective-permute-start.12 = (bf16[128,128]{1,0:T(8,128)(2,1)}, bf16[128,128]{1,0:T(8,128)(2,1)S(1)}, u32[]{:S(2)}, u32[]{:S(2)}) collective-permute-start(bf16[128,128]{1,0:T(8,128)(2,1)} %get-tuple-element.19), channel_id=1, source_target_pairs={{3,4},{7,8},{11,12},{15,16},{19,20},{23,24},{27,28}} | collective-permute-start | bytes 98312 | tf_op jit(solution)/shard_map/ppermute | solution.py:278
  72.7 1.3 %collective-permute-start.11 = (bf16[128,128]{1,0:T(8,128)(2,1)}, bf16[128,128]{1,0:T(8,128)(2,1)S(1)}, u32[]{:S(2)}, u32[]{:S(2)}) collective-permute-start(bf16[128,128]{1,0:T(8,128)(2,1)} %get-tuple-element.19), channel_id=1, source_target_pairs={{2,4},{3,5},{6,8},{7,9},{10,12},{11,13},{14,16},{15,17},{18,20},{1... | collective-permute-start | bytes 98312 | tf_op jit(solution)/shard_map/ppermute | solution.py:278
  74.0 1.3 %collective-permute-start.14 = (bf16[128,128]{1,0:T(8,128)(2,1)}, bf16[128,128]{1,0:T(8,128)(2,1)S(1)}, u32[]{:S(2)}, u32[]{:S(2)}) collective-permute-start(bf16[128,128]{1,0:T(8,128)(2,1)} %get-tuple-element.20), channel_id=1, source_target_pairs={{3,0},{7,4},{11,8},{15,12},{19,16},{23,20},{27,24},{31,28}} | collective-permute-start | bytes 98312 | tf_op jit(solution)/shard_map/ppermute | solution.py:278
  75.3 1.3 %collective-permute-start.13 = (bf16[128,128]{1,0:T(8,128)(2,1)}, bf16[128,128]{1,0:T(8,128)(2,1)S(1)}, u32[]{:S(2)}, u32[]{:S(2)}) collective-permute-start(bf16[128,128]{1,0:T(8,128)(2,1)} %get-tuple-element.20), channel_id=1, source_target_pairs={{2,0},{3,1},{6,4},{7,5},{10,8},{11,9},{14,12},{15,13},{18,16},{19,... | collective-permute-start | bytes 98312 | tf_op jit(solution)/shard_map/ppermute | solution.py:278
  76.6 2.0 %collective-permute-done.12.refs_1_ = bf16[128,128]{1,0:T(8,128)(2,1)S(1)} collective-permute-done((bf16[128,128]{1,0:T(8,128)(2,1)}, bf16[128,128]{1,0:T(8,128)(2,1)S(1)}, u32[]{:S(2)}, u32[]{:S(2)}) %collective-permute-start.12) | collective-permute-done | bytes 32800 | tf_op jit(solution)/shard_map/ppermute | solution.py:278
  78.6 3.6 %collective-permute-done.11.refs_0_ = bf16[128,128]{1,0:T(8,128)(2,1)S(1)} collective-permute-done((bf16[128,128]{1,0:T(8,128)(2,1)}, bf16[128,128]{1,0:T(8,128)(2,1)S(1)}, u32[]{:S(2)}, u32[]{:S(2)}) %collective-permute-start.11) | collective-permute-done | bytes 32800 | tf_op jit(solution)/shard_map/ppermute | solution.py:278
  82.2 3.9 %collective-permute-done.14.refs_3_ = bf16[128,128]{1,0:T(8,128)(2,1)S(1)} collective-permute-done((bf16[128,128]{1,0:T(8,128)(2,1)}, bf16[128,128]{1,0:T(8,128)(2,1)S(1)}, u32[]{:S(2)}, u32[]{:S(2)}) %collective-permute-start.14) | collective-permute-done | bytes 32800 | tf_op jit(solution)/shard_map/ppermute | solution.py:278
  86.1 0.0 collective-permute-done.13.refs_2_
  86.1 0.0 copy-done.2
  86.1 0.6 copy-done.3
  86.7 0.0 copy-done.4
  86.7 2.0 %combine.1 = f32[2,64,256]{2,1,0:T(8,128)} custom-call(s32[15]{0:T(128)} %margin_ref.7, f32[2,64,256]{2,1,0:T(8,128)} %bitcast.20, f32[2,256,128]{2,1,0:T(8,128)} %get-tuple-element.18.rows_ref, bf16[128,128]{1,0:T(8,128)(2,1)} %copy-done.2, bf16[128,128]{1,0:T(8,128)(2,1)} %copy-done.1, bf16[128,128]{1,0:T(8,128)(2,1)} %copy-done.4, bf16[128,128]{1,0:T(8,128)(2,1)} %copy-done.3), custom_call_target="tpu_custom_call" | custom-call | tf_op jit(solution)/shard_map/combine/pallas_call | solution.py:360
  (16 shorter events, 0.1 us)
Async XLA Ops:
  8.0 8.0 %collective-permute-start.6 = (bf16[32,1664]{1,0:T(8,128)(2,1)}, bf16[32,1664]{1,0:T(8,128)(2,1)S(1)}, u32[]{:S(2)}, u32[]{:S(2)}) collective-permute-start(bf16[32,1664]{1,0:T(8,128)(2,1)} %get-tuple-element.17), channel_id=1, source_target_pairs={{0,3},{1,0},{2,1},{3,2},{4,7},{5,4},{6,5},{7,6},{8,11},{9,8},{10,9... | collective-permute-start | bytes 319496 | tf_op jit(solution)/shard_map/ppermute | solution.py:284
  12.1 9.2 %collective-permute-start.5 = (bf16[32,1664]{1,0:T(8,128)(2,1)}, bf16[32,1664]{1,0:T(8,128)(2,1)S(1)}, u32[]{:S(2)}, u32[]{:S(2)}) collective-permute-start(bf16[32,1664]{1,0:T(8,128)(2,1)} %get-tuple-element.17), channel_id=1, source_target_pairs={{0,2},{1,3},{2,0},{3,1},{4,6},{5,7},{6,4},{7,5},{8,10},{9,11},{10,... | collective-permute-start | bytes 319496 | tf_op jit(solution)/shard_map/ppermute | solution.py:284
  12.1 9.2 %collective-permute-start.4 = (bf16[32,1664]{1,0:T(8,128)(2,1)}, bf16[32,1664]{1,0:T(8,128)(2,1)S(1)}, u32[]{:S(2)}, u32[]{:S(2)}) collective-permute-start(bf16[32,1664]{1,0:T(8,128)(2,1)} %get-tuple-element.17), channel_id=1, source_target_pairs={{0,1},{1,2},{2,3},{3,0},{4,5},{5,6},{6,7},{7,4},{8,9},{9,10},{10,1... | collective-permute-start | bytes 319496 | tf_op jit(solution)/shard_map/ppermute | solution.py:284
  12.6 12.4 %collective-permute-start.2 = (bf16[512,128]{1,0:T(8,128)(2,1)}, bf16[512,128]{1,0:T(8,128)(2,1)S(1)}, u32[]{:S(2)}, u32[]{:S(2)}) collective-permute-start(bf16[512,128]{1,0:T(8,128)(2,1)} %get-tuple-element.13.refs_0_), channel_id=1, source_target_pairs={{0,3},{1,0},{2,1},{3,2},{4,7},{5,4},{6,5},{7,6},{8,11},{9,8},{10,9... | collective-permute-start | bytes 393224 | tf_op jit(solution)/shard_map/ppermute | solution.py:284
  15.4 24.3 %collective-permute-start.1 = (bf16[512,128]{1,0:T(8,128)(2,1)}, bf16[512,128]{1,0:T(8,128)(2,1)S(1)}, u32[]{:S(2)}, u32[]{:S(2)}) collective-permute-start(bf16[512,128]{1,0:T(8,128)(2,1)} %get-tuple-element.13.refs_0_), channel_id=1, source_target_pairs={{0,2},{1,3},{2,0},{3,1},{4,6},{5,7},{6,4},{7,5},{8,10},{9,11},{10,... | collective-permute-start | bytes 393224 | tf_op jit(solution)/shard_map/ppermute | solution.py:284
  21.4 9.5 %collective-permute-start.8 = (bf16[3,32,1664]{2,1,0:T(8,128)(2,1)S(1)}, bf16[3,32,1664]{2,1,0:T(8,128)(2,1)S(1)}, u32[]{:S(2)}, u32[]{:S(2)}) collective-permute-start(bf16[3,32,1664]{2,1,0:T(8,128)(2,1)S(1)} %get-tuple-element.22), channel_id=1, source_target_pairs={{0,16},{4,20},{8,24},{12,28},{16,0},{20,4},{24,8},{28,12},{1,17},{... | collective-permute-start | bytes 958472 | tf_op jit(solution)/shard_map/ppermute | solution.py:281
  22.7 8.2 %collective-permute-start.7 = (bf16[3,32,1664]{2,1,0:T(8,128)(2,1)S(1)}, bf16[3,32,1664]{2,1,0:T(8,128)(2,1)S(1)}, u32[]{:S(2)}, u32[]{:S(2)}) collective-permute-start(bf16[3,32,1664]{2,1,0:T(8,128)(2,1)S(1)} %get-tuple-element.22), channel_id=1, source_target_pairs={{0,8},{4,12},{8,0},{12,4},{16,24},{20,28},{24,16},{28,20},{1,9},{5... | collective-permute-start | bytes 958472 | tf_op jit(solution)/shard_map/ppermute | solution.py:281
  23.9 11.3 %collective-permute-start.9 = (bf16[3,32,1664]{2,1,0:T(8,128)(2,1)S(1)}, bf16[3,32,1664]{2,1,0:T(8,128)(2,1)S(1)}, u32[]{:S(2)}, u32[]{:S(2)}) collective-permute-start(bf16[3,32,1664]{2,1,0:T(8,128)(2,1)S(1)} %get-tuple-element.22), channel_id=1, source_target_pairs={{0,24},{4,28},{8,16},{12,20},{16,8},{20,12},{24,0},{28,4},{1,25},{... | collective-permute-start | bytes 958472 | tf_op jit(solution)/shard_map/ppermute | solution.py:281
  24.9 10.5 %copy-start.5 = (bf16[512,128]{1,0:T(8,128)(2,1)}, bf16[512,128]{1,0:T(8,128)(2,1)S(1)}, u32[]{:S(2)}) copy-start(bf16[512,128]{1,0:T(8,128)(2,1)S(1)} %collective-permute-done.2.refs_3_) | copy-start | bytes 393220
  24.9 14.8 %collective-permute-start = (bf16[512,128]{1,0:T(8,128)(2,1)}, bf16[512,128]{1,0:T(8,128)(2,1)S(1)}, u32[]{:S(2)}, u32[]{:S(2)}) collective-permute-start(bf16[512,128]{1,0:T(8,128)(2,1)} %get-tuple-element.13.refs_0_), channel_id=1, source_target_pairs={{0,1},{1,2},{2,3},{3,0},{4,5},{5,6},{6,7},{7,4},{8,9},{9,10},{10,1... | collective-permute-start | bytes 393224 | tf_op jit(solution)/shard_map/ppermute | solution.py:284
  35.5 15.7 %copy-start = (bf16[4,3,32,1664]{3,2,1,0:T(8,128)(2,1)}, bf16[4,3,32,1664]{3,2,1,0:T(8,128)(2,1)S(1)}, u32[]{:S(2)}) copy-start(bf16[4,3,32,1664]{3,2,1,0:T(8,128)(2,1)S(1)} %pad_maximum_fusion.refs_4_) | copy-start | bytes 3833860
  35.5 26.1 %collective-permute-start.10 = (bf16[4,3,32,1664]{3,2,1,0:T(8,128)(2,1)S(1)}, bf16[4,3,32,1664]{3,2,1,0:T(8,128)(2,1)S(1)}, u32[]{:S(2)}, u32[]{:S(2)}) collective-permute-start(bf16[4,3,32,1664]{3,2,1,0:T(8,128)(2,1)S(1)} %pad_maximum_fusion.refs_4_), channel_id=1, source_target_pairs={{0,4},{4,0},{8,12},{12,8},{16,20},{20,16},{24,28},{28,24},{1,5},{5... | collective-permute-start | bytes 3833864 | tf_op jit(solution)/shard_map/ppermute | solution.py:281
  39.7 2.2 %copy-start.6 = (bf16[512,128]{1,0:T(8,128)(2,1)}, bf16[512,128]{1,0:T(8,128)(2,1)S(1)}, u32[]{:S(2)}) copy-start(bf16[512,128]{1,0:T(8,128)(2,1)S(1)} %collective-permute-done.1.refs_2_) | copy-start | bytes 393220
  39.7 2.2 %copy-start.7 = (bf16[512,128]{1,0:T(8,128)(2,1)}, bf16[512,128]{1,0:T(8,128)(2,1)S(1)}, u32[]{:S(2)}) copy-start(bf16[512,128]{1,0:T(8,128)(2,1)S(1)} %collective-permute-done.refs_1_) | copy-start | bytes 393220
  39.8 11.4 %collective-permute-start.3 = (bf16[4,256,128]{2,1,0:T(8,128)(2,1)S(1)}, bf16[4,256,128]{2,1,0:T(8,128)(2,1)S(1)}, u32[]{:S(2)}, u32[]{:S(2)}) collective-permute-start(bf16[4,256,128]{2,1,0:T(8,128)(2,1)S(1)} %pad_maximum_fusion.2), channel_id=1, source_target_pairs={{4,0},{5,1},{6,2},{7,3},{8,4},{9,5},{10,6},{11,7},{12,8},{13,9},{1... | collective-permute-start | bytes 786440 | tf_op jit(solution)/shard_map/ppermute | solution.py:278
  51.2 0.7 copy-start.9
  61.6 1.0 %copy-start.8 = (bf16[4,3,32,1664]{3,2,1,0:T(8,128)(2,1)}, bf16[4,3,32,1664]{3,2,1,0:T(8,128)(2,1)S(1)}, u32[]{:S(2)}) copy-start(bf16[4,3,32,1664]{3,2,1,0:T(8,128)(2,1)S(1)} %collective-permute-done.10.refs_5_) | copy-start | bytes 3833860
  71.4 7.2 %collective-permute-start.12 = (bf16[128,128]{1,0:T(8,128)(2,1)}, bf16[128,128]{1,0:T(8,128)(2,1)S(1)}, u32[]{:S(2)}, u32[]{:S(2)}) collective-permute-start(bf16[128,128]{1,0:T(8,128)(2,1)} %get-tuple-element.19), channel_id=1, source_target_pairs={{3,4},{7,8},{11,12},{15,16},{19,20},{23,24},{27,28}} | collective-permute-start | bytes 98312 | tf_op jit(solution)/shard_map/ppermute | solution.py:278
  72.7 9.5 %collective-permute-start.11 = (bf16[128,128]{1,0:T(8,128)(2,1)}, bf16[128,128]{1,0:T(8,128)(2,1)S(1)}, u32[]{:S(2)}, u32[]{:S(2)}) collective-permute-start(bf16[128,128]{1,0:T(8,128)(2,1)} %get-tuple-element.19), channel_id=1, source_target_pairs={{2,4},{3,5},{6,8},{7,9},{10,12},{11,13},{14,16},{15,17},{18,20},{1... | collective-permute-start | bytes 98312 | tf_op jit(solution)/shard_map/ppermute | solution.py:278
  74.0 12.1 %collective-permute-start.14 = (bf16[128,128]{1,0:T(8,128)(2,1)}, bf16[128,128]{1,0:T(8,128)(2,1)S(1)}, u32[]{:S(2)}, u32[]{:S(2)}) collective-permute-start(bf16[128,128]{1,0:T(8,128)(2,1)} %get-tuple-element.20), channel_id=1, source_target_pairs={{3,0},{7,4},{11,8},{15,12},{19,16},{23,20},{27,24},{31,28}} | collective-permute-start | bytes 98312 | tf_op jit(solution)/shard_map/ppermute | solution.py:278
  75.3 10.8 %collective-permute-start.13 = (bf16[128,128]{1,0:T(8,128)(2,1)}, bf16[128,128]{1,0:T(8,128)(2,1)S(1)}, u32[]{:S(2)}, u32[]{:S(2)}) collective-permute-start(bf16[128,128]{1,0:T(8,128)(2,1)} %get-tuple-element.20), channel_id=1, source_target_pairs={{2,0},{3,1},{6,4},{7,5},{10,8},{11,9},{14,12},{15,13},{18,16},{19,... | collective-permute-start | bytes 98312 | tf_op jit(solution)/shard_map/ppermute | solution.py:278
  78.6 7.5 %copy-start.1 = (bf16[128,128]{1,0:T(8,128)(2,1)}, bf16[128,128]{1,0:T(8,128)(2,1)S(1)}, u32[]{:S(2)}) copy-start(bf16[128,128]{1,0:T(8,128)(2,1)S(1)} %collective-permute-done.12.refs_1_) | copy-start | bytes 98308
  82.2 3.9 %copy-start.2 = (bf16[128,128]{1,0:T(8,128)(2,1)}, bf16[128,128]{1,0:T(8,128)(2,1)S(1)}, u32[]{:S(2)}) copy-start(bf16[128,128]{1,0:T(8,128)(2,1)S(1)} %collective-permute-done.11.refs_0_) | copy-start | bytes 98308
  86.1 0.6 copy-start.3
  86.1 0.6 copy-start.4

commit v2 on v1

--- a/solution.py
+++ b/solution.py
@@ -19,6 +19,10 @@
 SMEM = pl.BlockSpec(memory_space=pltpu.SMEM)
 
 
+def limit(mebibytes):
+    return pltpu.CompilerParams(vmem_limit_bytes=mebibytes << 20)
+
+
 def iota(shape, dim):
     return lax.broadcasted_iota(jnp.int32, shape, dim)
 
@@ -42,14 +46,13 @@
     return jnp.where((index >= 0) & (index < last), length, 0)
 
 
-def fold_kernel(shares, latent_ref, in_ref, gain_ref, qkv_ref, out_ref, final_ref, head_ref, *refs):
-    send_ref, back_ref, part_ref, direct_ref, gram_ref = refs
+def fold_kernel(shares, in_ref, gain_ref, qkv_ref, out_ref, final_ref, head_ref, *refs):
+    map_ref, back_ref, part_ref, direct_ref, gram_ref = refs
     weight = in_ref[...].astype(F32)
     channels, depth = weight.shape
     width = out_ref.shape[0]
-    share = latent_ref.shape[2]
     centered = weight - jnp.mean(weight, axis=-1, keepdims=True)
-    both = jnp.concatenate(split(centered * gain_ref[...]), axis=0)
+    both = jnp.concatenate(split(centered * gain_ref[...][None, :]), axis=0)
 
     def folded(which):
         product = matmul(both, qkv_ref[which])
@@ -63,7 +66,7 @@
     back = back - jnp.mean(back, axis=-1, keepdims=True)
     back_ref[:, :depth] = back.astype(BF16)
 
-    pieces = split(back * final_ref[...]) + split(centered * final_ref[...])
+    pieces = split(back * final_ref[...][None, :]) + split(centered * final_ref[...][None, :])
     scores = matmul_nt(jnp.concatenate(pieces, axis=0), head_ref[...])
     left = iota((width, LANES), 1) < channels
 
@@ -77,8 +80,7 @@
     sub = lax.rem(lax.axis_index("group"), shares)
     part_ref[...] = back_ref[pl.ds(pl.multiple_of(sub * rows, rows), rows), :]
 
-    send_ref[:width, :] = jnp.concatenate([folded(0), folded(1)], axis=0).T.astype(BF16)
-    send_ref[width:, :] = latent_ref[...].reshape(2 * channels, share).T.astype(BF16)
+    map_ref[...] = jnp.concatenate([folded(0), folded(1)], axis=0).T.astype(BF16)
 
     high, low = split(centered)
     direct_ref[:channels, :depth] = high
@@ -99,6 +101,7 @@
 
 def attend_kernel(count, window, margin_ref, *refs):
     piece_refs, refs = refs[:count], refs[count:]
+    map_refs, refs = refs[:count], refs[count:]
     gram_ref, refs = refs[0], refs[1:]
     if window:
         next_ref, refs = refs[0], refs[1:]
@@ -116,13 +119,13 @@
 
     next_scr[:OVMAX, :] = jnp.zeros((OVMAX, LANES), F32)
     for k in range(count):
-        source = lax.rem(seq_pos + (count - k), count) * share
+        source = jnp.bitwise_xor(seq_pos, k) * share
         at = pl.ds(pl.multiple_of(source, share), share)
         after = pl.ds(pl.multiple_of(source + OVMAX, share), share)
-        slot = piece_refs[k][width:, :].astype(F32)
+        slot = piece_refs[k][...].astype(F32)
         slot_scr[at, :] = pltpu.roll(slot, channels, 1) if window else slot
         next_scr[after, :] = next_ref[k].astype(F32) if window else pltpu.roll(slot, channels, 1)
-        map_scr[k * width : (k + 1) * width, :] = piece_refs[k][:width, :]
+        map_scr[k * width : (k + 1) * width, :] = map_refs[k][...]
     left = iota((OVMAX, LANES), 1) < channels
     for start in range(0, total, OVMAX):
         rows = slot_scr[start : start + OVMAX, :]
@@ -281,27 +284,30 @@
         return lax.ppermute(value, "group", [(g, g ^ bits) for g in range(groups)])
 
     def gathered(value):
-        return [lax.ppermute(value, "seq", [(i, (i + k) % count) for i in range(count)]) for k in range(1, count)]
+        return [lax.ppermute(value, "seq", [(i, i ^ k) for i in range(count)]) for k in range(1, count)]
 
     turned = latent.transpose(0, 2, 1)
-    send, back, part, direct, gram = pl.pallas_call(
+    packed = jnp.concatenate([latent[0], latent[1]], axis=1).astype(BF16)
+    pieces = [packed] + gathered(packed)
+    stacked = jnp.stack(pieces)
+    following = across(stacked, -1, [(i, i) for i in range(count)])
+    maps, back, part, direct, gram = pl.pallas_call(
         functools.partial(fold_kernel, shares),
         out_shape=(
-            jax.ShapeDtypeStruct((width + share, LANES), BF16),
+            jax.ShapeDtypeStruct((width, LANES), BF16),
             jax.ShapeDtypeStruct((width, depth + LANES), BF16),
             jax.ShapeDtypeStruct((width // shares, depth + LANES), BF16),
             jax.ShapeDtypeStruct((2 * channels, depth + LANES), BF16),
             jax.ShapeDtypeStruct((channels, 2 * LANES), BF16),
         ),
-        in_specs=[VMEM] * 7,
+        in_specs=[VMEM] * 6,
+        compiler_params=limit(20),
         out_specs=(VMEM,) * 5,
         cost_estimate=pl.CostEstimate(flops=width * depth * 1200, bytes_accessed=8 * width * depth, transcendentals=0),
         name="fold",
-    )(turned, in_weight, norm_gain[None, :], qkv_weight, out_weight, final_gain[None, :], head_out.T)
+    )(in_weight, norm_gain, qkv_weight, out_weight, final_gain, head_out.T)
     own_part = jnp.stack(gathered(part))
-    pieces = [send] + gathered(send)
-    stacked = jnp.stack([piece[width:] for piece in pieces])
-    following = across(stacked, -1, [(i, i) for i in range(count)])
+    map_pieces = [maps] + gathered(maps)
 
     def attend(window):
         rows = 4 * share
@@ -309,7 +315,8 @@
         return pl.pallas_call(
             functools.partial(attend_kernel, count, window),
             out_shape=jax.ShapeDtypeStruct((2 * share, full + LANES), BF16),
-            in_specs=[SMEM] + [VMEM] * (count + len(extra) + 1),
+            in_specs=[SMEM] + [VMEM] * (2 * count + len(extra) + 1),
+            compiler_params=limit(32),
             out_specs=VMEM,
             scratch_shapes=[
                 pltpu.VMEM((total, LANES), F32),
@@ -327,7 +334,7 @@
                 transcendentals=share * total * full // HDIM,
             ),
             name="attend",
-        )(margin_len, *pieces, gram, *extra)
+        )(margin_len, *pieces, *map_pieces, gram, *extra)
 
     first = attend(0)
     second = attend(1)
@@ -342,6 +349,7 @@
             jax.ShapeDtypeStruct((share // 2, LANES), BF16),
         ),
         in_specs=[SMEM] + [VMEM] * 6,
+        compiler_params=limit(24),
         out_specs=(VMEM, VMEM, VMEM),
         scratch_shapes=[
             pltpu.VMEM((full + 2 * channels, depth + LANES), BF16),
@@ -361,6 +369,7 @@
         functools.partial(combine_kernel, count, deltas),
         out_shape=jax.ShapeDtypeStruct(turned.shape, F32),
         in_specs=[SMEM] + [VMEM] * (2 + len(received)),
+        compiler_params=limit(8),
         out_specs=VMEM,
         scratch_shapes=[pltpu.VMEM((OVMAX + total + share, LANES), F32)],
         name="combine",

time: 89.4 us -> 95.5 us (1.068)
  waiting for transfers between devices: 19.3 us -> 31.9 us
  Pallas kernels: 35 us -> 25.2 us
  local copies, waits for them, and re-layouts: 5.8 us -> 11.3 us
  starting transfers between devices: 28.1 us -> 23.8 us
  other arithmetic: 0.28 us -> 2.18 us
    ppermute x4, waiting for transfers between devices: 4.4 us -> 12.8 us  [swap(): return lax.ppermute(value, 'group', [(g, g ^ bits) for g in range(groups)])]
    unnamed x20 -> x32, local copies, waits for them, and re-layouts: 2.35 us -> 10.6 us
    ppermute x6 -> x9, waiting for transfers between devices: 5.36 us -> 12.7 us  [gathered(): lax.ppermute(value, 'seq', [(i, i ^ k) for i in range(count)])]
    ppermute x6 -> x9, starting transfers between devices: 13.9 us -> 10.2 us  [gathered(): lax.ppermute(value, 'seq', [(i, i ^ k) for i in range(count)])]
    pallas_call x2, Pallas kernels: 19 us -> 15.6 us  [attend(): pl.pallas_call(functools.partial(attend_kernel, count, window), out_shape...]
    ppermute x5, waiting for transfers between devices: 9.54 us -> 6.36 us  [across(): return lax.ppermute(value, ('group', 'seq'), moves)]
    pallas_call x1, Pallas kernels: 5.38 us -> 2.33 us  [body(): pl.pallas_call(functools.partial(fold_kernel, shares), out_shape=(jax.Sha...]
    pallas_call x1, Pallas kernels: 8.72 us -> 5.8 us  [body(): pl.pallas_call(functools.partial(finish_kernel, count, shares, list(high)...]
  transfers between devices with their start and end apart: 15 -> 18, of which waited for: 5 -> 11; matrix products, arithmetic and copies ran while one was open for 1% -> 6% of each run, Pallas kernels for 21% -> 17%
where the time goes in v2:
time: 95.5 us; the launch traced here: 94.6 us
  waiting for transfers between devices  31.9 us (33%)
  Pallas kernels  25.2 us (26%)
  starting transfers between devices  23.8 us (25%)
  local copies, waits for them, and re-layouts  11.3 us (12%)
  other arithmetic  2.18 us (2%)
    pallas_call x2, Pallas kernels, attend(): pl.pallas_call(functools.partial(attend_kernel, count, window), out_shape...  15.6 us
    ppermute x4, waiting for transfers between devices, swap(): return lax.ppermute(value, 'group', [(g, g ^ bits) for g in range(groups)])  12.8 us
    ppermute x9, waiting for transfers between devices, gathered(): lax.ppermute(value, 'seq', [(i, i ^ k) for i in range(count)])  12.7 us
    unnamed x32, local copies, waits for them, and re-layouts  10.6 us
    ppermute x9, starting transfers between devices, gathered(): lax.ppermute(value, 'seq', [(i, i ^ k) for i in range(count)])  10.2 us
    ppermute x5, starting transfers between devices, across(): return lax.ppermute(value, ('group', 'seq'), moves)  8.35 us
    ppermute x5, waiting for transfers between devices, across(): return lax.ppermute(value, ('group', 'seq'), moves)  6.36 us
    pallas_call x1, Pallas kernels, body(): pl.pallas_call(functools.partial(finish_kernel, count, shares, list(high)...  5.8 us
  transfers between devices with their start and end apart: 18, of which 11 were waited for; matrix products, arithmetic and copies ran while one was open for 6% of the time, Pallas kernels for 17%

profile of v2, /device:TPU:1, one launch (start us, length us, event | category | flops | bytes accessed | tf_op | source)
XLA Modules:
  0.0 94.6 jit_solution(15931543944099404529)
XLA Ops:
  0.0 1.7 %copy-done = bf16[3,1536,256]{2,1,0:T(8,128)(2,1)S(1)} copy-done((bf16[3,1536,256]{2,1,0:T(8,128)(2,1)S(1)}, bf16[3,1536,256]{2,1,0:T(8,128)(2,1)}, u32[]{:S(2)}) %copy-start) | copy-done | bytes 2359320
  1.7 1.1 %copy-done.1 = bf16[256,1536]{1,0:T(8,128)(2,1)S(1)} copy-done((bf16[256,1536]{1,0:T(8,128)(2,1)S(1)}, bf16[256,1536]{1,0:T(8,128)(2,1)}, u32[]{:S(2)}) %copy-start.1) | copy-done | bytes 786456
  2.8 0.9 copy-done.3
  3.7 0.9 copy-done.4
  4.7 0.7 copy-done.5
  5.4 0.7 copy-done.6
  6.0 2.3 %fold.1 = (bf16[256,128]{1,0:T(8,128)(2,1)S(1)}, bf16[256,1664]{1,0:T(8,128)(2,1)S(1)}, bf16[32,1664]{1,0:T(8,128)(2,1)S(1)}, bf16[128,1664]{1,0:T(8,128)(2,1)S(1)}, bf16[64,256]{1,0:T(8,128)(2,1)S(1)}) custom-call(bf16[64,1536]{1,0:T(8,128)(2,1)S(1)} %copy-done.3, f32[1536]{0:T(1024)S(1)} %copy-done.5, bf16[3,1536,256]{2,1,0:T(8,128)(2,1)S(1)} %copy-done, ...), custom_call_target="tpu_custom_call" | custom-call | flops 471859200 | bytes 3145728 | tf_op jit(solution)/shard_map/fold/pallas_call | solution.py:294
  8.4 4.2 %collective-permute-start.9 = (bf16[32,1664]{1,0:T(8,128)(2,1)S(1)}, bf16[32,1664]{1,0:T(8,128)(2,1)S(1)}, u32[]{:S(2)}, u32[]{:S(2)}) collective-permute-start(bf16[32,1664]{1,0:T(8,128)(2,1)S(1)} %get-tuple-element.17), channel_id=1, source_target_pairs={{0,3},{1,2},{2,1},{3,0},{4,7},{5,6},{6,5},{7,4},{8,11},{9,10},{10,... | collective-permute-start | bytes 319496 | tf_op jit(solution)/shard_map/ppermute | solution.py:287
  12.6 0.4 collective-permute-start.7
  13.0 2.4 %collective-permute-done.9 = bf16[32,1664]{1,0:T(8,128)(2,1)S(1)} collective-permute-done((bf16[32,1664]{1,0:T(8,128)(2,1)S(1)}, bf16[32,1664]{1,0:T(8,128)(2,1)S(1)}, u32[]{:S(2)}, u32[]{:S(2)}) %collective-permute-start.9) | collective-permute-done | bytes 106528 | tf_op jit(solution)/shard_map/ppermute | solution.py:287
  15.3 5.8 %collective-permute-done.8 = bf16[32,1664]{1,0:T(8,128)(2,1)S(1)} collective-permute-done((bf16[32,1664]{1,0:T(8,128)(2,1)S(1)}, bf16[32,1664]{1,0:T(8,128)(2,1)S(1)}, u32[]{:S(2)}, u32[]{:S(2)}) %collective-permute-start.8) | collective-permute-done | bytes 106528 | tf_op jit(solution)/shard_map/ppermute | solution.py:287
  21.2 0.0 collective-permute-done.7
  21.2 0.1 fusion
  21.2 1.3 %collective-permute-start.11 = (bf16[3,32,1664]{2,1,0:T(8,128)(2,1)S(1)}, bf16[3,32,1664]{2,1,0:T(8,128)(2,1)S(1)}, u32[]{:S(2)}, u32[]{:S(2)}) collective-permute-start(bf16[3,32,1664]{2,1,0:T(8,128)(2,1)S(1)} %get-tuple-element.22), channel_id=1, source_target_pairs={{0,16},{4,20},{8,24},{12,28},{16,0},{20,4},{24,8},{28,12},{1,17},{... | collective-permute-start | bytes 958472 | tf_op jit(solution)/shard_map/ppermute | solution.py:284
  22.6 1.2 %collective-permute-start.10 = (bf16[3,32,1664]{2,1,0:T(8,128)(2,1)S(1)}, bf16[3,32,1664]{2,1,0:T(8,128)(2,1)S(1)}, u32[]{:S(2)}, u32[]{:S(2)}) collective-permute-start(bf16[3,32,1664]{2,1,0:T(8,128)(2,1)S(1)} %get-tuple-element.22), channel_id=1, source_target_pairs={{0,8},{4,12},{8,0},{12,4},{16,24},{20,28},{24,16},{28,20},{1,9},{5... | collective-permute-start | bytes 958472 | tf_op jit(solution)/shard_map/ppermute | solution.py:284
  23.8 0.2 collective-permute-start.12
  24.0 5.1 %collective-permute-done.11 = bf16[3,32,1664]{2,1,0:T(8,128)(2,1)S(1)} collective-permute-done((bf16[3,32,1664]{2,1,0:T(8,128)(2,1)S(1)}, bf16[3,32,1664]{2,1,0:T(8,128)(2,1)S(1)}, u32[]{:S(2)}, u32[]{:S(2)}) %collective-permute-start.11) | collective-permute-done | bytes 319520 | tf_op jit(solution)/shard_map/ppermute | solution.py:284
  29.1 1.0 %collective-permute-done.10 = bf16[3,32,1664]{2,1,0:T(8,128)(2,1)S(1)} collective-permute-done((bf16[3,32,1664]{2,1,0:T(8,128)(2,1)S(1)}, bf16[3,32,1664]{2,1,0:T(8,128)(2,1)S(1)}, u32[]{:S(2)}, u32[]{:S(2)}) %collective-permute-start.10) | collective-permute-done | bytes 319520 | tf_op jit(solution)/shard_map/ppermute | solution.py:284
  30.0 6.8 %collective-permute-done.12 = bf16[3,32,1664]{2,1,0:T(8,128)(2,1)S(1)} collective-permute-done((bf16[3,32,1664]{2,1,0:T(8,128)(2,1)S(1)}, bf16[3,32,1664]{2,1,0:T(8,128)(2,1)S(1)}, u32[]{:S(2)}, u32[]{:S(2)}) %collective-permute-start.12) | collective-permute-done | bytes 319520 | tf_op jit(solution)/shard_map/ppermute | solution.py:284
  36.8 0.2 pad_maximum_fusion.refs_4_
  37.0 2.5 %collective-permute-start.13 = (bf16[4,3,32,1664]{3,2,1,0:T(8,128)(2,1)S(1)}, bf16[4,3,32,1664]{3,2,1,0:T(8,128)(2,1)S(1)}, u32[]{:S(2)}, u32[]{:S(2)}) collective-permute-start(bf16[4,3,32,1664]{3,2,1,0:T(8,128)(2,1)S(1)} %pad_maximum_fusion.refs_4_), channel_id=1, source_target_pairs={{0,4},{4,0},{8,12},{12,8},{16,20},{20,16},{24,28},{28,24},{1,5},{5... | collective-permute-start | bytes 3833864 | tf_op jit(solution)/shard_map/ppermute | solution.py:284
  39.6 0.6 fusion.1
  40.2 1.5 %copy.11 = bf16[1,256,64]{2,1,0:T(8,128)(2,1)} copy(bf16[1,256,64]{1,2,0:T(8,128)(2,1)} %get-tuple-element.23) | data formatting | bytes 65536
  41.7 1.5 %copy.12 = bf16[1,256,64]{2,1,0:T(8,128)(2,1)} copy(bf16[1,256,64]{1,2,0:T(8,128)(2,1)} %get-tuple-element.24) | data formatting | bytes 65536
  43.2 1.0 %pad_maximum_fusion.3.refs_0_ = bf16[256,128]{1,0:T(8,128)(2,1)S(1)} fusion(bf16[256,64]{1,0:T(8,128)(2,1)} %bitcast.22, bf16[256,64]{1,0:T(8,128)(2,1)} %bitcast.21), kind=kLoop, calls=%fused_computation.3 | loop fusion | flops 131072 | bytes 131072 | tf_op jit(solution)/shard_map/concatenate | solution.py:290
  44.2 2.1 %collective-permute-start.2 = (bf16[256,128]{1,0:T(8,128)(2,1)S(1)}, bf16[256,128]{1,0:T(8,128)(2,1)S(1)}, u32[]{:S(2)}, u32[]{:S(2)}) collective-permute-start(bf16[256,128]{1,0:T(8,128)(2,1)S(1)} %pad_maximum_fusion.3.refs_0_), channel_id=1, source_target_pairs={{0,3},{1,2},{2,1},{3,0},{4,7},{5,6},{6,5},{7,4},{8,11},{9,10},{10,... | collective-permute-start | bytes 196616 | tf_op jit(solution)/shard_map/ppermute | solution.py:287
  46.2 1.5 %collective-permute-start = (bf16[256,128]{1,0:T(8,128)(2,1)S(1)}, bf16[256,128]{1,0:T(8,128)(2,1)S(1)}, u32[]{:S(2)}, u32[]{:S(2)}) collective-permute-start(bf16[256,128]{1,0:T(8,128)(2,1)S(1)} %pad_maximum_fusion.3.refs_0_), channel_id=1, source_target_pairs={{0,1},{1,0},{2,3},{3,2},{4,5},{5,4},{6,7},{7,6},{8,9},{9,8},{10,11... | collective-permute-start | bytes 196616 | tf_op jit(solution)/shard_map/ppermute | solution.py:287
  47.8 2.0 %collective-permute-start.5 = (bf16[256,128]{1,0:T(8,128)(2,1)}, bf16[256,128]{1,0:T(8,128)(2,1)S(1)}, u32[]{:S(2)}, u32[]{:S(2)}) collective-permute-start(bf16[256,128]{1,0:T(8,128)(2,1)} %copy-done.10), channel_id=1, source_target_pairs={{0,3},{1,2},{2,1},{3,0},{4,7},{5,6},{6,5},{7,4},{8,11},{9,10},{10,... | collective-permute-start | bytes 196616 | tf_op jit(solution)/shard_map/ppermute | solution.py:287
  49.8 0.0 collective-permute-start.4
  49.8 3.6 %collective-permute-done.1.refs_2_ = bf16[256,128]{1,0:T(8,128)(2,1)S(1)} collective-permute-done((bf16[256,128]{1,0:T(8,128)(2,1)S(1)}, bf16[256,128]{1,0:T(8,128)(2,1)S(1)}, u32[]{:S(2)}, u32[]{:S(2)}) %collective-permute-start.1) | collective-permute-done | bytes 65568 | tf_op jit(solution)/shard_map/ppermute | solution.py:287
  53.4 1.0 %pad_maximum_fusion.2 = bf16[4,256,128]{2,1,0:T(8,128)(2,1)S(1)} fusion(bf16[1,256,128]{2,1,0:T(8,128)(2,1)S(1)} %bitcast.18, bf16[1,256,128]{2,1,0:T(8,128)(2,1)S(1)} %bitcast.19, bf16[1,256,128]{2,1,0:T(8,128)(2,1)S(1)} %bitcast.20, bf16[1,256,64]{2,1,0:T(8,128)(2,1)} %copy.12, bf16[1,256,64]{2,1,0:T(8,128)(2,1)} %copy.11), kind=kLoop, calls=%fused_computation.2 | loop fusion | flops 1310720 | bytes 524288 | tf_op jit(solution)/shard_map/stack | solution.py:292
  54.3 3.2 %collective-permute-start.6 = (bf16[4,256,128]{2,1,0:T(8,128)(2,1)S(1)}, bf16[4,256,128]{2,1,0:T(8,128)(2,1)S(1)}, u32[]{:S(2)}, u32[]{:S(2)}) collective-permute-start(bf16[4,256,128]{2,1,0:T(8,128)(2,1)S(1)} %pad_maximum_fusion.2), channel_id=1, source_target_pairs={{4,0},{5,1},{6,2},{7,3},{8,4},{9,5},{10,6},{11,7},{12,8},{13,9},{1... | collective-permute-start | bytes 786440 | tf_op jit(solution)/shard_map/ppermute | solution.py:281
  57.5 0.0 collective-permute-done.5.refs_7_
  57.5 0.9 collective-permute-done.4.refs_6_
  58.5 0.8 copy-done.11
  59.3 0.8 copy-done.14
  60.1 7.7 %attend.2.refs_0_ = bf16[512,1152]{1,0:T(8,128)(2,1)S(1)} custom-call(s32[15]{0:T(128)S(1)} %copy-done.7, bf16[256,128]{1,0:T(8,128)(2,1)S(1)} %pad_maximum_fusion.3.refs_0_, bf16[256,128]{1,0:T(8,128)(2,1)S(1)} %collective-permute-done.refs_1_, bf16[256,128]{1,0:T(8,128)(2,1)S(1)} %collective-permute-done.1.refs_2_, ...), custom_call_target="tpu_custom_call" | custom-call | flops 4294967296 | bytes 1048576 | tf_op jit(solution)/shard_map/attend/pallas_call | solution.py:315
  67.8 7.9 %attend.3.refs_1_ = bf16[512,1152]{1,0:T(8,128)(2,1)S(1)} custom-call(s32[15]{0:T(128)S(1)} %copy-done.7, bf16[256,128]{1,0:T(8,128)(2,1)S(1)} %pad_maximum_fusion.3.refs_0_, bf16[256,128]{1,0:T(8,128)(2,1)S(1)} %collective-permute-done.refs_1_, bf16[256,128]{1,0:T(8,128)(2,1)S(1)} %collective-permute-done.1.refs_2_, ...), custom_call_target="tpu_custom_call" | custom-call | flops 4294967296 | bytes 1048576 | tf_op jit(solution)/shard_map/attend/pallas_call | solution.py:315
  75.8 5.8 %finish.1 = (f32[2,256,128]{2,1,0:T(8,128)S(1)}, bf16[128,128]{1,0:T(8,128)(2,1)S(1)}, bf16[128,128]{1,0:T(8,128)(2,1)S(1)}) custom-call(s32[15]{0:T(128)S(1)} %copy-done.7, bf16[512,1152]{1,0:T(8,128)(2,1)S(1)} %attend.2.refs_0_, bf16[512,1152]{1,0:T(8,128)(2,1)S(1)} %attend.3.refs_1_, bf16[128,1664]{1,0:T(8,128)(2,1)S(1)} %copy-done.9, ...), custom_call_target="tpu_custom_call" | custom-call | flops 3221225472 | bytes 3145728 | tf_op jit(solution)/shard_map/finish/pallas_call | solution.py:344
  81.6 1.3 %collective-permute-start.15 = (bf16[128,128]{1,0:T(8,128)(2,1)S(1)}, bf16[128,128]{1,0:T(8,128)(2,1)S(1)}, u32[]{:S(2)}, u32[]{:S(2)}) collective-permute-start(bf16[128,128]{1,0:T(8,128)(2,1)S(1)} %get-tuple-element.19), channel_id=1, source_target_pairs={{3,4},{7,8},{11,12},{15,16},{19,20},{23,24},{27,28}} | collective-permute-start | bytes 98312 | tf_op jit(solution)/shard_map/ppermute | solution.py:281
  82.9 1.3 %collective-permute-start.14 = (bf16[128,128]{1,0:T(8,128)(2,1)S(1)}, bf16[128,128]{1,0:T(8,128)(2,1)S(1)}, u32[]{:S(2)}, u32[]{:S(2)}) collective-permute-start(bf16[128,128]{1,0:T(8,128)(2,1)S(1)} %get-tuple-element.19), channel_id=1, source_target_pairs={{2,4},{3,5},{6,8},{7,9},{10,12},{11,13},{14,16},{15,17},{18,20},{1... | collective-permute-start | bytes 98312 | tf_op jit(solution)/shard_map/ppermute | solution.py:281
  84.2 1.3 %collective-permute-start.17 = (bf16[128,128]{1,0:T(8,128)(2,1)S(1)}, bf16[128,128]{1,0:T(8,128)(2,1)S(1)}, u32[]{:S(2)}, u32[]{:S(2)}) collective-permute-start(bf16[128,128]{1,0:T(8,128)(2,1)S(1)} %get-tuple-element.20), channel_id=1, source_target_pairs={{3,0},{7,4},{11,8},{15,12},{19,16},{23,20},{27,24},{31,28}} | collective-permute-start | bytes 98312 | tf_op jit(solution)/shard_map/ppermute | solution.py:281
  85.5 1.3 %collective-permute-start.16 = (bf16[128,128]{1,0:T(8,128)(2,1)S(1)}, bf16[128,128]{1,0:T(8,128)(2,1)S(1)}, u32[]{:S(2)}, u32[]{:S(2)}) collective-permute-start(bf16[128,128]{1,0:T(8,128)(2,1)S(1)} %get-tuple-element.20), channel_id=1, source_target_pairs={{2,0},{3,1},{6,4},{7,5},{10,8},{11,9},{14,12},{15,13},{18,16},{19,... | collective-permute-start | bytes 98312 | tf_op jit(solution)/shard_map/ppermute | solution.py:281
  86.8 1.8 %collective-permute-done.15.refs_1_ = bf16[128,128]{1,0:T(8,128)(2,1)S(1)} collective-permute-done((bf16[128,128]{1,0:T(8,128)(2,1)S(1)}, bf16[128,128]{1,0:T(8,128)(2,1)S(1)}, u32[]{:S(2)}, u32[]{:S(2)}) %collective-permute-start.15) | collective-permute-done | bytes 32800 | tf_op jit(solution)/shard_map/ppermute | solution.py:281
  88.6 0.4 collective-permute-done.14.refs_0_
  89.0 4.0 %collective-permute-done.17.refs_3_ = bf16[128,128]{1,0:T(8,128)(2,1)S(1)} collective-permute-done((bf16[128,128]{1,0:T(8,128)(2,1)S(1)}, bf16[128,128]{1,0:T(8,128)(2,1)S(1)}, u32[]{:S(2)}, u32[]{:S(2)}) %collective-permute-start.17) | collective-permute-done | bytes 32800 | tf_op jit(solution)/shard_map/ppermute | solution.py:281
  93.0 0.2 collective-permute-done.16.refs_2_
  93.1 1.5 %combine.1 = f32[2,64,256]{2,1,0:T(8,128)} custom-call(s32[15]{0:T(128)S(1)} %copy-done.7, f32[2,64,256]{2,1,0:T(8,128)S(1)} %bitcast.16, f32[2,256,128]{2,1,0:T(8,128)S(1)} %get-tuple-element.18.rows_ref, bf16[128,128]{1,0:T(8,128)(2,1)S(1)} %collective-permute-done.14.refs_0_, bf16[128,128]{1,0:T(8,128)(2,1)S(1)} %collective-permute-done.15.refs_1_, ...), custom_call_target="tpu_custom_call" | custom-call | tf_op jit(solution)/shard_map/combine/pallas_call | solution.py:368
  (30 shorter events, 0.1 us)
Async XLA Ops:
  0.0 1.7 %copy-start = (bf16[3,1536,256]{2,1,0:T(8,128)(2,1)S(1)}, bf16[3,1536,256]{2,1,0:T(8,128)(2,1)}, u32[]{:S(2)}) copy-start(bf16[3,1536,256]{2,1,0:T(8,128)(2,1)} %qkv_ref.1) | copy-start | bytes 7077892
  1.7 1.1 %copy-start.1 = (bf16[256,1536]{1,0:T(8,128)(2,1)S(1)}, bf16[256,1536]{1,0:T(8,128)(2,1)}, u32[]{:S(2)}) copy-start(bf16[256,1536]{1,0:T(8,128)(2,1)} %out_ref.1) | copy-start | bytes 2359300
  2.8 0.9 copy-start.3
  3.7 0.9 copy-start.4
  4.7 0.7 copy-start.5
  5.4 0.7 copy-start.6
  8.4 28.6 %copy-start.8 = (bf16[128,1664]{1,0:T(8,128)(2,1)}, bf16[128,1664]{1,0:T(8,128)(2,1)S(1)}, u32[]{:S(2)}) copy-start(bf16[128,1664]{1,0:T(8,128)(2,1)S(1)} %get-tuple-element.15.refs_2_) | copy-start | bytes 1277956
  8.4 28.6 %copy-start.10 = (bf16[256,128]{1,0:T(8,128)(2,1)}, bf16[256,128]{1,0:T(8,128)(2,1)S(1)}, u32[]{:S(2)}) copy-start(bf16[256,128]{1,0:T(8,128)(2,1)S(1)} %get-tuple-element.13.refs_4_) | copy-start | bytes 196612
  8.4 28.6 %copy-start.13 = (bf16[64,256]{1,0:T(8,128)(2,1)}, bf16[64,256]{1,0:T(8,128)(2,1)S(1)}, u32[]{:S(2)}) copy-start(bf16[64,256]{1,0:T(8,128)(2,1)S(1)} %get-tuple-element.14.refs_8_) | copy-start | bytes 98308
  8.4 6.9 %collective-permute-start.9 = (bf16[32,1664]{1,0:T(8,128)(2,1)S(1)}, bf16[32,1664]{1,0:T(8,128)(2,1)S(1)}, u32[]{:S(2)}, u32[]{:S(2)}) collective-permute-start(bf16[32,1664]{1,0:T(8,128)(2,1)S(1)} %get-tuple-element.17), channel_id=1, source_target_pairs={{0,3},{1,2},{2,1},{3,0},{4,7},{5,6},{6,5},{7,4},{8,11},{9,10},{10,... | collective-permute-start | bytes 319496 | tf_op jit(solution)/shard_map/ppermute | solution.py:287
  12.6 8.6 %collective-permute-start.8 = (bf16[32,1664]{1,0:T(8,128)(2,1)S(1)}, bf16[32,1664]{1,0:T(8,128)(2,1)S(1)}, u32[]{:S(2)}, u32[]{:S(2)}) collective-permute-start(bf16[32,1664]{1,0:T(8,128)(2,1)S(1)} %get-tuple-element.17), channel_id=1, source_target_pairs={{0,2},{1,3},{2,0},{3,1},{4,6},{5,7},{6,4},{7,5},{8,10},{9,11},{10,... | collective-permute-start | bytes 319496 | tf_op jit(solution)/shard_map/ppermute | solution.py:287
  12.6 8.6 %collective-permute-start.7 = (bf16[32,1664]{1,0:T(8,128)(2,1)S(1)}, bf16[32,1664]{1,0:T(8,128)(2,1)S(1)}, u32[]{:S(2)}, u32[]{:S(2)}) collective-permute-start(bf16[32,1664]{1,0:T(8,128)(2,1)S(1)} %get-tuple-element.17), channel_id=1, source_target_pairs={{0,1},{1,0},{2,3},{3,2},{4,5},{5,4},{6,7},{7,6},{8,9},{9,8},{10,11... | collective-permute-start | bytes 319496 | tf_op jit(solution)/shard_map/ppermute | solution.py:287
  21.2 7.8 %collective-permute-start.11 = (bf16[3,32,1664]{2,1,0:T(8,128)(2,1)S(1)}, bf16[3,32,1664]{2,1,0:T(8,128)(2,1)S(1)}, u32[]{:S(2)}, u32[]{:S(2)}) collective-permute-start(bf16[3,32,1664]{2,1,0:T(8,128)(2,1)S(1)} %get-tuple-element.22), channel_id=1, source_target_pairs={{0,16},{4,20},{8,24},{12,28},{16,0},{20,4},{24,8},{28,12},{1,17},{... | collective-permute-start | bytes 958472 | tf_op jit(solution)/shard_map/ppermute | solution.py:284
  22.6 7.5 %collective-permute-start.10 = (bf16[3,32,1664]{2,1,0:T(8,128)(2,1)S(1)}, bf16[3,32,1664]{2,1,0:T(8,128)(2,1)S(1)}, u32[]{:S(2)}, u32[]{:S(2)}) collective-permute-start(bf16[3,32,1664]{2,1,0:T(8,128)(2,1)S(1)} %get-tuple-element.22), channel_id=1, source_target_pairs={{0,8},{4,12},{8,0},{12,4},{16,24},{20,28},{24,16},{28,20},{1,9},{5... | collective-permute-start | bytes 958472 | tf_op jit(solution)/shard_map/ppermute | solution.py:284
  23.8 13.0 %collective-permute-start.12 = (bf16[3,32,1664]{2,1,0:T(8,128)(2,1)S(1)}, bf16[3,32,1664]{2,1,0:T(8,128)(2,1)S(1)}, u32[]{:S(2)}, u32[]{:S(2)}) collective-permute-start(bf16[3,32,1664]{2,1,0:T(8,128)(2,1)S(1)} %get-tuple-element.22), channel_id=1, source_target_pairs={{0,24},{4,28},{8,16},{12,20},{16,8},{20,12},{24,0},{28,4},{1,25},{... | collective-permute-start | bytes 958472 | tf_op jit(solution)/shard_map/ppermute | solution.py:284
  36.8 2.8 %copy-start.2 = (f32[2,256,64]{1,2,0:T(8,128)S(1)}, f32[2,256,64]{1,2,0:T(8,128)}, u32[]{:S(2)}) copy-start(f32[2,256,64]{1,2,0:T(8,128)} %param.8) | copy-start | bytes 393220
  36.8 21.7 %copy-start.7 = (s32[15]{0:T(128)S(1)}, s32[15]{0:T(128)}, u32[]{:S(2)}) copy-start(s32[15]{0:T(128)} %margin_ref.7) | copy-start | bytes 184
  37.0 38.7 %collective-permute-start.13 = (bf16[4,3,32,1664]{3,2,1,0:T(8,128)(2,1)S(1)}, bf16[4,3,32,1664]{3,2,1,0:T(8,128)(2,1)S(1)}, u32[]{:S(2)}, u32[]{:S(2)}) collective-permute-start(bf16[4,3,32,1664]{3,2,1,0:T(8,128)(2,1)S(1)} %pad_maximum_fusion.refs_4_), channel_id=1, source_target_pairs={{0,4},{4,0},{8,12},{12,8},{16,20},{20,16},{24,28},{28,24},{1,5},{5... | collective-permute-start | bytes 3833864 | tf_op jit(solution)/shard_map/ppermute | solution.py:284
  44.2 5.6 %collective-permute-start.2 = (bf16[256,128]{1,0:T(8,128)(2,1)S(1)}, bf16[256,128]{1,0:T(8,128)(2,1)S(1)}, u32[]{:S(2)}, u32[]{:S(2)}) collective-permute-start(bf16[256,128]{1,0:T(8,128)(2,1)S(1)} %pad_maximum_fusion.3.refs_0_), channel_id=1, source_target_pairs={{0,3},{1,2},{2,1},{3,0},{4,7},{5,6},{6,5},{7,4},{8,11},{9,10},{10,... | collective-permute-start | bytes 196616 | tf_op jit(solution)/shard_map/ppermute | solution.py:287
  46.2 7.1 %collective-permute-start.1 = (bf16[256,128]{1,0:T(8,128)(2,1)S(1)}, bf16[256,128]{1,0:T(8,128)(2,1)S(1)}, u32[]{:S(2)}, u32[]{:S(2)}) collective-permute-start(bf16[256,128]{1,0:T(8,128)(2,1)S(1)} %pad_maximum_fusion.3.refs_0_), channel_id=1, source_target_pairs={{0,2},{1,3},{2,0},{3,1},{4,6},{5,7},{6,4},{7,5},{8,10},{9,11},{10,... | collective-permute-start | bytes 196616 | tf_op jit(solution)/shard_map/ppermute | solution.py:287
  46.2 7.1 %collective-permute-start = (bf16[256,128]{1,0:T(8,128)(2,1)S(1)}, bf16[256,128]{1,0:T(8,128)(2,1)S(1)}, u32[]{:S(2)}, u32[]{:S(2)}) collective-permute-start(bf16[256,128]{1,0:T(8,128)(2,1)S(1)} %pad_maximum_fusion.3.refs_0_), channel_id=1, source_target_pairs={{0,1},{1,0},{2,3},{3,2},{4,5},{5,4},{6,7},{7,6},{8,9},{9,8},{10,11... | collective-permute-start | bytes 196616 | tf_op jit(solution)/shard_map/ppermute | solution.py:287
  47.8 9.8 %collective-permute-start.5 = (bf16[256,128]{1,0:T(8,128)(2,1)}, bf16[256,128]{1,0:T(8,128)(2,1)S(1)}, u32[]{:S(2)}, u32[]{:S(2)}) collective-permute-start(bf16[256,128]{1,0:T(8,128)(2,1)} %copy-done.10), channel_id=1, source_target_pairs={{0,3},{1,2},{2,1},{3,0},{4,7},{5,6},{6,5},{7,4},{8,11},{9,10},{10,... | collective-permute-start | bytes 196616 | tf_op jit(solution)/shard_map/ppermute | solution.py:287
  49.8 8.7 %collective-permute-start.4 = (bf16[256,128]{1,0:T(8,128)(2,1)}, bf16[256,128]{1,0:T(8,128)(2,1)S(1)}, u32[]{:S(2)}, u32[]{:S(2)}) collective-permute-start(bf16[256,128]{1,0:T(8,128)(2,1)} %copy-done.10), channel_id=1, source_target_pairs={{0,2},{1,3},{2,0},{3,1},{4,6},{5,7},{6,4},{7,5},{8,10},{9,11},{10,... | collective-permute-start | bytes 196616 | tf_op jit(solution)/shard_map/ppermute | solution.py:287
  53.4 5.1 %collective-permute-start.3 = (bf16[256,128]{1,0:T(8,128)(2,1)}, bf16[256,128]{1,0:T(8,128)(2,1)S(1)}, u32[]{:S(2)}, u32[]{:S(2)}) collective-permute-start(bf16[256,128]{1,0:T(8,128)(2,1)} %copy-done.10), channel_id=1, source_target_pairs={{0,1},{1,0},{2,3},{3,2},{4,5},{5,4},{6,7},{7,6},{8,9},{9,8},{10,11... | collective-permute-start | bytes 196616 | tf_op jit(solution)/shard_map/ppermute | solution.py:287
  54.3 13.5 %collective-permute-start.6 = (bf16[4,256,128]{2,1,0:T(8,128)(2,1)S(1)}, bf16[4,256,128]{2,1,0:T(8,128)(2,1)S(1)}, u32[]{:S(2)}, u32[]{:S(2)}) collective-permute-start(bf16[4,256,128]{2,1,0:T(8,128)(2,1)S(1)} %pad_maximum_fusion.2), channel_id=1, source_target_pairs={{4,0},{5,1},{6,2},{7,3},{8,4},{9,5},{10,6},{11,7},{12,8},{13,9},{1... | collective-permute-start | bytes 786440 | tf_op jit(solution)/shard_map/ppermute | solution.py:281
  58.5 0.8 copy-start.11
  59.3 0.8 copy-start.14
  60.1 7.7 %copy-start.12 = (bf16[256,128]{1,0:T(8,128)(2,1)S(1)}, bf16[256,128]{1,0:T(8,128)(2,1)}, u32[]{:S(2)}) copy-start(bf16[256,128]{1,0:T(8,128)(2,1)} %copy-done.10) | copy-start | bytes 196612
  67.8 8.0 %copy-start.9 = (bf16[128,1664]{1,0:T(8,128)(2,1)S(1)}, bf16[128,1664]{1,0:T(8,128)(2,1)}, u32[]{:S(2)}) copy-start(bf16[128,1664]{1,0:T(8,128)(2,1)} %copy-done.8) | copy-start | bytes 1277956
  81.6 7.0 %collective-permute-start.15 = (bf16[128,128]{1,0:T(8,128)(2,1)S(1)}, bf16[128,128]{1,0:T(8,128)(2,1)S(1)}, u32[]{:S(2)}, u32[]{:S(2)}) collective-permute-start(bf16[128,128]{1,0:T(8,128)(2,1)S(1)} %get-tuple-element.19), channel_id=1, source_target_pairs={{3,4},{7,8},{11,12},{15,16},{19,20},{23,24},{27,28}} | collective-permute-start | bytes 98312 | tf_op jit(solution)/shard_map/ppermute | solution.py:281
  82.9 6.1 %collective-permute-start.14 = (bf16[128,128]{1,0:T(8,128)(2,1)S(1)}, bf16[128,128]{1,0:T(8,128)(2,1)S(1)}, u32[]{:S(2)}, u32[]{:S(2)}) collective-permute-start(bf16[128,128]{1,0:T(8,128)(2,1)S(1)} %get-tuple-element.19), channel_id=1, source_target_pairs={{2,4},{3,5},{6,8},{7,9},{10,12},{11,13},{14,16},{15,17},{18,20},{1... | collective-permute-start | bytes 98312 | tf_op jit(solution)/shard_map/ppermute | solution.py:281
  84.2 8.8 %collective-permute-start.17 = (bf16[128,128]{1,0:T(8,128)(2,1)S(1)}, bf16[128,128]{1,0:T(8,128)(2,1)S(1)}, u32[]{:S(2)}, u32[]{:S(2)}) collective-permute-start(bf16[128,128]{1,0:T(8,128)(2,1)S(1)} %get-tuple-element.20), channel_id=1, source_target_pairs={{3,0},{7,4},{11,8},{15,12},{19,16},{23,20},{27,24},{31,28}} | collective-permute-start | bytes 98312 | tf_op jit(solution)/shard_map/ppermute | solution.py:281
  85.5 7.7 %collective-permute-start.16 = (bf16[128,128]{1,0:T(8,128)(2,1)S(1)}, bf16[128,128]{1,0:T(8,128)(2,1)S(1)}, u32[]{:S(2)}, u32[]{:S(2)}) collective-permute-start(bf16[128,128]{1,0:T(8,128)(2,1)S(1)} %get-tuple-element.20), channel_id=1, source_target_pairs={{2,0},{3,1},{6,4},{7,5},{10,8},{11,9},{14,12},{15,13},{18,16},{19,... | collective-permute-start | bytes 98312 | tf_op jit(solution)/shard_map/ppermute | solution.py:281

commit v3 on v2

--- a/solution.py
+++ b/solution.py
@@ -46,8 +46,17 @@
     return jnp.where((index >= 0) & (index < last), length, 0)
 
 
-def fold_kernel(shares, in_ref, gain_ref, qkv_ref, out_ref, final_ref, head_ref, *refs):
-    map_ref, back_ref, part_ref, direct_ref, gram_ref = refs
+def fold_kernel(shares, in_hbm, gain_hbm, qkv_hbm, out_hbm, final_hbm, head_hbm, *refs):
+    map_ref, back_ref, part_ref, direct_ref, gram_ref = refs[:5]
+    in_ref, gain_ref, qkv_ref, out_ref, final_ref, head_ref, sem = refs[5:]
+    pairs = [(in_hbm, in_ref), (gain_hbm, gain_ref), (qkv_hbm.at[2], qkv_ref.at[2]), (out_hbm, out_ref)]
+    pairs += [(final_hbm, final_ref), (head_hbm, head_ref)]
+    pairs += [(qkv_hbm.at[0], qkv_ref.at[0]), (qkv_hbm.at[1], qkv_ref.at[1])]
+    copies = [pltpu.make_async_copy(source, target, sem.at[i]) for i, (source, target) in enumerate(pairs)]
+    for copy in copies:
+        copy.start()
+    copies[0].wait()
+    copies[1].wait()
     weight = in_ref[...].astype(F32)
     channels, depth = weight.shape
     width = out_ref.shape[0]
@@ -58,7 +67,9 @@
         product = matmul(both, qkv_ref[which])
         return product[:channels] + product[channels:]
 
+    copies[2].wait()
     values = folded(2)
+    copies[3].wait()
     tiled = jnp.concatenate([values] * (width // HDIM), axis=0)
     same = iota((width, width), 0) // channels == iota((width, width), 1) // HDIM
     high, low = split(jnp.where(same, tiled, 0.0))
@@ -66,6 +77,8 @@
     back = back - jnp.mean(back, axis=-1, keepdims=True)
     back_ref[:, :depth] = back.astype(BF16)
 
+    copies[4].wait()
+    copies[5].wait()
     pieces = split(back * final_ref[...][None, :]) + split(centered * final_ref[...][None, :])
     scores = matmul_nt(jnp.concatenate(pieces, axis=0), head_ref[...])
     left = iota((width, LANES), 1) < channels
@@ -80,6 +93,8 @@
     sub = lax.rem(lax.axis_index("group"), shares)
     part_ref[...] = back_ref[pl.ds(pl.multiple_of(sub * rows, rows), rows), :]
 
+    copies[6].wait()
+    copies[7].wait()
     map_ref[...] = jnp.concatenate([folded(0), folded(1)], axis=0).T.astype(BF16)
 
     high, low = split(centered)
@@ -197,54 +212,54 @@
             sum_ref[share:, at] = jnp.where(left, pltpu.roll(even, HDIM, 1), odd).astype(BF16)
 
 
-def finish_kernel(count, shares, high, margin_ref, *refs):
-    first_ref, second_ref, direct_ref, back_ref, far_ref, near_ref = refs[:6]
-    rows_ref, packed_first, packed_second, all_scr, square_scr = refs[6:]
+def score_window(count, window, known, all_ref, square_scr, margin_ref, rows_ref, packed_ref):
+    depth = all_ref.shape[1] - LANES
+    share = rows_ref.shape[0]
+    total = share * count
+    channels = LANES // 2
+    tile = 2 * LANES
+    for start in range(0, depth, tile):
+        mixed = matmul(known, all_ref[:, start : start + tile])
+        squares = mixed * mixed
+        squares = squares[:, :LANES] + squares[:, LANES:]
+        square_scr[...] = squares if start == 0 else square_scr[...] + squares
+    score = matmul(known, all_ref[:, depth:])
+    variance = jnp.sum(square_scr[...], axis=-1, keepdims=True) * (1.0 / depth)
+    score = (score + pltpu.roll(score, channels, 1)) * lax.rsqrt(variance + 1e-05)
+    position = iota((share, LANES), 0) + lax.axis_index("seq") * share
+    left = iota((share // 2, LANES), 1) < channels
+    own = total - margin_at(margin_ref, 2 * lax.axis_index("group") + window)
+    signed = score[:share] - jnp.where(position >= own, score[share:], 0.0)
+    rows_ref[...] = signed
+    packed_ref[...] = jnp.where(left, signed[: share // 2], signed[share // 2 :]).astype(BF16)
+
+
+def finish_second_kernel(count, shares, high, margin_ref, known_ref, direct_ref, back_ref, far_ref, near_ref, *refs):
+    rows_ref, packed_ref, all_ref, square_scr = refs
     width = back_ref.shape[0]
-    depth = back_ref.shape[1] - LANES
-    share = first_ref.shape[0] // 2
-    full = width * count
-    total = share * count
     part = width // shares
-    channels = direct_ref.shape[0] // 2
-    group_pos = lax.axis_index("group")
-    seq_pos = lax.axis_index("seq")
-    sub = lax.rem(group_pos, shares)
-    all_scr[:width, :] = back_ref[...]
-    all_scr[full:, :] = direct_ref[...]
+    sub = lax.rem(lax.axis_index("group"), shares)
+    all_ref[:width, :] = back_ref[...]
+    all_ref[width * count :, :] = direct_ref[...]
     for i, m in enumerate(high):
         for near, ref in ((0, far_ref), (1, near_ref)):
             place = jnp.bitwise_xor(sub, m ^ near) * part
             for k in range(1, count):
-                all_scr[pl.ds(pl.multiple_of(place + k * width, part), part), :] = ref[i, k - 1]
-    tile = 2 * LANES
-    known = jnp.concatenate([first_ref[...], second_ref[...]], axis=0)
-    for start in range(0, depth, tile):
-        mixed = matmul(known, all_scr[:, start : start + tile])
-        squares = mixed * mixed
-        squares = squares[:, :LANES] + squares[:, LANES:]
-        square_scr[...] = squares if start == 0 else square_scr[...] + squares
-    score = matmul(known, all_scr[:, depth:])
-    variance = jnp.sum(square_scr[...], axis=-1, keepdims=True) * (1.0 / depth)
-    score = (score + pltpu.roll(score, channels, 1)) * lax.rsqrt(variance + 1e-05)
-    position = iota((share, LANES), 0) + seq_pos * share
-    left = iota((share // 2, LANES), 1) < channels
-    for window, packed_ref in enumerate((packed_first, packed_second)):
-        at = 2 * share * window
-        own = total - margin_at(margin_ref, 2 * group_pos + window)
-        margin = jnp.where(position >= own, score[at + share : at + 2 * share], 0.0)
-        signed = score[at : at + share] - margin
-        rows_ref[window] = signed
-        packed_ref[...] = jnp.where(left, signed[: share // 2], signed[share // 2 :]).astype(BF16)
-
-
-def combine_kernel(count, deltas, margin_ref, latent_ref, rows_ref, *refs):
+                all_ref[pl.ds(pl.multiple_of(place + k * width, part), part), :] = ref[i, k - 1]
+    score_window(count, 1, known_ref[...], all_ref, square_scr, margin_ref, rows_ref, packed_ref)
+
+
+def finish_first_kernel(count, margin_ref, known_ref, all_ref, rows_ref, packed_ref, square_scr):
+    score_window(count, 0, known_ref[...], all_ref, square_scr, margin_ref, rows_ref, packed_ref)
+
+
+def combine_kernel(count, deltas, margin_ref, latent_ref, first_ref, second_ref, *refs):
     out_ref, tail_scr = refs[2 * len(deltas) :]
     channels, share = latent_ref.shape[1:]
     total = share * count
     group_pos = lax.axis_index("group")
     seq_pos = lax.axis_index("seq")
-    for slot in range(2):
+    for slot, rows_ref in enumerate((first_ref, second_ref)):
         before = margin_at(margin_ref, 2 * group_pos + slot - 1)
         own = total - margin_at(margin_ref, 2 * group_pos + slot)
         tail_scr[...] = jnp.zeros_like(tail_scr)
@@ -256,7 +271,7 @@
                 at = pl.ds(pl.multiple_of(row + half * (share // 2), share // 2), share // 2)
                 tail_scr[at, :] = value
         moved = tail_scr[pl.ds(OVMAX - before + seq_pos * share, share), :]
-        score = (rows_ref[slot] + moved).T[:channels]
+        score = (rows_ref[...] + moved).T[:channels]
         keep = iota(score.shape, 1) + seq_pos * share < own
         out_ref[slot] = jnp.where(keep, latent_ref[slot] + STEP * score, 0.0)
 
@@ -300,9 +315,18 @@
             jax.ShapeDtypeStruct((2 * channels, depth + LANES), BF16),
             jax.ShapeDtypeStruct((channels, 2 * LANES), BF16),
         ),
-        in_specs=[VMEM] * 6,
+        in_specs=[pl.BlockSpec(memory_space=pltpu.HBM)] * 6,
         compiler_params=limit(20),
         out_specs=(VMEM,) * 5,
+        scratch_shapes=[
+            pltpu.VMEM(in_weight.shape, BF16),
+            pltpu.VMEM(norm_gain.shape, F32),
+            pltpu.VMEM(qkv_weight.shape, BF16),
+            pltpu.VMEM(out_weight.shape, BF16),
+            pltpu.VMEM(final_gain.shape, F32),
+            pltpu.VMEM(head_out.shape[::-1], BF16),
+            pltpu.SemaphoreType.DMA((8,)),
+        ],
         cost_estimate=pl.CostEstimate(flops=width * depth * 1200, bytes_accessed=8 * width * depth, transcendentals=0),
         name="fold",
     )(in_weight, norm_gain, qkv_weight, out_weight, final_gain, head_out.T)
@@ -341,39 +365,48 @@
     planes = [swap(own_part, bits) for bits in high[1:]]
     far = jnp.stack([own_part] + planes)
     near = swap(far, 1)
-    rows, *tails = pl.pallas_call(
-        functools.partial(finish_kernel, count, shares, list(high)),
-        out_shape=(
-            jax.ShapeDtypeStruct((2, share, LANES), F32),
-            jax.ShapeDtypeStruct((share // 2, LANES), BF16),
-            jax.ShapeDtypeStruct((share // 2, LANES), BF16),
-        ),
-        in_specs=[SMEM] + [VMEM] * 6,
-        compiler_params=limit(24),
-        out_specs=(VMEM, VMEM, VMEM),
-        scratch_shapes=[
-            pltpu.VMEM((full + 2 * channels, depth + LANES), BF16),
-            pltpu.VMEM((4 * share, LANES), F32),
-        ],
-        cost_estimate=pl.CostEstimate(
-            flops=8 * share * full * depth, bytes_accessed=2 * full * depth, transcendentals=0
-        ),
-        name="finish",
-    )(margin_len, first, second, direct, back, far, near)
-
+    scored = (
+        jax.ShapeDtypeStruct((share, LANES), F32),
+        jax.ShapeDtypeStruct((share // 2, LANES), BF16),
+    )
+    squares = pltpu.VMEM((2 * share, LANES), F32)
+    cost = pl.CostEstimate(flops=4 * share * full * depth, bytes_accessed=2 * full * depth, transcendentals=0)
+    rows_second, tail_second, all_maps = pl.pallas_call(
+        functools.partial(finish_second_kernel, count, shares, list(high)),
+        out_shape=scored + (jax.ShapeDtypeStruct((full + 2 * channels, depth + LANES), BF16),),
+        in_specs=[SMEM] + [VMEM] * 5,
+        compiler_params=limit(20),
+        out_specs=(VMEM,) * 3,
+        scratch_shapes=[squares],
+        cost_estimate=cost,
+        name="finish_second",
+    )(margin_len, second, direct, back, far, near)
     deltas = list(range((total - OVMAX) // share, count))
-    received = []
-    for window, group_by in ((1, 1), (0, 0)):
-        received += [across(tails[window], group_by, [(i, i - d) for i in range(d, count)]) for d in deltas]
+
+    def tails(value, group_by):
+        return [across(value, group_by, [(i, i - d) for i in range(d, count)]) for d in deltas]
+
+    received = tails(tail_second, 1)
+    rows_first, tail_first = pl.pallas_call(
+        functools.partial(finish_first_kernel, count),
+        out_shape=scored,
+        in_specs=[SMEM] + [VMEM] * 2,
+        compiler_params=limit(20),
+        out_specs=(VMEM,) * 2,
+        scratch_shapes=[squares],
+        cost_estimate=cost,
+        name="finish_first",
+    )(margin_len, first, all_maps)
+    received += tails(tail_first, 0)
     turned = pl.pallas_call(
         functools.partial(combine_kernel, count, deltas),
         out_shape=jax.ShapeDtypeStruct(turned.shape, F32),
-        in_specs=[SMEM] + [VMEM] * (2 + len(received)),
+        in_specs=[SMEM] + [VMEM] * (3 + len(received)),
         compiler_params=limit(8),
         out_specs=VMEM,
         scratch_shapes=[pltpu.VMEM((OVMAX + total + share, LANES), F32)],
         name="combine",
-    )(margin_len, turned, rows, *received)
+    )(margin_len, turned, rows_first, rows_second, *received)
     return turned.transpose(0, 2, 1)
 
 

time: 95.5 us -> 99.5 us (1.042)
  starting transfers between devices: 23.8 us -> 33 us
  waiting for transfers between devices: 31.9 us -> 24.2 us
  Pallas kernels: 25.2 us -> 27.7 us
    ppermute x9, starting transfers between devices: 10.2 us -> 17.3 us  [gathered(): lax.ppermute(value, 'seq', [(i, i ^ k) for i in range(count)])]
    ppermute x9, waiting for transfers between devices: 12.7 us -> 6.9 us  [gathered(): lax.ppermute(value, 'seq', [(i, i ^ k) for i in range(count)])]
    pallas_call x1, Pallas kernels: 2.33 us -> 4.02 us  [body(): pl.pallas_call(functools.partial(fold_kernel, shares), out_shape=(jax.Sha...]
    ppermute x4, waiting for transfers between devices: 12.8 us -> 11.3 us  [swap(): return lax.ppermute(value, 'group', [(g, g ^ bits) for g in range(groups)])]
    ppermute x4, starting transfers between devices: 5.26 us -> 6.78 us  [swap(): return lax.ppermute(value, 'group', [(g, g ^ bits) for g in range(groups)])]
    pallas_call x1 -> x2, Pallas kernels: 5.8 us -> 6.58 us  [the longest x1 3.42 us: body(): pl.pallas_call(functools.partial(finish_second_kernel, count, shares, lis...]
  transfers between devices with their start and end apart: 18 -> 18, of which waited for: 11 -> 10; matrix products, arithmetic and copies ran while one was open for 6% -> 6% of each run, Pallas kernels for 17% -> 16%
where the time goes in v3:
time: 99.5 us; the launch traced here: 98.6 us
  starting transfers between devices  33 us (33%)
  Pallas kernels  27.7 us (28%)
  waiting for transfers between devices  24.2 us (24%)
  local copies, waits for them, and re-layouts  11.3 us (11%)
  other arithmetic  2.18 us (2%)
    ppermute x9, starting transfers between devices, gathered(): lax.ppermute(value, 'seq', [(i, i ^ k) for i in range(count)])  17.3 us
    pallas_call x2, Pallas kernels, attend(): pl.pallas_call(functools.partial(attend_kernel, count, window), out_shape...  15.6 us
    ppermute x4, waiting for transfers between devices, swap(): return lax.ppermute(value, 'group', [(g, g ^ bits) for g in range(groups)])  11.3 us
    unnamed x32, local copies, waits for them, and re-layouts  10.6 us
    ppermute x5, starting transfers between devices, across(): return lax.ppermute(value, ('group', 'seq'), moves)  8.96 us
    ppermute x9, waiting for transfers between devices, gathered(): lax.ppermute(value, 'seq', [(i, i ^ k) for i in range(count)])  6.9 us
    ppermute x4, starting transfers between devices, swap(): return lax.ppermute(value, 'group', [(g, g ^ bits) for g in range(groups)])  6.78 us
    ppermute x5, waiting for transfers between devices, across(): return lax.ppermute(value, ('group', 'seq'), moves)  6.01 us
  transfers between devices with their start and end apart: 18, of which 10 were waited for; matrix products, arithmetic and copies ran while one was open for 6% of the time, Pallas kernels for 16%

profile of v3, /device:TPU:1, one launch (start us, length us, event | category | flops | bytes accessed | tf_op | source)
XLA Modules:
  0.0 98.6 jit_solution(3699959704082311079)
XLA Ops:
  0.0 1.7 %copy-done = bf16[3,1536,256]{2,1,0:T(8,128)(2,1)S(1)} copy-done((bf16[3,1536,256]{2,1,0:T(8,128)(2,1)S(1)}, bf16[3,1536,256]{2,1,0:T(8,128)(2,1)}, u32[]{:S(2)}) %copy-start) | copy-done | bytes 2359320
  1.7 1.1 %copy-done.1 = bf16[256,1536]{1,0:T(8,128)(2,1)S(1)} copy-done((bf16[256,1536]{1,0:T(8,128)(2,1)S(1)}, bf16[256,1536]{1,0:T(8,128)(2,1)}, u32[]{:S(2)}) %copy-start.1) | copy-done | bytes 786456
  2.8 0.9 copy-done.3
  3.7 0.9 copy-done.4
  4.7 0.7 copy-done.5
  5.4 0.7 copy-done.6
  6.0 4.0 %fold.1 = (bf16[256,128]{1,0:T(8,128)(2,1)S(1)}, bf16[256,1664]{1,0:T(8,128)(2,1)S(1)}, bf16[32,1664]{1,0:T(8,128)(2,1)S(1)}, bf16[128,1664]{1,0:T(8,128)(2,1)S(1)}, bf16[64,256]{1,0:T(8,128)(2,1)S(1)}) custom-call(bf16[64,1536]{1,0:T(8,128)(2,1)S(1)} %copy-done.3, f32[1536]{0:T(1024)S(1)} %copy-done.5, bf16[3,1536,256]{2,1,0:T(8,128)(2,1)S(1)} %copy-done, ...), custom_call_target="tpu_custom_call" | custom-call | flops 471859200 | bytes 3145728 | tf_op jit(solution)/shard_map/fold/pallas_call | solution.py:309
  10.1 2.2 %collective-permute-start.7 = (bf16[32,1664]{1,0:T(8,128)(2,1)S(1)}, bf16[32,1664]{1,0:T(8,128)(2,1)S(1)}, u32[]{:S(2)}, u32[]{:S(2)}) collective-permute-start(bf16[32,1664]{1,0:T(8,128)(2,1)S(1)} %get-tuple-element.19), channel_id=1, source_target_pairs={{0,1},{1,0},{2,3},{3,2},{4,5},{5,4},{6,7},{7,6},{8,9},{9,8},{10,11... | collective-permute-start | bytes 319496 | tf_op jit(solution)/shard_map/ppermute | solution.py:302
  12.3 2.3 %collective-permute-start.8 = (bf16[32,1664]{1,0:T(8,128)(2,1)S(1)}, bf16[32,1664]{1,0:T(8,128)(2,1)S(1)}, u32[]{:S(2)}, u32[]{:S(2)}) collective-permute-start(bf16[32,1664]{1,0:T(8,128)(2,1)S(1)} %get-tuple-element.19), channel_id=1, source_target_pairs={{0,2},{1,3},{2,0},{3,1},{4,6},{5,7},{6,4},{7,5},{8,10},{9,11},{10,... | collective-permute-start | bytes 319496 | tf_op jit(solution)/shard_map/ppermute | solution.py:302
  14.6 0.4 collective-permute-done.7
  15.0 1.9 %collective-permute-done.8 = bf16[32,1664]{1,0:T(8,128)(2,1)S(1)} collective-permute-done((bf16[32,1664]{1,0:T(8,128)(2,1)S(1)}, bf16[32,1664]{1,0:T(8,128)(2,1)S(1)}, u32[]{:S(2)}, u32[]{:S(2)}) %collective-permute-start.8) | collective-permute-done | bytes 106528 | tf_op jit(solution)/shard_map/ppermute | solution.py:302
  16.9 4.6 %collective-permute-done.9 = bf16[32,1664]{1,0:T(8,128)(2,1)S(1)} collective-permute-done((bf16[32,1664]{1,0:T(8,128)(2,1)S(1)}, bf16[32,1664]{1,0:T(8,128)(2,1)S(1)}, u32[]{:S(2)}, u32[]{:S(2)}) %collective-permute-start.9) | collective-permute-done | bytes 106528 | tf_op jit(solution)/shard_map/ppermute | solution.py:302
  21.5 0.1 fusion
  21.5 1.2 %collective-permute-start.10 = (bf16[3,32,1664]{2,1,0:T(8,128)(2,1)S(1)}, bf16[3,32,1664]{2,1,0:T(8,128)(2,1)S(1)}, u32[]{:S(2)}, u32[]{:S(2)}) collective-permute-start(bf16[3,32,1664]{2,1,0:T(8,128)(2,1)S(1)} %get-tuple-element.26), channel_id=1, source_target_pairs={{0,8},{4,12},{8,0},{12,4},{16,24},{20,28},{24,16},{28,20},{1,9},{5... | collective-permute-start | bytes 958472 | tf_op jit(solution)/shard_map/ppermute | solution.py:299
  22.8 0.9 collective-permute-start.11
  23.7 0.5 collective-permute-start.12
  24.3 3.6 %collective-permute-done.10 = bf16[3,32,1664]{2,1,0:T(8,128)(2,1)S(1)} collective-permute-done((bf16[3,32,1664]{2,1,0:T(8,128)(2,1)S(1)}, bf16[3,32,1664]{2,1,0:T(8,128)(2,1)S(1)}, u32[]{:S(2)}, u32[]{:S(2)}) %collective-permute-start.10) | collective-permute-done | bytes 319520 | tf_op jit(solution)/shard_map/ppermute | solution.py:299
  27.9 1.2 %collective-permute-done.11 = bf16[3,32,1664]{2,1,0:T(8,128)(2,1)S(1)} collective-permute-done((bf16[3,32,1664]{2,1,0:T(8,128)(2,1)S(1)}, bf16[3,32,1664]{2,1,0:T(8,128)(2,1)S(1)}, u32[]{:S(2)}, u32[]{:S(2)}) %collective-permute-start.11) | collective-permute-done | bytes 319520 | tf_op jit(solution)/shard_map/ppermute | solution.py:299
  29.1 6.5 %collective-permute-done.12 = bf16[3,32,1664]{2,1,0:T(8,128)(2,1)S(1)} collective-permute-done((bf16[3,32,1664]{2,1,0:T(8,128)(2,1)S(1)}, bf16[3,32,1664]{2,1,0:T(8,128)(2,1)S(1)}, u32[]{:S(2)}, u32[]{:S(2)}) %collective-permute-start.12) | collective-permute-done | bytes 319520 | tf_op jit(solution)/shard_map/ppermute | solution.py:299
  35.6 0.2 pad_maximum_fusion.far_ref
  35.8 4.1 %collective-permute-start.13 = (bf16[4,3,32,1664]{3,2,1,0:T(8,128)(2,1)S(1)}, bf16[4,3,32,1664]{3,2,1,0:T(8,128)(2,1)S(1)}, u32[]{:S(2)}, u32[]{:S(2)}) collective-permute-start(bf16[4,3,32,1664]{3,2,1,0:T(8,128)(2,1)S(1)} %pad_maximum_fusion.far_ref), channel_id=1, source_target_pairs={{0,4},{4,0},{8,12},{12,8},{16,20},{20,16},{24,28},{28,24},{1,5},{5... | collective-permute-start | bytes 3833864 | tf_op jit(solution)/shard_map/ppermute | solution.py:299
  39.9 0.6 fusion.1
  40.5 1.5 %copy.11 = bf16[1,256,64]{2,1,0:T(8,128)(2,1)} copy(bf16[1,256,64]{1,2,0:T(8,128)(2,1)} %get-tuple-element.27) | data formatting | bytes 65536
  42.0 1.5 %copy.12 = bf16[1,256,64]{2,1,0:T(8,128)(2,1)} copy(bf16[1,256,64]{1,2,0:T(8,128)(2,1)} %get-tuple-element.28) | data formatting | bytes 65536
  43.5 1.0 pad_maximum_fusion.3.refs_0_
  44.4 2.5 %collective-permute-start = (bf16[256,128]{1,0:T(8,128)(2,1)S(1)}, bf16[256,128]{1,0:T(8,128)(2,1)S(1)}, u32[]{:S(2)}, u32[]{:S(2)}) collective-permute-start(bf16[256,128]{1,0:T(8,128)(2,1)S(1)} %pad_maximum_fusion.3.refs_0_), channel_id=1, source_target_pairs={{0,1},{1,0},{2,3},{3,2},{4,5},{5,4},{6,7},{7,6},{8,9},{9,8},{10,11... | collective-permute-start | bytes 196616 | tf_op jit(solution)/shard_map/ppermute | solution.py:302
  46.9 1.5 %collective-permute-start.1 = (bf16[256,128]{1,0:T(8,128)(2,1)S(1)}, bf16[256,128]{1,0:T(8,128)(2,1)S(1)}, u32[]{:S(2)}, u32[]{:S(2)}) collective-permute-start(bf16[256,128]{1,0:T(8,128)(2,1)S(1)} %pad_maximum_fusion.3.refs_0_), channel_id=1, source_target_pairs={{0,2},{1,3},{2,0},{3,1},{4,6},{5,7},{6,4},{7,5},{8,10},{9,11},{10,... | collective-permute-start | bytes 196616 | tf_op jit(solution)/shard_map/ppermute | solution.py:302
  48.4 1.1 %collective-permute-start.2 = (bf16[256,128]{1,0:T(8,128)(2,1)S(1)}, bf16[256,128]{1,0:T(8,128)(2,1)S(1)}, u32[]{:S(2)}, u32[]{:S(2)}) collective-permute-start(bf16[256,128]{1,0:T(8,128)(2,1)S(1)} %pad_maximum_fusion.3.refs_0_), channel_id=1, source_target_pairs={{0,3},{1,2},{2,1},{3,0},{4,7},{5,6},{6,5},{7,4},{8,11},{9,10},{10,... | collective-permute-start | bytes 196616 | tf_op jit(solution)/shard_map/ppermute | solution.py:302
  49.5 0.3 collective-permute-start.3
  49.8 2.2 %collective-permute-start.4 = (bf16[256,128]{1,0:T(8,128)(2,1)}, bf16[256,128]{1,0:T(8,128)(2,1)S(1)}, u32[]{:S(2)}, u32[]{:S(2)}) collective-permute-start(bf16[256,128]{1,0:T(8,128)(2,1)} %copy-done.10), channel_id=1, source_target_pairs={{0,2},{1,3},{2,0},{3,1},{4,6},{5,7},{6,4},{7,5},{8,10},{9,11},{10,... | collective-permute-start | bytes 196616 | tf_op jit(solution)/shard_map/ppermute | solution.py:302
  52.0 5.2 %collective-permute-start.5 = (bf16[256,128]{1,0:T(8,128)(2,1)}, bf16[256,128]{1,0:T(8,128)(2,1)S(1)}, u32[]{:S(2)}, u32[]{:S(2)}) collective-permute-start(bf16[256,128]{1,0:T(8,128)(2,1)} %copy-done.10), channel_id=1, source_target_pairs={{0,3},{1,2},{2,1},{3,0},{4,7},{5,6},{6,5},{7,4},{8,11},{9,10},{10,... | collective-permute-start | bytes 196616 | tf_op jit(solution)/shard_map/ppermute | solution.py:302
  57.2 1.0 pad_maximum_fusion.2
  58.2 3.8 %collective-permute-start.6 = (bf16[4,256,128]{2,1,0:T(8,128)(2,1)S(1)}, bf16[4,256,128]{2,1,0:T(8,128)(2,1)S(1)}, u32[]{:S(2)}, u32[]{:S(2)}) collective-permute-start(bf16[4,256,128]{2,1,0:T(8,128)(2,1)S(1)} %pad_maximum_fusion.2), channel_id=1, source_target_pairs={{4,0},{5,1},{6,2},{7,3},{8,4},{9,5},{10,6},{11,7},{12,8},{13,9},{1... | collective-permute-start | bytes 786440 | tf_op jit(solution)/shard_map/ppermute | solution.py:296
  62.1 0.8 copy-done.11
  62.9 0.8 copy-done.14
  63.7 7.7 %attend.2.known_ref = bf16[512,1152]{1,0:T(8,128)(2,1)S(1)} custom-call(s32[15]{0:T(128)S(1)} %copy-done.7, bf16[256,128]{1,0:T(8,128)(2,1)S(1)} %pad_maximum_fusion.3.refs_0_, bf16[256,128]{1,0:T(8,128)(2,1)S(1)} %collective-permute-done.refs_1_, bf16[256,128]{1,0:T(8,128)(2,1)S(1)} %collective-permute-done.1.refs_2_, ...), custom_call_target="tpu_custom_call" | custom-call | flops 4294967296 | bytes 1048576 | tf_op jit(solution)/shard_map/attend/pallas_call | solution.py:339
  71.4 8.0 %attend.3.known_ref = bf16[512,1152]{1,0:T(8,128)(2,1)S(1)} custom-call(s32[15]{0:T(128)S(1)} %copy-done.7, bf16[256,128]{1,0:T(8,128)(2,1)S(1)} %pad_maximum_fusion.3.refs_0_, bf16[256,128]{1,0:T(8,128)(2,1)S(1)} %collective-permute-done.refs_1_, bf16[256,128]{1,0:T(8,128)(2,1)S(1)} %collective-permute-done.1.refs_2_, ...), custom_call_target="tpu_custom_call" | custom-call | flops 4294967296 | bytes 1048576 | tf_op jit(solution)/shard_map/attend/pallas_call | solution.py:339
  79.4 3.4 %finish_second.1 = (f32[256,128]{1,0:T(8,128)S(1)}, bf16[128,128]{1,0:T(8,128)(2,1)S(1)}, bf16[1152,1664]{1,0:T(8,128)(2,1)S(1)}) custom-call(s32[15]{0:T(128)S(1)} %copy-done.7, bf16[512,1152]{1,0:T(8,128)(2,1)S(1)} %attend.3.known_ref, bf16[128,1664]{1,0:T(8,128)(2,1)S(1)} %copy-done.9, bf16[256,1664]{1,0:T(8,128)(2,1)S(1)} %get-tuple-element.18.back_ref, ...), custom_call_target="tpu_custom_call" | custom-call | flops 1610612736 | bytes 3145728 | tf_op jit(solution)/shard_map/finish_second/pallas_call | solution.py:374
  82.8 3.2 %finish_first.1 = (f32[256,128]{1,0:T(8,128)S(1)}, bf16[128,128]{1,0:T(8,128)(2,1)S(1)}) custom-call(s32[15]{0:T(128)S(1)} %copy-done.7, bf16[512,1152]{1,0:T(8,128)(2,1)S(1)} %attend.2.known_ref, bf16[1152,1664]{1,0:T(8,128)(2,1)S(1)} %get-tuple-element.20.all_ref), custom_call_target="tpu_custom_call" | custom-call | flops 1610612736 | bytes 3145728 | tf_op jit(solution)/shard_map/finish_first/pallas_call | solution.py:390
  86.0 1.3 %collective-permute-start.16 = (bf16[128,128]{1,0:T(8,128)(2,1)S(1)}, bf16[128,128]{1,0:T(8,128)(2,1)S(1)}, u32[]{:S(2)}, u32[]{:S(2)}) collective-permute-start(bf16[128,128]{1,0:T(8,128)(2,1)S(1)} %get-tuple-element.24), channel_id=1, source_target_pairs={{2,0},{3,1},{6,4},{7,5},{10,8},{11,9},{14,12},{15,13},{18,16},{19,... | collective-permute-start | bytes 98312 | tf_op jit(solution)/shard_map/ppermute | solution.py:296
  87.3 1.3 %collective-permute-start.17 = (bf16[128,128]{1,0:T(8,128)(2,1)S(1)}, bf16[128,128]{1,0:T(8,128)(2,1)S(1)}, u32[]{:S(2)}, u32[]{:S(2)}) collective-permute-start(bf16[128,128]{1,0:T(8,128)(2,1)S(1)} %get-tuple-element.24), channel_id=1, source_target_pairs={{3,0},{7,4},{11,8},{15,12},{19,16},{23,20},{27,24},{31,28}} | collective-permute-start | bytes 98312 | tf_op jit(solution)/shard_map/ppermute | solution.py:296
  88.6 1.3 %collective-permute-start.14 = (bf16[128,128]{1,0:T(8,128)(2,1)S(1)}, bf16[128,128]{1,0:T(8,128)(2,1)S(1)}, u32[]{:S(2)}, u32[]{:S(2)}) collective-permute-start(bf16[128,128]{1,0:T(8,128)(2,1)S(1)} %get-tuple-element.23), channel_id=1, source_target_pairs={{2,4},{3,5},{6,8},{7,9},{10,12},{11,13},{14,16},{15,17},{18,20},{1... | collective-permute-start | bytes 98312 | tf_op jit(solution)/shard_map/ppermute | solution.py:296
  89.9 1.3 %collective-permute-start.15 = (bf16[128,128]{1,0:T(8,128)(2,1)S(1)}, bf16[128,128]{1,0:T(8,128)(2,1)S(1)}, u32[]{:S(2)}, u32[]{:S(2)}) collective-permute-start(bf16[128,128]{1,0:T(8,128)(2,1)S(1)} %get-tuple-element.23), channel_id=1, source_target_pairs={{3,4},{7,8},{11,12},{15,16},{19,20},{23,24},{27,28}} | collective-permute-start | bytes 98312 | tf_op jit(solution)/shard_map/ppermute | solution.py:296
  91.2 0.5 collective-permute-done.16.refs_2_
  91.6 2.1 %collective-permute-done.17.refs_3_ = bf16[128,128]{1,0:T(8,128)(2,1)S(1)} collective-permute-done((bf16[128,128]{1,0:T(8,128)(2,1)S(1)}, bf16[128,128]{1,0:T(8,128)(2,1)S(1)}, u32[]{:S(2)}, u32[]{:S(2)}) %collective-permute-start.17) | collective-permute-done | bytes 32800 | tf_op jit(solution)/shard_map/ppermute | solution.py:296
  93.7 2.0 %collective-permute-done.14.refs_0_ = bf16[128,128]{1,0:T(8,128)(2,1)S(1)} collective-permute-done((bf16[128,128]{1,0:T(8,128)(2,1)S(1)}, bf16[128,128]{1,0:T(8,128)(2,1)S(1)}, u32[]{:S(2)}, u32[]{:S(2)}) %collective-permute-start.14) | collective-permute-done | bytes 32800 | tf_op jit(solution)/shard_map/ppermute | solution.py:296
  95.7 1.5 %collective-permute-done.15.refs_1_ = bf16[128,128]{1,0:T(8,128)(2,1)S(1)} collective-permute-done((bf16[128,128]{1,0:T(8,128)(2,1)S(1)}, bf16[128,128]{1,0:T(8,128)(2,1)S(1)}, u32[]{:S(2)}, u32[]{:S(2)}) %collective-permute-start.15) | collective-permute-done | bytes 32800 | tf_op jit(solution)/shard_map/ppermute | solution.py:296
  97.2 1.5 %combine.1 = f32[2,64,256]{2,1,0:T(8,128)} custom-call(s32[15]{0:T(128)S(1)} %copy-done.7, f32[2,64,256]{2,1,0:T(8,128)S(1)} %bitcast.16, f32[256,128]{1,0:T(8,128)S(1)} %get-tuple-element.21.first_ref, f32[256,128]{1,0:T(8,128)S(1)} %get-tuple-element.22.second_ref, bf16[128,128]{1,0:T(8,128)(2,1)S(1)} %collective-permute-done.14.refs_0_, ...), custom_call_target="tpu_custom_call" | custom-call | tf_op jit(solution)/shard_map/combine/pallas_call | solution.py:401
  (31 shorter events, 0.1 us)
Async XLA Ops:
  0.0 1.7 %copy-start = (bf16[3,1536,256]{2,1,0:T(8,128)(2,1)S(1)}, bf16[3,1536,256]{2,1,0:T(8,128)(2,1)}, u32[]{:S(2)}) copy-start(bf16[3,1536,256]{2,1,0:T(8,128)(2,1)} %qkv_hbm.1) | copy-start | bytes 7077892
  1.7 1.1 %copy-start.1 = (bf16[256,1536]{1,0:T(8,128)(2,1)S(1)}, bf16[256,1536]{1,0:T(8,128)(2,1)}, u32[]{:S(2)}) copy-start(bf16[256,1536]{1,0:T(8,128)(2,1)} %out_hbm.1) | copy-start | bytes 2359300
  2.8 0.9 copy-start.3
  3.7 0.9 copy-start.4
  4.7 0.7 copy-start.5
  5.4 0.7 copy-start.6
  10.1 25.7 %copy-start.8 = (bf16[128,1664]{1,0:T(8,128)(2,1)}, bf16[128,1664]{1,0:T(8,128)(2,1)S(1)}, u32[]{:S(2)}) copy-start(bf16[128,1664]{1,0:T(8,128)(2,1)S(1)} %get-tuple-element.17.direct_ref) | copy-start | bytes 1277956
  10.1 25.7 %copy-start.10 = (bf16[256,128]{1,0:T(8,128)(2,1)}, bf16[256,128]{1,0:T(8,128)(2,1)S(1)}, u32[]{:S(2)}) copy-start(bf16[256,128]{1,0:T(8,128)(2,1)S(1)} %get-tuple-element.15.refs_4_) | copy-start | bytes 196612
  10.1 25.7 %copy-start.13 = (bf16[64,256]{1,0:T(8,128)(2,1)}, bf16[64,256]{1,0:T(8,128)(2,1)S(1)}, u32[]{:S(2)}) copy-start(bf16[64,256]{1,0:T(8,128)(2,1)S(1)} %get-tuple-element.16.refs_8_) | copy-start | bytes 98308
  10.1 4.9 %collective-permute-start.7 = (bf16[32,1664]{1,0:T(8,128)(2,1)S(1)}, bf16[32,1664]{1,0:T(8,128)(2,1)S(1)}, u32[]{:S(2)}, u32[]{:S(2)}) collective-permute-start(bf16[32,1664]{1,0:T(8,128)(2,1)S(1)} %get-tuple-element.19), channel_id=1, source_target_pairs={{0,1},{1,0},{2,3},{3,2},{4,5},{5,4},{6,7},{7,6},{8,9},{9,8},{10,11... | collective-permute-start | bytes 319496 | tf_op jit(solution)/shard_map/ppermute | solution.py:302
  12.3 4.6 %collective-permute-start.8 = (bf16[32,1664]{1,0:T(8,128)(2,1)S(1)}, bf16[32,1664]{1,0:T(8,128)(2,1)S(1)}, u32[]{:S(2)}, u32[]{:S(2)}) collective-permute-start(bf16[32,1664]{1,0:T(8,128)(2,1)S(1)} %get-tuple-element.19), channel_id=1, source_target_pairs={{0,2},{1,3},{2,0},{3,1},{4,6},{5,7},{6,4},{7,5},{8,10},{9,11},{10,... | collective-permute-start | bytes 319496 | tf_op jit(solution)/shard_map/ppermute | solution.py:302
  14.6 6.9 %collective-permute-start.9 = (bf16[32,1664]{1,0:T(8,128)(2,1)S(1)}, bf16[32,1664]{1,0:T(8,128)(2,1)S(1)}, u32[]{:S(2)}, u32[]{:S(2)}) collective-permute-start(bf16[32,1664]{1,0:T(8,128)(2,1)S(1)} %get-tuple-element.19), channel_id=1, source_target_pairs={{0,3},{1,2},{2,1},{3,0},{4,7},{5,6},{6,5},{7,4},{8,11},{9,10},{10,... | collective-permute-start | bytes 319496 | tf_op jit(solution)/shard_map/ppermute | solution.py:302
  21.5 6.4 %collective-permute-start.10 = (bf16[3,32,1664]{2,1,0:T(8,128)(2,1)S(1)}, bf16[3,32,1664]{2,1,0:T(8,128)(2,1)S(1)}, u32[]{:S(2)}, u32[]{:S(2)}) collective-permute-start(bf16[3,32,1664]{2,1,0:T(8,128)(2,1)S(1)} %get-tuple-element.26), channel_id=1, source_target_pairs={{0,8},{4,12},{8,0},{12,4},{16,24},{20,28},{24,16},{28,20},{1,9},{5... | collective-permute-start | bytes 958472 | tf_op jit(solution)/shard_map/ppermute | solution.py:299
  22.8 6.3 %collective-permute-start.11 = (bf16[3,32,1664]{2,1,0:T(8,128)(2,1)S(1)}, bf16[3,32,1664]{2,1,0:T(8,128)(2,1)S(1)}, u32[]{:S(2)}, u32[]{:S(2)}) collective-permute-start(bf16[3,32,1664]{2,1,0:T(8,128)(2,1)S(1)} %get-tuple-element.26), channel_id=1, source_target_pairs={{0,16},{4,20},{8,24},{12,28},{16,0},{20,4},{24,8},{28,12},{1,17},{... | collective-permute-start | bytes 958472 | tf_op jit(solution)/shard_map/ppermute | solution.py:299
  23.7 11.9 %collective-permute-start.12 = (bf16[3,32,1664]{2,1,0:T(8,128)(2,1)S(1)}, bf16[3,32,1664]{2,1,0:T(8,128)(2,1)S(1)}, u32[]{:S(2)}, u32[]{:S(2)}) collective-permute-start(bf16[3,32,1664]{2,1,0:T(8,128)(2,1)S(1)} %get-tuple-element.26), channel_id=1, source_target_pairs={{0,24},{4,28},{8,16},{12,20},{16,8},{20,12},{24,0},{28,4},{1,25},{... | collective-permute-start | bytes 958472 | tf_op jit(solution)/shard_map/ppermute | solution.py:299
  35.6 4.3 %copy-start.2 = (f32[2,256,64]{1,2,0:T(8,128)S(1)}, f32[2,256,64]{1,2,0:T(8,128)}, u32[]{:S(2)}) copy-start(f32[2,256,64]{1,2,0:T(8,128)} %param.8) | copy-start | bytes 393220
  35.6 26.5 %copy-start.7 = (s32[15]{0:T(128)S(1)}, s32[15]{0:T(128)}, u32[]{:S(2)}) copy-start(s32[15]{0:T(128)} %margin_ref.9) | copy-start | bytes 184
  35.8 43.5 %collective-permute-start.13 = (bf16[4,3,32,1664]{3,2,1,0:T(8,128)(2,1)S(1)}, bf16[4,3,32,1664]{3,2,1,0:T(8,128)(2,1)S(1)}, u32[]{:S(2)}, u32[]{:S(2)}) collective-permute-start(bf16[4,3,32,1664]{3,2,1,0:T(8,128)(2,1)S(1)} %pad_maximum_fusion.far_ref), channel_id=1, source_target_pairs={{0,4},{4,0},{8,12},{12,8},{16,20},{20,16},{24,28},{28,24},{1,5},{5... | collective-permute-start | bytes 3833864 | tf_op jit(solution)/shard_map/ppermute | solution.py:299
  44.4 5.4 %collective-permute-start = (bf16[256,128]{1,0:T(8,128)(2,1)S(1)}, bf16[256,128]{1,0:T(8,128)(2,1)S(1)}, u32[]{:S(2)}, u32[]{:S(2)}) collective-permute-start(bf16[256,128]{1,0:T(8,128)(2,1)S(1)} %pad_maximum_fusion.3.refs_0_), channel_id=1, source_target_pairs={{0,1},{1,0},{2,3},{3,2},{4,5},{5,4},{6,7},{7,6},{8,9},{9,8},{10,11... | collective-permute-start | bytes 196616 | tf_op jit(solution)/shard_map/ppermute | solution.py:302
  46.9 5.1 %collective-permute-start.1 = (bf16[256,128]{1,0:T(8,128)(2,1)S(1)}, bf16[256,128]{1,0:T(8,128)(2,1)S(1)}, u32[]{:S(2)}, u32[]{:S(2)}) collective-permute-start(bf16[256,128]{1,0:T(8,128)(2,1)S(1)} %pad_maximum_fusion.3.refs_0_), channel_id=1, source_target_pairs={{0,2},{1,3},{2,0},{3,1},{4,6},{5,7},{6,4},{7,5},{8,10},{9,11},{10,... | collective-permute-start | bytes 196616 | tf_op jit(solution)/shard_map/ppermute | solution.py:302
  48.4 8.8 %collective-permute-start.2 = (bf16[256,128]{1,0:T(8,128)(2,1)S(1)}, bf16[256,128]{1,0:T(8,128)(2,1)S(1)}, u32[]{:S(2)}, u32[]{:S(2)}) collective-permute-start(bf16[256,128]{1,0:T(8,128)(2,1)S(1)} %pad_maximum_fusion.3.refs_0_), channel_id=1, source_target_pairs={{0,3},{1,2},{2,1},{3,0},{4,7},{5,6},{6,5},{7,4},{8,11},{9,10},{10,... | collective-permute-start | bytes 196616 | tf_op jit(solution)/shard_map/ppermute | solution.py:302
  49.5 12.5 %collective-permute-start.3 = (bf16[256,128]{1,0:T(8,128)(2,1)}, bf16[256,128]{1,0:T(8,128)(2,1)S(1)}, u32[]{:S(2)}, u32[]{:S(2)}) collective-permute-start(bf16[256,128]{1,0:T(8,128)(2,1)} %copy-done.10), channel_id=1, source_target_pairs={{0,1},{1,0},{2,3},{3,2},{4,5},{5,4},{6,7},{7,6},{8,9},{9,8},{10,11... | collective-permute-start | bytes 196616 | tf_op jit(solution)/shard_map/ppermute | solution.py:302
  49.8 12.2 %collective-permute-start.4 = (bf16[256,128]{1,0:T(8,128)(2,1)}, bf16[256,128]{1,0:T(8,128)(2,1)S(1)}, u32[]{:S(2)}, u32[]{:S(2)}) collective-permute-start(bf16[256,128]{1,0:T(8,128)(2,1)} %copy-done.10), channel_id=1, source_target_pairs={{0,2},{1,3},{2,0},{3,1},{4,6},{5,7},{6,4},{7,5},{8,10},{9,11},{10,... | collective-permute-start | bytes 196616 | tf_op jit(solution)/shard_map/ppermute | solution.py:302
  52.0 10.0 %collective-permute-start.5 = (bf16[256,128]{1,0:T(8,128)(2,1)}, bf16[256,128]{1,0:T(8,128)(2,1)S(1)}, u32[]{:S(2)}, u32[]{:S(2)}) collective-permute-start(bf16[256,128]{1,0:T(8,128)(2,1)} %copy-done.10), channel_id=1, source_target_pairs={{0,3},{1,2},{2,1},{3,0},{4,7},{5,6},{6,5},{7,4},{8,11},{9,10},{10,... | collective-permute-start | bytes 196616 | tf_op jit(solution)/shard_map/ppermute | solution.py:302
  58.2 13.2 %collective-permute-start.6 = (bf16[4,256,128]{2,1,0:T(8,128)(2,1)S(1)}, bf16[4,256,128]{2,1,0:T(8,128)(2,1)S(1)}, u32[]{:S(2)}, u32[]{:S(2)}) collective-permute-start(bf16[4,256,128]{2,1,0:T(8,128)(2,1)S(1)} %pad_maximum_fusion.2), channel_id=1, source_target_pairs={{4,0},{5,1},{6,2},{7,3},{8,4},{9,5},{10,6},{11,7},{12,8},{13,9},{1... | collective-permute-start | bytes 786440 | tf_op jit(solution)/shard_map/ppermute | solution.py:296
  62.0 0.8 copy-start.11
  62.9 0.8 copy-start.14
  63.6 7.7 %copy-start.12 = (bf16[256,128]{1,0:T(8,128)(2,1)S(1)}, bf16[256,128]{1,0:T(8,128)(2,1)}, u32[]{:S(2)}) copy-start(bf16[256,128]{1,0:T(8,128)(2,1)} %copy-done.10) | copy-start | bytes 196612
  71.4 8.0 %copy-start.9 = (bf16[128,1664]{1,0:T(8,128)(2,1)S(1)}, bf16[128,1664]{1,0:T(8,128)(2,1)}, u32[]{:S(2)}) copy-start(bf16[128,1664]{1,0:T(8,128)(2,1)} %copy-done.8) | copy-start | bytes 1277956
  86.0 5.7 %collective-permute-start.16 = (bf16[128,128]{1,0:T(8,128)(2,1)S(1)}, bf16[128,128]{1,0:T(8,128)(2,1)S(1)}, u32[]{:S(2)}, u32[]{:S(2)}) collective-permute-start(bf16[128,128]{1,0:T(8,128)(2,1)S(1)} %get-tuple-element.24), channel_id=1, source_target_pairs={{2,0},{3,1},{6,4},{7,5},{10,8},{11,9},{14,12},{15,13},{18,16},{19,... | collective-permute-start | bytes 98312 | tf_op jit(solution)/shard_map/ppermute | solution.py:296
  87.3 6.5 %collective-permute-start.17 = (bf16[128,128]{1,0:T(8,128)(2,1)S(1)}, bf16[128,128]{1,0:T(8,128)(2,1)S(1)}, u32[]{:S(2)}, u32[]{:S(2)}) collective-permute-start(bf16[128,128]{1,0:T(8,128)(2,1)S(1)} %get-tuple-element.24), channel_id=1, source_target_pairs={{3,0},{7,4},{11,8},{15,12},{19,16},{23,20},{27,24},{31,28}} | collective-permute-start | bytes 98312 | tf_op jit(solution)/shard_map/ppermute | solution.py:296
  88.6 7.1 %collective-permute-start.14 = (bf16[128,128]{1,0:T(8,128)(2,1)S(1)}, bf16[128,128]{1,0:T(8,128)(2,1)S(1)}, u32[]{:S(2)}, u32[]{:S(2)}) collective-permute-start(bf16[128,128]{1,0:T(8,128)(2,1)S(1)} %get-tuple-element.23), channel_id=1, source_target_pairs={{2,4},{3,5},{6,8},{7,9},{10,12},{11,13},{14,16},{15,17},{18,20},{1... | collective-permute-start | bytes 98312 | tf_op jit(solution)/shard_map/ppermute | solution.py:296
  89.9 7.3 %collective-permute-start.15 = (bf16[128,128]{1,0:T(8,128)(2,1)S(1)}, bf16[128,128]{1,0:T(8,128)(2,1)S(1)}, u32[]{:S(2)}, u32[]{:S(2)}) collective-permute-start(bf16[128,128]{1,0:T(8,128)(2,1)S(1)} %get-tuple-element.23), channel_id=1, source_target_pairs={{3,4},{7,8},{11,12},{15,16},{19,20},{23,24},{27,28}} | collective-permute-start | bytes 98312 | tf_op jit(solution)/shard_map/ppermute | solution.py:296

commit v4 on v2

--- a/solution.py
+++ b/solution.py
@@ -46,8 +46,17 @@
     return jnp.where((index >= 0) & (index < last), length, 0)
 
 
-def fold_kernel(shares, in_ref, gain_ref, qkv_ref, out_ref, final_ref, head_ref, *refs):
-    map_ref, back_ref, part_ref, direct_ref, gram_ref = refs
+def fold_kernel(shares, in_hbm, gain_hbm, qkv_hbm, out_hbm, final_hbm, head_hbm, *refs):
+    map_ref, back_ref, part_ref, direct_ref, gram_ref = refs[:5]
+    in_ref, gain_ref, qkv_ref, out_ref, final_ref, head_ref, sem = refs[5:]
+    pairs = [(in_hbm, in_ref), (gain_hbm, gain_ref), (qkv_hbm.at[2], qkv_ref.at[2]), (out_hbm, out_ref)]
+    pairs += [(final_hbm, final_ref), (head_hbm, head_ref)]
+    pairs += [(qkv_hbm.at[0], qkv_ref.at[0]), (qkv_hbm.at[1], qkv_ref.at[1])]
+    copies = [pltpu.make_async_copy(source, target, sem.at[i]) for i, (source, target) in enumerate(pairs)]
+    for copy in copies:
+        copy.start()
+    copies[0].wait()
+    copies[1].wait()
     weight = in_ref[...].astype(F32)
     channels, depth = weight.shape
     width = out_ref.shape[0]
@@ -58,7 +67,9 @@
         product = matmul(both, qkv_ref[which])
         return product[:channels] + product[channels:]
 
+    copies[2].wait()
     values = folded(2)
+    copies[3].wait()
     tiled = jnp.concatenate([values] * (width // HDIM), axis=0)
     same = iota((width, width), 0) // channels == iota((width, width), 1) // HDIM
     high, low = split(jnp.where(same, tiled, 0.0))
@@ -66,6 +77,8 @@
     back = back - jnp.mean(back, axis=-1, keepdims=True)
     back_ref[:, :depth] = back.astype(BF16)
 
+    copies[4].wait()
+    copies[5].wait()
     pieces = split(back * final_ref[...][None, :]) + split(centered * final_ref[...][None, :])
     scores = matmul_nt(jnp.concatenate(pieces, axis=0), head_ref[...])
     left = iota((width, LANES), 1) < channels
@@ -80,6 +93,8 @@
     sub = lax.rem(lax.axis_index("group"), shares)
     part_ref[...] = back_ref[pl.ds(pl.multiple_of(sub * rows, rows), rows), :]
 
+    copies[6].wait()
+    copies[7].wait()
     map_ref[...] = jnp.concatenate([folded(0), folded(1)], axis=0).T.astype(BF16)
 
     high, low = split(centered)
@@ -300,9 +315,18 @@
             jax.ShapeDtypeStruct((2 * channels, depth + LANES), BF16),
             jax.ShapeDtypeStruct((channels, 2 * LANES), BF16),
         ),
-        in_specs=[VMEM] * 6,
-        compiler_params=limit(20),
+        in_specs=[pl.BlockSpec(memory_space=pltpu.HBM)] * 6,
+        compiler_params=limit(62),
         out_specs=(VMEM,) * 5,
+        scratch_shapes=[
+            pltpu.VMEM(in_weight.shape, BF16),
+            pltpu.VMEM(norm_gain.shape, F32),
+            pltpu.VMEM(qkv_weight.shape, BF16),
+            pltpu.VMEM(out_weight.shape, BF16),
+            pltpu.VMEM(final_gain.shape, F32),
+            pltpu.VMEM(head_out.shape[::-1], BF16),
+            pltpu.SemaphoreType.DMA((8,)),
+        ],
         cost_estimate=pl.CostEstimate(flops=width * depth * 1200, bytes_accessed=8 * width * depth, transcendentals=0),
         name="fold",
     )(in_weight, norm_gain, qkv_weight, out_weight, final_gain, head_out.T)

time: 95.5 us -> 86.9 us (0.910)
  local copies, waits for them, and re-layouts: 11.3 us -> 0.26 us
  Pallas kernels: 25.2 us -> 28.1 us
  other arithmetic: 2.18 us -> 0.44 us
  starting transfers between devices: 23.8 us -> 25.2 us
    unnamed x32 -> x14, local copies, waits for them, and re-layouts: 10.6 us -> 0.25 us
    pallas_call x1, Pallas kernels: 2.33 us -> 5.18 us  [body(): pl.pallas_call(functools.partial(fold_kernel, shares), out_shape=(jax.Sha...]
    ppermute x5, starting transfers between devices: 8.35 us -> 9.71 us  [across(): return lax.ppermute(value, ('group', 'seq'), moves)]
  transfers between devices with their start and end apart: 18 -> 18, of which waited for: 11 -> 10; matrix products, arithmetic and copies ran while one was open for 6% -> 0% of each run, Pallas kernels for 17% -> 18%
where the time goes in v4:
time: 86.9 us; the launch traced here: 86.5 us
  waiting for transfers between devices  32.4 us (37%)
  Pallas kernels  28.1 us (32%)
  starting transfers between devices  25.2 us (29%)
    pallas_call x2, Pallas kernels, attend(): pl.pallas_call(functools.partial(attend_kernel, count, window), out_shape...  15.6 us
    ppermute x4, waiting for transfers between devices, swap(): return lax.ppermute(value, 'group', [(g, g ^ bits) for g in range(groups)])  12.9 us
    ppermute x9, waiting for transfers between devices, gathered(): lax.ppermute(value, 'seq', [(i, i ^ k) for i in range(count)])  12.4 us
    ppermute x9, starting transfers between devices, gathered(): lax.ppermute(value, 'seq', [(i, i ^ k) for i in range(count)])  10.2 us
    ppermute x5, starting transfers between devices, across(): return lax.ppermute(value, ('group', 'seq'), moves)  9.71 us
    ppermute x5, waiting for transfers between devices, across(): return lax.ppermute(value, ('group', 'seq'), moves)  7.08 us
    pallas_call x1, Pallas kernels, body(): pl.pallas_call(functools.partial(finish_kernel, count, shares, list(high)...  5.8 us
    ppermute x4, starting transfers between devices, swap(): return lax.ppermute(value, 'group', [(g, g ^ bits) for g in range(groups)])  5.26 us
  transfers between devices with their start and end apart: 18, of which 10 were waited for; matrix products, arithmetic and copies ran while one was open for 0% of the time, Pallas kernels for 18%

profile of v4, /device:TPU:1, one launch (start us, length us, event | category | flops | bytes accessed | tf_op | source)
XLA Modules:
  0.0 86.5 jit_solution(4686233661718409459)
XLA Ops:
  0.0 5.2 %fold.1 = (bf16[256,128]{1,0:T(8,128)(2,1)}, bf16[256,1664]{1,0:T(8,128)(2,1)}, bf16[32,1664]{1,0:T(8,128)(2,1)}, bf16[128,1664]{1,0:T(8,128)(2,1)}, bf16[64,256]{1,0:T(8,128)(2,1)}) custom-call(bf16[64,1536]{1,0:T(8,128)(2,1)} %in_hbm.1, f32[1536]{0:T(1024)} %gain_hbm.1, bf16[3,1536,256]{2,1,0:T(8,128)(2,1)} %qkv_hbm.1, bf16[256,1536]{1,0:T(8,128)(2,1)} %out_hbm.1, ...), custom_call_target="tpu_custom_call" | custom-call | flops 471859200 | bytes 3145728 | tf_op jit(solution)/shard_map/fold/pallas_call | solution.py:309
  5.2 4.2 %collective-permute-start.9 = (bf16[32,1664]{1,0:T(8,128)(2,1)}, bf16[32,1664]{1,0:T(8,128)(2,1)S(1)}, u32[]{:S(2)}, u32[]{:S(2)}) collective-permute-start(bf16[32,1664]{1,0:T(8,128)(2,1)} %get-tuple-element.17), channel_id=1, source_target_pairs={{0,3},{1,2},{2,1},{3,0},{4,7},{5,6},{6,5},{7,4},{8,11},{9,10},{10,... | collective-permute-start | bytes 319496 | tf_op jit(solution)/shard_map/ppermute | solution.py:302
  9.4 0.0 collective-permute-start.8
  9.4 0.4 collective-permute-start.7
  9.8 2.6 %collective-permute-done.9 = bf16[32,1664]{1,0:T(8,128)(2,1)S(1)} collective-permute-done((bf16[32,1664]{1,0:T(8,128)(2,1)}, bf16[32,1664]{1,0:T(8,128)(2,1)S(1)}, u32[]{:S(2)}, u32[]{:S(2)}) %collective-permute-start.9) | collective-permute-done | bytes 106528 | tf_op jit(solution)/shard_map/ppermute | solution.py:302
  12.3 5.9 %collective-permute-done.8 = bf16[32,1664]{1,0:T(8,128)(2,1)S(1)} collective-permute-done((bf16[32,1664]{1,0:T(8,128)(2,1)}, bf16[32,1664]{1,0:T(8,128)(2,1)S(1)}, u32[]{:S(2)}, u32[]{:S(2)}) %collective-permute-start.8) | collective-permute-done | bytes 106528 | tf_op jit(solution)/shard_map/ppermute | solution.py:302
  18.2 0.0 collective-permute-done.7
  18.2 0.1 fusion
  18.2 1.3 %collective-permute-start.11 = (bf16[3,32,1664]{2,1,0:T(8,128)(2,1)S(1)}, bf16[3,32,1664]{2,1,0:T(8,128)(2,1)S(1)}, u32[]{:S(2)}, u32[]{:S(2)}) collective-permute-start(bf16[3,32,1664]{2,1,0:T(8,128)(2,1)S(1)} %get-tuple-element.22), channel_id=1, source_target_pairs={{0,16},{4,20},{8,24},{12,28},{16,0},{20,4},{24,8},{28,12},{1,17},{... | collective-permute-start | bytes 958472 | tf_op jit(solution)/shard_map/ppermute | solution.py:299
  19.5 1.2 %collective-permute-start.10 = (bf16[3,32,1664]{2,1,0:T(8,128)(2,1)S(1)}, bf16[3,32,1664]{2,1,0:T(8,128)(2,1)S(1)}, u32[]{:S(2)}, u32[]{:S(2)}) collective-permute-start(bf16[3,32,1664]{2,1,0:T(8,128)(2,1)S(1)} %get-tuple-element.22), channel_id=1, source_target_pairs={{0,8},{4,12},{8,0},{12,4},{16,24},{20,28},{24,16},{28,20},{1,9},{5... | collective-permute-start | bytes 958472 | tf_op jit(solution)/shard_map/ppermute | solution.py:299
  20.8 0.2 collective-permute-start.12
  21.0 5.1 %collective-permute-done.11 = bf16[3,32,1664]{2,1,0:T(8,128)(2,1)S(1)} collective-permute-done((bf16[3,32,1664]{2,1,0:T(8,128)(2,1)S(1)}, bf16[3,32,1664]{2,1,0:T(8,128)(2,1)S(1)}, u32[]{:S(2)}, u32[]{:S(2)}) %collective-permute-start.11) | collective-permute-done | bytes 319520 | tf_op jit(solution)/shard_map/ppermute | solution.py:299
  26.1 1.0 %collective-permute-done.10 = bf16[3,32,1664]{2,1,0:T(8,128)(2,1)S(1)} collective-permute-done((bf16[3,32,1664]{2,1,0:T(8,128)(2,1)S(1)}, bf16[3,32,1664]{2,1,0:T(8,128)(2,1)S(1)}, u32[]{:S(2)}, u32[]{:S(2)}) %collective-permute-start.10) | collective-permute-done | bytes 319520 | tf_op jit(solution)/shard_map/ppermute | solution.py:299
  27.0 6.8 %collective-permute-done.12 = bf16[3,32,1664]{2,1,0:T(8,128)(2,1)S(1)} collective-permute-done((bf16[3,32,1664]{2,1,0:T(8,128)(2,1)S(1)}, bf16[3,32,1664]{2,1,0:T(8,128)(2,1)S(1)}, u32[]{:S(2)}, u32[]{:S(2)}) %collective-permute-start.12) | collective-permute-done | bytes 319520 | tf_op jit(solution)/shard_map/ppermute | solution.py:299
  33.8 0.2 pad_maximum_fusion.refs_4_
  34.0 2.5 %collective-permute-start.13 = (bf16[4,3,32,1664]{3,2,1,0:T(8,128)(2,1)S(1)}, bf16[4,3,32,1664]{3,2,1,0:T(8,128)(2,1)S(1)}, u32[]{:S(2)}, u32[]{:S(2)}) collective-permute-start(bf16[4,3,32,1664]{3,2,1,0:T(8,128)(2,1)S(1)} %pad_maximum_fusion.refs_4_), channel_id=1, source_target_pairs={{0,4},{4,0},{8,12},{12,8},{16,20},{20,16},{24,28},{28,24},{1,5},{5... | collective-permute-start | bytes 3833864 | tf_op jit(solution)/shard_map/ppermute | solution.py:299
  36.6 0.0 copy-done
  36.6 0.1 copy.11
  36.7 0.1 copy.12
  36.8 0.1 pad_maximum_fusion.3.refs_0_
  36.9 2.1 %collective-permute-start.2 = (bf16[256,128]{1,0:T(8,128)(2,1)S(1)}, bf16[256,128]{1,0:T(8,128)(2,1)S(1)}, u32[]{:S(2)}, u32[]{:S(2)}) collective-permute-start(bf16[256,128]{1,0:T(8,128)(2,1)S(1)} %pad_maximum_fusion.3.refs_0_), channel_id=1, source_target_pairs={{0,3},{1,2},{2,1},{3,0},{4,7},{5,6},{6,5},{7,4},{8,11},{9,10},{10,... | collective-permute-start | bytes 196616 | tf_op jit(solution)/shard_map/ppermute | solution.py:302
  39.0 0.0 collective-permute-start.1
  39.0 1.5 %collective-permute-start = (bf16[256,128]{1,0:T(8,128)(2,1)S(1)}, bf16[256,128]{1,0:T(8,128)(2,1)S(1)}, u32[]{:S(2)}, u32[]{:S(2)}) collective-permute-start(bf16[256,128]{1,0:T(8,128)(2,1)S(1)} %pad_maximum_fusion.3.refs_0_), channel_id=1, source_target_pairs={{0,1},{1,0},{2,3},{3,2},{4,5},{5,4},{6,7},{7,6},{8,9},{9,8},{10,11... | collective-permute-start | bytes 196616 | tf_op jit(solution)/shard_map/ppermute | solution.py:302
  40.5 2.0 %collective-permute-start.5 = (bf16[256,128]{1,0:T(8,128)(2,1)S(1)}, bf16[256,128]{1,0:T(8,128)(2,1)S(1)}, u32[]{:S(2)}, u32[]{:S(2)}) collective-permute-start(bf16[256,128]{1,0:T(8,128)(2,1)S(1)} %copy-done.4), channel_id=1, source_target_pairs={{0,3},{1,2},{2,1},{3,0},{4,7},{5,6},{6,5},{7,4},{8,11},{9,10},{10,... | collective-permute-start | bytes 196616 | tf_op jit(solution)/shard_map/ppermute | solution.py:302
  42.6 0.0 collective-permute-done.2.refs_3_
  42.6 0.0 collective-permute-start.4
  42.6 4.0 %collective-permute-done.1.refs_2_ = bf16[256,128]{1,0:T(8,128)(2,1)S(1)} collective-permute-done((bf16[256,128]{1,0:T(8,128)(2,1)S(1)}, bf16[256,128]{1,0:T(8,128)(2,1)S(1)}, u32[]{:S(2)}, u32[]{:S(2)}) %collective-permute-start.1) | collective-permute-done | bytes 65568 | tf_op jit(solution)/shard_map/ppermute | solution.py:302
  46.6 0.0 collective-permute-start.3
  46.6 0.0 collective-permute-done.refs_1_
  46.6 0.1 pad_maximum_fusion.2
  46.7 4.5 %collective-permute-start.6 = (bf16[4,256,128]{2,1,0:T(8,128)(2,1)S(1)}, bf16[4,256,128]{2,1,0:T(8,128)(2,1)S(1)}, u32[]{:S(2)}, u32[]{:S(2)}) collective-permute-start(bf16[4,256,128]{2,1,0:T(8,128)(2,1)S(1)} %pad_maximum_fusion.2), channel_id=1, source_target_pairs={{4,0},{5,1},{6,2},{7,3},{8,4},{9,5},{10,6},{11,7},{12,8},{13,9},{1... | collective-permute-start | bytes 786440 | tf_op jit(solution)/shard_map/ppermute | solution.py:296
  51.2 0.0 collective-permute-done.5.refs_7_
  51.2 0.0 collective-permute-done.4.refs_6_
  51.2 0.0 collective-permute-done.3.refs_5_
  51.3 7.7 %attend.2.refs_0_ = bf16[512,1152]{1,0:T(8,128)(2,1)S(1)} custom-call(s32[15]{0:T(128)S(1)} %copy-done.1, bf16[256,128]{1,0:T(8,128)(2,1)S(1)} %pad_maximum_fusion.3.refs_0_, bf16[256,128]{1,0:T(8,128)(2,1)S(1)} %collective-permute-done.refs_1_, bf16[256,128]{1,0:T(8,128)(2,1)S(1)} %collective-permute-done.1.refs_2_, ...), custom_call_target="tpu_custom_call" | custom-call | flops 4294967296 | bytes 1048576 | tf_op jit(solution)/shard_map/attend/pallas_call | solution.py:339
  59.0 0.0 collective-permute-done.6.refs_9_
  59.0 7.9 %attend.3.refs_1_ = bf16[512,1152]{1,0:T(8,128)(2,1)S(1)} custom-call(s32[15]{0:T(128)S(1)} %copy-done.1, bf16[256,128]{1,0:T(8,128)(2,1)S(1)} %pad_maximum_fusion.3.refs_0_, bf16[256,128]{1,0:T(8,128)(2,1)S(1)} %collective-permute-done.refs_1_, bf16[256,128]{1,0:T(8,128)(2,1)S(1)} %collective-permute-done.1.refs_2_, ...), custom_call_target="tpu_custom_call" | custom-call | flops 4294967296 | bytes 1048576 | tf_op jit(solution)/shard_map/attend/pallas_call | solution.py:339
  67.0 0.0 collective-permute-done.13.refs_5_
  67.0 5.8 %finish.1 = (f32[2,256,128]{2,1,0:T(8,128)S(1)}, bf16[128,128]{1,0:T(8,128)(2,1)S(1)}, bf16[128,128]{1,0:T(8,128)(2,1)S(1)}) custom-call(s32[15]{0:T(128)S(1)} %copy-done.1, bf16[512,1152]{1,0:T(8,128)(2,1)S(1)} %attend.2.refs_0_, bf16[512,1152]{1,0:T(8,128)(2,1)S(1)} %attend.3.refs_1_, bf16[128,1664]{1,0:T(8,128)(2,1)S(1)} %copy-done.3, ...), custom_call_target="tpu_custom_call" | custom-call | flops 3221225472 | bytes 3145728 | tf_op jit(solution)/shard_map/finish/pallas_call | solution.py:368
  72.8 1.3 %collective-permute-start.15 = (bf16[128,128]{1,0:T(8,128)(2,1)S(1)}, bf16[128,128]{1,0:T(8,128)(2,1)S(1)}, u32[]{:S(2)}, u32[]{:S(2)}) collective-permute-start(bf16[128,128]{1,0:T(8,128)(2,1)S(1)} %get-tuple-element.19), channel_id=1, source_target_pairs={{3,4},{7,8},{11,12},{15,16},{19,20},{23,24},{27,28}} | collective-permute-start | bytes 98312 | tf_op jit(solution)/shard_map/ppermute | solution.py:296
  74.1 1.3 %collective-permute-start.14 = (bf16[128,128]{1,0:T(8,128)(2,1)S(1)}, bf16[128,128]{1,0:T(8,128)(2,1)S(1)}, u32[]{:S(2)}, u32[]{:S(2)}) collective-permute-start(bf16[128,128]{1,0:T(8,128)(2,1)S(1)} %get-tuple-element.19), channel_id=1, source_target_pairs={{2,4},{3,5},{6,8},{7,9},{10,12},{11,13},{14,16},{15,17},{18,20},{1... | collective-permute-start | bytes 98312 | tf_op jit(solution)/shard_map/ppermute | solution.py:296
  75.4 1.3 %collective-permute-start.17 = (bf16[128,128]{1,0:T(8,128)(2,1)S(1)}, bf16[128,128]{1,0:T(8,128)(2,1)S(1)}, u32[]{:S(2)}, u32[]{:S(2)}) collective-permute-start(bf16[128,128]{1,0:T(8,128)(2,1)S(1)} %get-tuple-element.20), channel_id=1, source_target_pairs={{3,0},{7,4},{11,8},{15,12},{19,16},{23,20},{27,24},{31,28}} | collective-permute-start | bytes 98312 | tf_op jit(solution)/shard_map/ppermute | solution.py:296
  76.7 1.3 %collective-permute-start.16 = (bf16[128,128]{1,0:T(8,128)(2,1)S(1)}, bf16[128,128]{1,0:T(8,128)(2,1)S(1)}, u32[]{:S(2)}, u32[]{:S(2)}) collective-permute-start(bf16[128,128]{1,0:T(8,128)(2,1)S(1)} %get-tuple-element.20), channel_id=1, source_target_pairs={{2,0},{3,1},{6,4},{7,5},{10,8},{11,9},{14,12},{15,13},{18,16},{19,... | collective-permute-start | bytes 98312 | tf_op jit(solution)/shard_map/ppermute | solution.py:296
  78.0 1.8 %collective-permute-done.15.refs_1_ = bf16[128,128]{1,0:T(8,128)(2,1)S(1)} collective-permute-done((bf16[128,128]{1,0:T(8,128)(2,1)S(1)}, bf16[128,128]{1,0:T(8,128)(2,1)S(1)}, u32[]{:S(2)}, u32[]{:S(2)}) %collective-permute-start.15) | collective-permute-done | bytes 32800 | tf_op jit(solution)/shard_map/ppermute | solution.py:296
  79.8 0.4 collective-permute-done.14.refs_0_
  80.2 4.6 %collective-permute-done.17.refs_3_ = bf16[128,128]{1,0:T(8,128)(2,1)S(1)} collective-permute-done((bf16[128,128]{1,0:T(8,128)(2,1)S(1)}, bf16[128,128]{1,0:T(8,128)(2,1)S(1)}, u32[]{:S(2)}, u32[]{:S(2)}) %collective-permute-start.17) | collective-permute-done | bytes 32800 | tf_op jit(solution)/shard_map/ppermute | solution.py:296
  84.8 0.3 collective-permute-done.16.refs_2_
  85.1 1.5 %combine.1 = f32[2,64,256]{2,1,0:T(8,128)} custom-call(s32[15]{0:T(128)S(1)} %copy-done.1, f32[2,64,256]{2,1,0:T(8,128)S(1)} %bitcast.16, f32[2,256,128]{2,1,0:T(8,128)S(1)} %get-tuple-element.18.rows_ref, bf16[128,128]{1,0:T(8,128)(2,1)S(1)} %collective-permute-done.14.refs_0_, bf16[128,128]{1,0:T(8,128)(2,1)S(1)} %collective-permute-done.15.refs_1_, ...), custom_call_target="tpu_custom_call" | custom-call | tf_op jit(solution)/shard_map/combine/pallas_call | solution.py:392
  (12 shorter events, 0.0 us)
Async XLA Ops:
  5.2 7.1 %collective-permute-start.9 = (bf16[32,1664]{1,0:T(8,128)(2,1)}, bf16[32,1664]{1,0:T(8,128)(2,1)S(1)}, u32[]{:S(2)}, u32[]{:S(2)}) collective-permute-start(bf16[32,1664]{1,0:T(8,128)(2,1)} %get-tuple-element.17), channel_id=1, source_target_pairs={{0,3},{1,2},{2,1},{3,0},{4,7},{5,6},{6,5},{7,4},{8,11},{9,10},{10,... | collective-permute-start | bytes 319496 | tf_op jit(solution)/shard_map/ppermute | solution.py:302
  9.4 8.8 %collective-permute-start.8 = (bf16[32,1664]{1,0:T(8,128)(2,1)}, bf16[32,1664]{1,0:T(8,128)(2,1)S(1)}, u32[]{:S(2)}, u32[]{:S(2)}) collective-permute-start(bf16[32,1664]{1,0:T(8,128)(2,1)} %get-tuple-element.17), channel_id=1, source_target_pairs={{0,2},{1,3},{2,0},{3,1},{4,6},{5,7},{6,4},{7,5},{8,10},{9,11},{10,... | collective-permute-start | bytes 319496 | tf_op jit(solution)/shard_map/ppermute | solution.py:302
  9.4 8.8 %collective-permute-start.7 = (bf16[32,1664]{1,0:T(8,128)(2,1)}, bf16[32,1664]{1,0:T(8,128)(2,1)S(1)}, u32[]{:S(2)}, u32[]{:S(2)}) collective-permute-start(bf16[32,1664]{1,0:T(8,128)(2,1)} %get-tuple-element.17), channel_id=1, source_target_pairs={{0,1},{1,0},{2,3},{3,2},{4,5},{5,4},{6,7},{7,6},{8,9},{9,8},{10,11... | collective-permute-start | bytes 319496 | tf_op jit(solution)/shard_map/ppermute | solution.py:302
  18.2 7.8 %collective-permute-start.11 = (bf16[3,32,1664]{2,1,0:T(8,128)(2,1)S(1)}, bf16[3,32,1664]{2,1,0:T(8,128)(2,1)S(1)}, u32[]{:S(2)}, u32[]{:S(2)}) collective-permute-start(bf16[3,32,1664]{2,1,0:T(8,128)(2,1)S(1)} %get-tuple-element.22), channel_id=1, source_target_pairs={{0,16},{4,20},{8,24},{12,28},{16,0},{20,4},{24,8},{28,12},{1,17},{... | collective-permute-start | bytes 958472 | tf_op jit(solution)/shard_map/ppermute | solution.py:299
  19.5 7.5 %collective-permute-start.10 = (bf16[3,32,1664]{2,1,0:T(8,128)(2,1)S(1)}, bf16[3,32,1664]{2,1,0:T(8,128)(2,1)S(1)}, u32[]{:S(2)}, u32[]{:S(2)}) collective-permute-start(bf16[3,32,1664]{2,1,0:T(8,128)(2,1)S(1)} %get-tuple-element.22), channel_id=1, source_target_pairs={{0,8},{4,12},{8,0},{12,4},{16,24},{20,28},{24,16},{28,20},{1,9},{5... | collective-permute-start | bytes 958472 | tf_op jit(solution)/shard_map/ppermute | solution.py:299
  20.8 13.1 %collective-permute-start.12 = (bf16[3,32,1664]{2,1,0:T(8,128)(2,1)S(1)}, bf16[3,32,1664]{2,1,0:T(8,128)(2,1)S(1)}, u32[]{:S(2)}, u32[]{:S(2)}) collective-permute-start(bf16[3,32,1664]{2,1,0:T(8,128)(2,1)S(1)} %get-tuple-element.22), channel_id=1, source_target_pairs={{0,24},{4,28},{8,16},{12,20},{16,8},{20,12},{24,0},{28,4},{1,25},{... | collective-permute-start | bytes 958472 | tf_op jit(solution)/shard_map/ppermute | solution.py:299
  33.8 2.8 %copy-start = (f32[2,256,64]{1,2,0:T(8,128)S(1)}, f32[2,256,64]{1,2,0:T(8,128)}, u32[]{:S(2)}) copy-start(f32[2,256,64]{1,2,0:T(8,128)} %param.8) | copy-start | bytes 393220
  33.8 6.7 %copy-start.4 = (bf16[256,128]{1,0:T(8,128)(2,1)S(1)}, bf16[256,128]{1,0:T(8,128)(2,1)}, u32[]{:S(2)}) copy-start(bf16[256,128]{1,0:T(8,128)(2,1)} %get-tuple-element.13.refs_4_) | copy-start | bytes 196612
  33.8 17.4 %copy-start.1 = (s32[15]{0:T(128)S(1)}, s32[15]{0:T(128)}, u32[]{:S(2)}) copy-start(s32[15]{0:T(128)} %margin_ref.7) | copy-start | bytes 184
  33.8 17.4 %copy-start.5 = (bf16[64,256]{1,0:T(8,128)(2,1)S(1)}, bf16[64,256]{1,0:T(8,128)(2,1)}, u32[]{:S(2)}) copy-start(bf16[64,256]{1,0:T(8,128)(2,1)} %get-tuple-element.14.refs_8_) | copy-start | bytes 98308
  34.0 32.9 %collective-permute-start.13 = (bf16[4,3,32,1664]{3,2,1,0:T(8,128)(2,1)S(1)}, bf16[4,3,32,1664]{3,2,1,0:T(8,128)(2,1)S(1)}, u32[]{:S(2)}, u32[]{:S(2)}) collective-permute-start(bf16[4,3,32,1664]{3,2,1,0:T(8,128)(2,1)S(1)} %pad_maximum_fusion.refs_4_), channel_id=1, source_target_pairs={{0,4},{4,0},{8,12},{12,8},{16,20},{20,16},{24,28},{28,24},{1,5},{5... | collective-permute-start | bytes 3833864 | tf_op jit(solution)/shard_map/ppermute | solution.py:299
  36.9 5.6 %collective-permute-start.2 = (bf16[256,128]{1,0:T(8,128)(2,1)S(1)}, bf16[256,128]{1,0:T(8,128)(2,1)S(1)}, u32[]{:S(2)}, u32[]{:S(2)}) collective-permute-start(bf16[256,128]{1,0:T(8,128)(2,1)S(1)} %pad_maximum_fusion.3.refs_0_), channel_id=1, source_target_pairs={{0,3},{1,2},{2,1},{3,0},{4,7},{5,6},{6,5},{7,4},{8,11},{9,10},{10,... | collective-permute-start | bytes 196616 | tf_op jit(solution)/shard_map/ppermute | solution.py:302
  39.0 7.6 %collective-permute-start.1 = (bf16[256,128]{1,0:T(8,128)(2,1)S(1)}, bf16[256,128]{1,0:T(8,128)(2,1)S(1)}, u32[]{:S(2)}, u32[]{:S(2)}) collective-permute-start(bf16[256,128]{1,0:T(8,128)(2,1)S(1)} %pad_maximum_fusion.3.refs_0_), channel_id=1, source_target_pairs={{0,2},{1,3},{2,0},{3,1},{4,6},{5,7},{6,4},{7,5},{8,10},{9,11},{10,... | collective-permute-start | bytes 196616 | tf_op jit(solution)/shard_map/ppermute | solution.py:302
  39.0 7.6 %collective-permute-start = (bf16[256,128]{1,0:T(8,128)(2,1)S(1)}, bf16[256,128]{1,0:T(8,128)(2,1)S(1)}, u32[]{:S(2)}, u32[]{:S(2)}) collective-permute-start(bf16[256,128]{1,0:T(8,128)(2,1)S(1)} %pad_maximum_fusion.3.refs_0_), channel_id=1, source_target_pairs={{0,1},{1,0},{2,3},{3,2},{4,5},{5,4},{6,7},{7,6},{8,9},{9,8},{10,11... | collective-permute-start | bytes 196616 | tf_op jit(solution)/shard_map/ppermute | solution.py:302
  40.5 10.7 %collective-permute-start.5 = (bf16[256,128]{1,0:T(8,128)(2,1)S(1)}, bf16[256,128]{1,0:T(8,128)(2,1)S(1)}, u32[]{:S(2)}, u32[]{:S(2)}) collective-permute-start(bf16[256,128]{1,0:T(8,128)(2,1)S(1)} %copy-done.4), channel_id=1, source_target_pairs={{0,3},{1,2},{2,1},{3,0},{4,7},{5,6},{6,5},{7,4},{8,11},{9,10},{10,... | collective-permute-start | bytes 196616 | tf_op jit(solution)/shard_map/ppermute | solution.py:302
  42.6 8.7 %collective-permute-start.4 = (bf16[256,128]{1,0:T(8,128)(2,1)S(1)}, bf16[256,128]{1,0:T(8,128)(2,1)S(1)}, u32[]{:S(2)}, u32[]{:S(2)}) collective-permute-start(bf16[256,128]{1,0:T(8,128)(2,1)S(1)} %copy-done.4), channel_id=1, source_target_pairs={{0,2},{1,3},{2,0},{3,1},{4,6},{5,7},{6,4},{7,5},{8,10},{9,11},{10,... | collective-permute-start | bytes 196616 | tf_op jit(solution)/shard_map/ppermute | solution.py:302
  46.6 4.7 %collective-permute-start.3 = (bf16[256,128]{1,0:T(8,128)(2,1)S(1)}, bf16[256,128]{1,0:T(8,128)(2,1)S(1)}, u32[]{:S(2)}, u32[]{:S(2)}) collective-permute-start(bf16[256,128]{1,0:T(8,128)(2,1)S(1)} %copy-done.4), channel_id=1, source_target_pairs={{0,1},{1,0},{2,3},{3,2},{4,5},{5,4},{6,7},{7,6},{8,9},{9,8},{10,11... | collective-permute-start | bytes 196616 | tf_op jit(solution)/shard_map/ppermute | solution.py:302
  46.7 12.3 %collective-permute-start.6 = (bf16[4,256,128]{2,1,0:T(8,128)(2,1)S(1)}, bf16[4,256,128]{2,1,0:T(8,128)(2,1)S(1)}, u32[]{:S(2)}, u32[]{:S(2)}) collective-permute-start(bf16[4,256,128]{2,1,0:T(8,128)(2,1)S(1)} %pad_maximum_fusion.2), channel_id=1, source_target_pairs={{4,0},{5,1},{6,2},{7,3},{8,4},{9,5},{10,6},{11,7},{12,8},{13,9},{1... | collective-permute-start | bytes 786440 | tf_op jit(solution)/shard_map/ppermute | solution.py:296
  59.0 8.0 %copy-start.2 = (bf16[256,1664]{1,0:T(8,128)(2,1)S(1)}, bf16[256,1664]{1,0:T(8,128)(2,1)}, u32[]{:S(2)}) copy-start(bf16[256,1664]{1,0:T(8,128)(2,1)} %get-tuple-element.16.refs_3_) | copy-start | bytes 2555908
  59.0 8.0 %copy-start.3 = (bf16[128,1664]{1,0:T(8,128)(2,1)S(1)}, bf16[128,1664]{1,0:T(8,128)(2,1)}, u32[]{:S(2)}) copy-start(bf16[128,1664]{1,0:T(8,128)(2,1)} %get-tuple-element.15.refs_2_) | copy-start | bytes 1277956
  72.8 7.0 %collective-permute-start.15 = (bf16[128,128]{1,0:T(8,128)(2,1)S(1)}, bf16[128,128]{1,0:T(8,128)(2,1)S(1)}, u32[]{:S(2)}, u32[]{:S(2)}) collective-permute-start(bf16[128,128]{1,0:T(8,128)(2,1)S(1)} %get-tuple-element.19), channel_id=1, source_target_pairs={{3,4},{7,8},{11,12},{15,16},{19,20},{23,24},{27,28}} | collective-permute-start | bytes 98312 | tf_op jit(solution)/shard_map/ppermute | solution.py:296
  74.1 6.1 %collective-permute-start.14 = (bf16[128,128]{1,0:T(8,128)(2,1)S(1)}, bf16[128,128]{1,0:T(8,128)(2,1)S(1)}, u32[]{:S(2)}, u32[]{:S(2)}) collective-permute-start(bf16[128,128]{1,0:T(8,128)(2,1)S(1)} %get-tuple-element.19), channel_id=1, source_target_pairs={{2,4},{3,5},{6,8},{7,9},{10,12},{11,13},{14,16},{15,17},{18,20},{1... | collective-permute-start | bytes 98312 | tf_op jit(solution)/shard_map/ppermute | solution.py:296
  75.4 9.4 %collective-permute-start.17 = (bf16[128,128]{1,0:T(8,128)(2,1)S(1)}, bf16[128,128]{1,0:T(8,128)(2,1)S(1)}, u32[]{:S(2)}, u32[]{:S(2)}) collective-permute-start(bf16[128,128]{1,0:T(8,128)(2,1)S(1)} %get-tuple-element.20), channel_id=1, source_target_pairs={{3,0},{7,4},{11,8},{15,12},{19,16},{23,20},{27,24},{31,28}} | collective-permute-start | bytes 98312 | tf_op jit(solution)/shard_map/ppermute | solution.py:296
  76.7 8.4 %collective-permute-start.16 = (bf16[128,128]{1,0:T(8,128)(2,1)S(1)}, bf16[128,128]{1,0:T(8,128)(2,1)S(1)}, u32[]{:S(2)}, u32[]{:S(2)}) collective-permute-start(bf16[128,128]{1,0:T(8,128)(2,1)S(1)} %get-tuple-element.20), channel_id=1, source_target_pairs={{2,0},{3,1},{6,4},{7,5},{10,8},{11,9},{14,12},{15,13},{18,16},{19,... | collective-permute-start | bytes 98312 | tf_op jit(solution)/shard_map/ppermute | solution.py:296

commit v5 on v2

v5 whole, which is shorter than its diff:
```python
import functools
import math

import jax
import jax.numpy as jnp
from jax import lax
from jax.experimental import pallas as pl
from jax.experimental.pallas import tpu as pltpu
from jax.sharding import PartitionSpec as P

HDIM = 64
OVMAX = 512
LANES = 128
QUAD = 4 * HDIM
STEP = -0.5
F32 = jnp.float32
BF16 = jnp.bfloat16
VMEM = pl.BlockSpec(memory_space=pltpu.VMEM)
SMEM = pl.BlockSpec(memory_space=pltpu.SMEM)


def limit(mebibytes):
    return pltpu.CompilerParams(vmem_limit_bytes=mebibytes << 20)


def iota(shape, dim):
    return lax.broadcasted_iota(jnp.int32, shape, dim)


def matmul(lhs, rhs):
    return jnp.dot(lhs, rhs, preferred_element_type=F32)


def matmul_nt(lhs, rhs, precision=None):
    return lax.dot_general(lhs, rhs, (((1,), (1,)), ((), ())), precision=precision, preferred_element_type=F32)


def split(value):
    high = value.astype(BF16)
    return high, (value - high.astype(F32)).astype(BF16)


def margin_at(margin_ref, index):
    last = margin_ref.shape[0]
    length = margin_ref[jnp.clip(index, 0, last - 1)]
    return jnp.where((index >= 0) & (index < last), length, 0)


def started(pairs, sem):
    copies = [pltpu.make_async_copy(source, target, sem.at[i]) for i, (source, target) in enumerate(pairs)]
    for copy in copies:
        copy.start()
    return copies


def folded(both, weights, channels):
    product = matmul(both, weights)
    return product[:channels] + product[channels:]


def halves(value):
    channels = value.shape[1]
    value = jnp.concatenate([value, value], axis=1)
    high, low = split(value)
    left = iota(value.shape, 1) < channels
    return jnp.where(left, high.astype(F32), low.astype(F32)).astype(BF16)


def centered_rows(in_ref):
    weight = in_ref[...].astype(F32)
    return weight - jnp.mean(weight, axis=-1, keepdims=True)


def fold_back_kernel(shares, in_hbm, gain_hbm, qkv_hbm, out_hbm, final_hbm, head_hbm, *refs):
    back_ref, part_ref, in_ref, gain_ref, value_ref, out_ref, final_ref, head_ref, sem = refs
    pairs = [(in_hbm, in_ref), (gain_hbm, gain_ref), (qkv_hbm.at[2], value_ref), (out_hbm, out_ref)]
    copies = started(pairs + [(final_hbm, final_ref), (head_hbm, head_ref)], sem)
    copies[0].wait()
    copies[1].wait()
    centered = centered_rows(in_ref)
    channels, depth = centered.shape
    width = out_ref.shape[0]
    both = jnp.concatenate(split(centered * gain_ref[...][None, :]), axis=0)
    copies[2].wait()
    values = folded(both, value_ref[...], channels)
    copies[3].wait()
    tiled = jnp.concatenate([values] * (width // HDIM), axis=0)
    same = iota((width, width), 0) // channels == iota((width, width), 1) // HDIM
    high, low = split(jnp.where(same, tiled, 0.0))
    back = matmul(high, out_ref[...]) + matmul(low, out_ref[...])
    back = back - jnp.mean(back, axis=-1, keepdims=True)
    back_ref[:, :depth] = back.astype(BF16)
    copies[4].wait()
    copies[5].wait()
    scores = matmul_nt(jnp.concatenate(split(back * final_ref[...][None, :]), axis=0), head_ref[...])
    back_ref[:, depth:] = halves(scores[:width] + scores[width:])
    rows = width // shares
    sub = lax.rem(lax.axis_index("group"), shares)
    part_ref[...] = back_ref[pl.ds(pl.multiple_of(sub * rows, rows), rows), :]


def fold_maps_kernel(in_hbm, gain_hbm, qkv_hbm, final_hbm, head_hbm, *refs):
    map_ref, direct_ref, gram_ref, in_ref, gain_ref, query_ref, key_ref, final_ref, head_ref, sem = refs
    pairs = [(in_hbm, in_ref), (gain_hbm, gain_ref), (qkv_hbm.at[0], query_ref), (qkv_hbm.at[1], key_ref)]
    copies = started(pairs + [(final_hbm, final_ref), (head_hbm, head_ref)], sem)
    copies[0].wait()
    copies[1].wait()
    centered = centered_rows(in_ref)
    channels, depth = centered.shape
    both = jnp.concatenate(split(centered * gain_ref[...][None, :]), axis=0)

    high, low = split(centered)
    direct_ref[:channels, :depth] = high
    direct_ref[channels:, :depth] = low
    gram = matmul_nt(jnp.concatenate([high, low], axis=0), jnp.concatenate([high, low], axis=0))
    gram = (gram[:channels] + gram[channels:]) * (1.0 / depth)
    gram = gram + pltpu.roll(gram, channels, 1)
    first, _ = split(gram)
    second, third = split(gram - first.astype(F32))
    left = iota((channels, LANES), 1) < channels
    gram_ref[:, :LANES] = jnp.where(left, first.astype(F32), second.astype(F32)).astype(BF16)
    gram_ref[:, LANES:] = jnp.where(left, third.astype(F32), 0.0).astype(BF16)

    copies[2].wait()
    queries = folded(both, query_ref[...], channels)
    copies[3].wait()
    keys = folded(both, key_ref[...], channels)
    map_ref[...] = jnp.concatenate([queries, keys], axis=0).T.astype(BF16)

    copies[4].wait()
    copies[5].wait()
    scores = matmul_nt(jnp.concatenate(split(centered * final_ref[...][None, :]), axis=0), head_ref[...])
    direct_ref[:channels, depth:] = halves(scores[:channels] + scores[channels:])
    direct_ref[channels:, depth:] = jnp.zeros((channels, LANES), BF16)


def twice(tokens):
    tokens = tokens.astype(F32)
    return tokens + pltpu.roll(tokens, LANES // 2, 1)


def bend(tokens, doubled, gram_ref):
    bent = matmul(tokens[:, : gram_ref.shape[0]], gram_ref[...])
    return (bent[:, :LANES] + bent[:, LANES:]) * doubled


def variance(bent):
    return jnp.maximum(jnp.sum(bent, axis=-1, keepdims=True), 0.0) + 1e-05


def quads(maps, mine, query_eps, key_eps, right_ref, ext_ref, sum_ref, key_scr, query_scr, p_scr):
    heads_width = maps.shape[0]
    total = right_ref.shape[0]
    share = mine.shape[0]
    channels = LANES // 2
    tile = min(total, 256)
    for start in range(0, total, tile):
        keys = matmul_nt(maps, right_ref[start : start + tile]).reshape(heads_width // HDIM, HDIM, tile)
        norm = jnp.mean(keys * keys, axis=1, keepdims=True)
        keys = keys * lax.rsqrt(norm + key_eps[None, :, start : start + tile])
        key_scr[:, start : start + tile] = keys.reshape(heads_width, tile).astype(BF16)
    one_head = iota((QUAD, QUAD), 0) // HDIM == iota((QUAD, QUAD), 1) // HDIM
    spread = jnp.where(one_head, 1.0 / HDIM, 0.0).astype(BF16)
    head_of = iota((share, QUAD), 1) // HDIM
    scale = HDIM ** (-0.5) * math.log2(math.e)
    left = iota((share, LANES), 1) < channels
    for quad in range(heads_width // QUAD):
        span = slice(quad * QUAD, (quad + 1) * QUAD)
        queries = matmul_nt(mine, maps[span, :])
        norm = matmul((queries * queries).astype(BF16), spread)
        queries = (queries * lax.rsqrt(norm + query_eps)).astype(BF16)
        for head in range(4):
            query_scr[quad % 2, head * share : (head + 1) * share, :] = jnp.where(
                head_of == head, queries, jnp.zeros_like(queries)
            )
        for start in range(0, total, tile):
            scores = matmul(query_scr[quad % 2], key_scr[span, start : start + tile])
            p_scr[quad % 2, :, start : start + tile] = jnp.exp2(scores * scale).astype(BF16)
        summed = matmul(p_scr[quad % 2], ext_ref[...])
        summed = summed[:, :LANES] / summed[:, LANES:]
        for pair in range(2):
            even = summed[2 * pair * share : (2 * pair + 1) * share]
            odd = summed[(2 * pair + 1) * share : (2 * pair + 2) * share]
            at = slice(quad * QUAD + pair * LANES, quad * QUAD + (pair + 1) * LANES)
            sum_ref[:share, at] = jnp.where(left, even, pltpu.roll(odd, HDIM, 1)).astype(BF16)
            sum_ref[share:, at] = jnp.where(left, pltpu.roll(even, HDIM, 1), odd).astype(BF16)


def attend_own_kernel(count, window, own_width, margin_ref, *refs):
    piece_refs, refs = refs[:count], refs[count:]
    map_ref, gram_ref, refs = refs[0], refs[1], refs[2:]
    if window:
        next_ref, refs = refs[0], refs[1:]
    sum_ref, right_ref, mine_ref, ext_ref, eps_ref, slot_scr, next_scr, win_scr, key_scr, query_scr, p_scr = refs
    total = win_scr.shape[0]
    channels = gram_ref.shape[0]
    share = total // count
    low = total - OVMAX
    group_pos = lax.axis_index("group")
    seq_pos = lax.axis_index("seq")
    over_len = margin_at(margin_ref, 2 * group_pos + window)
    own = total - over_len

    next_scr[:OVMAX, :] = jnp.zeros((OVMAX, LANES), F32)
    for k in range(count):
        source = jnp.bitwise_xor(seq_pos, k) * share
        at = pl.ds(pl.multiple_of(source, share), share)
        after = pl.ds(pl.multiple_of(source + OVMAX, share), share)
        slot = piece_refs[k][...].astype(F32)
        slot_scr[at, :] = pltpu.roll(slot, channels, 1) if window else slot
        next_scr[after, :] = next_ref[k].astype(F32) if window else pltpu.roll(slot, channels, 1)
    left = iota((OVMAX, LANES), 1) < channels
    for start in range(0, total, OVMAX):
        rows = slot_scr[start : start + OVMAX, :]
        if start >= low:
            tail = next_scr[pl.ds(over_len + (start - low), OVMAX), :]
            rows = jnp.where(iota(rows.shape, 0) + start < own, rows, tail)
        win_scr[start : start + OVMAX, :] = jnp.where(left, rows, 0.0).astype(BF16)

    win = win_scr[...]
    mine = win_scr[pl.ds(pl.multiple_of(seq_pos * share, share), share), :]
    mine_ref[...] = mine
    mine_twice = twice(mine)
    sum_ref[:share, own_width:] = mine_twice.astype(BF16)
    sum_ref[share:, own_width:] = mine_twice.astype(BF16)
    query_eps = variance(bend(mine, mine_twice, gram_ref)) * 1e-06
    doubled = twice(win)
    bent = bend(win, doubled, gram_ref)
    ones = jnp.ones((16, LANES), BF16)
    key_eps = (jnp.maximum(matmul_nt(ones, bent.astype(BF16))[:8], 0.0) + 1e-05) * 1e-06
    eps_ref[...] = key_eps

    scaled = doubled * lax.rsqrt(variance(bent))
    counted = (iota((total, LANES), 0) >= jnp.minimum(own, total - 1)).astype(F32)
    left = iota((total, LANES), 1) < channels
    ext_ref[:, :LANES] = jnp.where(left, scaled, scaled * counted).astype(BF16)
    ext_ref[:, LANES:] = jnp.where(left, 1.0, counted).astype(BF16)
    right_ref[...] = jnp.where(left, 0.0, doubled).astype(BF16)
    if own_width:
        quads(map_ref[...], mine, query_eps, key_eps[:1], right_ref, ext_ref, sum_ref, key_scr, query_scr, p_scr)


def attend_rest_kernel(gram_ref, right_ref, mine_ref, ext_ref, eps_ref, *refs):
    map_refs, refs = refs[:-5], refs[-5:]
    sum_ref, map_scr, key_scr, query_scr, p_scr = refs
    width = map_refs[0].shape[0]
    for k, ref in enumerate(map_refs):
        map_scr[k * width : (k + 1) * width, :] = ref[...]
    mine = mine_ref[...]
    query_eps = variance(bend(mine, twice(mine), gram_ref)) * 1e-06
    maps = map_scr[...]
    quads(maps, mine, query_eps, eps_ref[:1, :], right_ref, ext_ref, sum_ref, key_scr, query_scr, p_scr)


def finish_kernel(count, shares, high, margin_ref, *refs):
    first_ref, first_rest, second_ref, second_rest, direct_ref, back_ref, far_ref, near_ref = refs[:8]
    rows_ref, packed_first, packed_second, all_scr, square_scr = refs[8:]
    width = back_ref.shape[0]
    depth = back_ref.shape[1] - LANES
    share = first_ref.shape[0] // 2
    full = width * count
    total = share * count
    part = width // shares
    channels = direct_ref.shape[0] // 2
    group_pos = lax.axis_index("group")
    seq_pos = lax.axis_index("seq")
    sub = lax.rem(group_pos, shares)
    all_scr[:width, :] = back_ref[...]
    all_scr[full:, :] = direct_ref[...]
    for i, m in enumerate(high):
        for near, ref in ((0, far_ref), (1, near_ref)):
            place = jnp.bitwise_xor(sub, m ^ near) * part
            for k in range(1, count):
                all_scr[pl.ds(pl.multiple_of(place + k * width, part), part), :] = ref[i, k - 1]
    tile = 2 * LANES
    own = first_ref.shape[1] - LANES
    windows = ((first_ref, first_rest), (second_ref, second_rest))
    known = jnp.concatenate(
        [jnp.concatenate([ref[:, :own], rest[...], ref[:, own:]][not own :], axis=1) for ref, rest in windows], axis=0
    )
    for start in range(0, depth, tile):
        mixed = matmul(known, all_scr[:, start : start + tile])
        squares = mixed * mixed
        squares = squares[:, :LANES] + squares[:, LANES:]
        square_scr[...] = squares if start == 0 else square_scr[...] + squares
    score = matmul(known, all_scr[:, depth:])
    variance = jnp.sum(square_scr[...], axis=-1, keepdims=True) * (1.0 / depth)
    score = (score + pltpu.roll(score, channels, 1)) * lax.rsqrt(variance + 1e-05)
    position = iota((share, LANES), 0) + seq_pos * share
    left = iota((share // 2, LANES), 1) < channels
    for window, packed_ref in enumerate((packed_first, packed_second)):
        at = 2 * share * window
        own = total - margin_at(margin_ref, 2 * group_pos + window)
        margin = jnp.where(position >= own, score[at + share : at + 2 * share], 0.0)
        signed = score[at : at + share] - margin
        rows_ref[window] = signed
        packed_ref[...] = jnp.where(left, signed[: share // 2], signed[share // 2 :]).astype(BF16)


def combine_kernel(count, deltas, margin_ref, latent_ref, rows_ref, *refs):
    out_ref, tail_scr = refs[2 * len(deltas) :]
    channels, share = latent_ref.shape[1:]
    total = share * count
    group_pos = lax.axis_index("group")
    seq_pos = lax.axis_index("seq")
    for slot in range(2):
        before = margin_at(margin_ref, 2 * group_pos + slot - 1)
        own = total - margin_at(margin_ref, 2 * group_pos + slot)
        tail_scr[...] = jnp.zeros_like(tail_scr)
        for delta, ref in zip(deltas, refs[slot * len(deltas) : (slot + 1) * len(deltas)]):
            row = (seq_pos + delta) * share - (total - OVMAX)
            for half in range(2):
                value = ref[...].astype(F32)
                value = pltpu.roll(value, channels, 1) if half else value
                at = pl.ds(pl.multiple_of(row + half * (share // 2), share // 2), share // 2)
                tail_scr[at, :] = value
        moved = tail_scr[pl.ds(OVMAX - before + seq_pos * share, share), :]
        score = (rows_ref[slot] + moved).T[:channels]
        keep = iota(score.shape, 1) + seq_pos * share < own
        out_ref[slot] = jnp.where(keep, latent_ref[slot] + STEP * score, 0.0)


def body(latent, margin_len, in_weight, norm_gain, qkv_weight, out_weight, final_gain, head_out):
    count = lax.axis_size("seq")
    groups = lax.axis_size("group")
    share, channels = latent.shape[1:]
    total = share * count
    width, depth = out_weight.shape
    full = width * count
    shares = min(groups, width // 16)
    high = range(0, shares, 2)

    def across(value, group_by, pairs):
        moves = [
            (g * count + i, (g + group_by) * count + j)
            for g in range(groups)
            for i, j in pairs
            if 0 <= g + group_by < groups
        ]
        return lax.ppermute(value, ("group", "seq"), moves)

    def swap(value, bits):
        return lax.ppermute(value, "group", [(g, g ^ bits) for g in range(groups)])

    def gathered(value):
        return [lax.ppermute(value, "seq", [(i, i ^ k) for i in range(count)]) for k in range(1, count)]

    turned = latent.transpose(0, 2, 1)
    packed = jnp.concatenate([latent[0], latent[1]], axis=1).astype(BF16)
    pieces = [packed] + gathered(packed)
    stacked = jnp.stack(pieces)
    following = across(stacked, -1, [(i, i) for i in range(count)])
    hbm = pl.BlockSpec(memory_space=pltpu.HBM)
    small = (pltpu.VMEM(final_gain.shape, F32), pltpu.VMEM(head_out.shape[::-1], BF16), pltpu.SemaphoreType.DMA((6,)))
    fronts = (pltpu.VMEM(in_weight.shape, BF16), pltpu.VMEM(norm_gain.shape, F32))
    matrix = pltpu.VMEM(qkv_weight.shape[1:], BF16)
    back, part = pl.pallas_call(
        functools.partial(fold_back_kernel, shares),
        out_shape=(
            jax.ShapeDtypeStruct((width, depth + LANES), BF16),
            jax.ShapeDtypeStruct((width // shares, depth + LANES), BF16),
        ),
        in_specs=[hbm] * 6,
        compiler_params=limit(62),
        out_specs=(VMEM,) * 2,
        scratch_shapes=[*fronts, matrix, pltpu.VMEM(out_weight.shape, BF16), *small],
        cost_estimate=pl.CostEstimate(flops=width * depth * 1000, bytes_accessed=5 * width * depth, transcendentals=0),
        name="fold_back",
    )(in_weight, norm_gain, qkv_weight, out_weight, final_gain, head_out.T)
    own_part = jnp.stack(gathered(part))
    maps, direct, gram = pl.pallas_call(
        fold_maps_kernel,
        out_shape=(
            jax.ShapeDtypeStruct((width, LANES), BF16),
            jax.ShapeDtypeStruct((2 * channels, depth + LANES), BF16),
            jax.ShapeDtypeStruct((channels, 2 * LANES), BF16),
        ),
        in_specs=[hbm] * 5,
        compiler_params=limit(62),
        out_specs=(VMEM,) * 3,
        scratch_shapes=[*fronts, matrix, matrix, *small],
        cost_estimate=pl.CostEstimate(flops=width * depth * 600, bytes_accessed=5 * width * depth, transcendentals=0),
        name="fold_maps",
    )(in_weight, norm_gain, qkv_weight, final_gain, head_out.T)
    far_maps = gathered(maps)
    own_width = width // QUAD * QUAD
    rest_maps = far_maps if own_width else [maps] + far_maps
    rest_width = full - own_width

    def attention(lanes):
        return pl.CostEstimate(
            flops=16 * share * total * lanes,
            bytes_accessed=4 * lanes * share,
            transcendentals=share * total * lanes // HDIM,
        )

    def scratch(lanes):
        return [
            pltpu.VMEM((lanes, total), BF16),
            pltpu.VMEM((2, 4 * share, QUAD), BF16),
            pltpu.VMEM((2, 4 * share, total), BF16),
        ]

    def attend_own(window):
        extra = [following] if window else []
        return pl.pallas_call(
            functools.partial(attend_own_kernel, count, window, own_width),
            out_shape=(
                jax.ShapeDtypeStruct((2 * share, own_width + LANES), BF16),
                jax.ShapeDtypeStruct((total, LANES), BF16),
                jax.ShapeDtypeStruct((share, LANES), BF16),
                jax.ShapeDtypeStruct((total, QUAD), BF16),
                jax.ShapeDtypeStruct((8, total), F32),
            ),
            in_specs=[SMEM] + [VMEM] * (count + len(extra) + 2),
            compiler_params=limit(24),
            out_specs=(VMEM,) * 5,
            scratch_shapes=[
                pltpu.VMEM((total, LANES), F32),
                pltpu.VMEM((OVMAX + total, LANES), F32),
                pltpu.VMEM((total, LANES), BF16),
                *scratch(max(own_width, QUAD)),
            ],
            cost_estimate=attention(max(own_width, QUAD)),
            name="attend_own",
        )(margin_len, *pieces, maps, gram, *extra)

    def attend_rest(state):
        return pl.pallas_call(
            attend_rest_kernel,
            out_shape=jax.ShapeDtypeStruct((2 * share, rest_width), BF16),
            in_specs=[VMEM] * (5 + len(rest_maps)),
            compiler_params=limit(28),
            out_specs=VMEM,
            scratch_shapes=[pltpu.VMEM((rest_width, LANES), BF16), *scratch(rest_width)],
            cost_estimate=attention(rest_width),
            name="attend_rest",
        )(gram, *state, *rest_maps)

    first, *first_state = attend_own(0)
    second, *second_state = attend_own(1)
    first_rest = attend_rest(first_state)
    second_rest = attend_rest(second_state)
    planes = [swap(own_part, bits) for bits in high[1:]]
    far = jnp.stack([own_part] + planes)
    near = swap(far, 1)
    rows, *tails = pl.pallas_call(
        functools.partial(finish_kernel, count, shares, list(high)),
        out_shape=(
            jax.ShapeDtypeStruct((2, share, LANES), F32),
            jax.ShapeDtypeStruct((share // 2, LANES), BF16),
            jax.ShapeDtypeStruct((share // 2, LANES), BF16),
        ),
        in_specs=[SMEM] + [VMEM] * 8,
        compiler_params=limit(24),
        out_specs=(VMEM, VMEM, VMEM),
        scratch_shapes=[
            pltpu.VMEM((full + 2 * channels, depth + LANES), BF16),
            pltpu.VMEM((4 * share, LANES), F32),
        ],
        cost_estimate=pl.CostEstimate(
            flops=8 * share * full * depth, bytes_accessed=2 * full * depth, transcendentals=0
        ),
        name="finish",
    )(margin_len, first, first_rest, second, second_rest, direct, back, far, near)

    deltas = list(range((total - OVMAX) // share, count))
    received = []
    for window, group_by in ((1, 1), (0, 0)):
        received += [across(tails[window], group_by, [(i, i - d) for i in range(d, count)]) for d in deltas]
    turned = pl.pallas_call(
        functools.partial(combine_kernel, count, deltas),
        out_shape=jax.ShapeDtypeStruct(turned.shape, F32),
        in_specs=[SMEM] + [VMEM] * (2 + len(received)),
        compiler_params=limit(8),
        out_specs=VMEM,
        scratch_shapes=[pltpu.VMEM((OVMAX + total + share, LANES), F32)],
        name="combine",
    )(margin_len, turned, rows, *received)
    return turned.transpose(0, 2, 1)


def solution(mesh):
    in_specs = (
        P("group", "seq", None),
        P(),
        P(),
        P(),
        P(None, None, "seq"),
        P("seq", None),
        P(),
        P(),
    )
    out_specs = P("group", "seq", None)

    return jax.shard_map(body, mesh=mesh, in_specs=in_specs, out_specs=out_specs, check_vma=False)
```

time: 95.5 us -> 88.5 us (0.927)
  local copies, waits for them, and re-layouts: 11.3 us -> 1.86 us
  Pallas kernels: 25.2 us -> 32 us
  waiting for transfers between devices: 31.9 us -> 26.6 us
  starting transfers between devices: 23.8 us -> 26.6 us
  other arithmetic: 2.18 us -> 0.44 us
    unnamed x32 -> x18, local copies, waits for them, and re-layouts: 10.6 us -> 1.85 us
    pallas_call x3 -> x6, Pallas kernels: 18 us -> 24 us  [the longest x2 10 us: attend_rest(): pl.pallas_call(attend_rest_kernel, out_shape=jax.ShapeDtypeStruct((2 * sh...]
    ppermute x9, waiting for transfers between devices: 12.7 us -> 8.44 us  [gathered(): lax.ppermute(value, 'seq', [(i, i ^ k) for i in range(count)])]
    ppermute x9, starting transfers between devices: 10.2 us -> 11.8 us  [gathered(): lax.ppermute(value, 'seq', [(i, i ^ k) for i in range(count)])]
    ppermute x5, starting transfers between devices: 8.35 us -> 9.57 us  [across(): return lax.ppermute(value, ('group', 'seq'), moves)]
    ppermute x5, waiting for transfers between devices: 6.36 us -> 5.29 us  [across(): return lax.ppermute(value, ('group', 'seq'), moves)]
  transfers between devices with their start and end apart: 18 -> 18, of which waited for: 11 -> 9; matrix products, arithmetic and copies ran while one was open for 6% -> 0% of each run, Pallas kernels for 17% -> 23%
where the time goes in v5:
time: 88.5 us; the launch traced here: 87.8 us
  Pallas kernels  32 us (36%)
  starting transfers between devices  26.6 us (30%)
  waiting for transfers between devices  26.6 us (30%)
  local copies, waits for them, and re-layouts  1.86 us (2%)
    ppermute x4, waiting for transfers between devices, swap(): return lax.ppermute(value, 'group', [(g, g ^ bits) for g in range(groups)])  12.9 us
    ppermute x9, starting transfers between devices, gathered(): lax.ppermute(value, 'seq', [(i, i ^ k) for i in range(count)])  11.8 us
    pallas_call x2, Pallas kernels, attend_rest(): pl.pallas_call(attend_rest_kernel, out_shape=jax.ShapeDtypeStruct((2 * sh...  10 us
    ppermute x5, starting transfers between devices, across(): return lax.ppermute(value, ('group', 'seq'), moves)  9.57 us
    ppermute x9, waiting for transfers between devices, gathered(): lax.ppermute(value, 'seq', [(i, i ^ k) for i in range(count)])  8.44 us
    pallas_call x1, Pallas kernels, body(): pl.pallas_call(functools.partial(finish_kernel, count, shares, list(high)...  6.57 us
    pallas_call x2, Pallas kernels, attend_own(): pl.pallas_call(functools.partial(attend_own_kernel, count, window, own_wi...  6.35 us
    ppermute x5, waiting for transfers between devices, across(): return lax.ppermute(value, ('group', 'seq'), moves)  5.29 us
  transfers between devices with their start and end apart: 18, of which 9 were waited for; matrix products, arithmetic and copies ran while one was open for 0% of the time, Pallas kernels for 23%

profile of v5, /device:TPU:1, one launch (start us, length us, event | category | flops | bytes accessed | tf_op | source)
XLA Modules:
  0.0 87.8 jit_solution(1199001906928461814)
XLA Ops:
  0.0 4.1 %fold_back.1 = (bf16[256,1664]{1,0:T(8,128)(2,1)}, bf16[32,1664]{1,0:T(8,128)(2,1)}) custom-call(bf16[64,1536]{1,0:T(8,128)(2,1)} %in_hbm.3, f32[1536]{0:T(1024)} %gain_hbm.3, bf16[3,1536,256]{2,1,0:T(8,128)(2,1)} %qkv_hbm.3, bf16[256,1536]{1,0:T(8,128)(2,1)} %out_hbm.1, f32[1536]{0:T(1024)} %final_hbm.3, bf16[64,1536]{1,0:T(8,128)(2,1)} %bitcast.20), custom_call_target="tpu_custom_call" | custom-call | flops 393216000 | bytes 1966080 | tf_op jit(solution)/shard_map/fold_back/pallas_call | solution.py:357
  4.1 4.2 %collective-permute-start.9 = (bf16[32,1664]{1,0:T(8,128)(2,1)}, bf16[32,1664]{1,0:T(8,128)(2,1)S(1)}, u32[]{:S(2)}, u32[]{:S(2)}) collective-permute-start(bf16[32,1664]{1,0:T(8,128)(2,1)} %get-tuple-element.37), channel_id=1, source_target_pairs={{0,3},{1,2},{2,1},{3,0},{4,7},{5,6},{6,5},{7,4},{8,11},{9,10},{10,... | collective-permute-start | bytes 319496 | tf_op jit(solution)/shard_map/ppermute | solution.py:346
  8.3 0.4 collective-permute-start.7
  8.7 2.6 %collective-permute-done.9 = bf16[32,1664]{1,0:T(8,128)(2,1)S(1)} collective-permute-done((bf16[32,1664]{1,0:T(8,128)(2,1)}, bf16[32,1664]{1,0:T(8,128)(2,1)S(1)}, u32[]{:S(2)}, u32[]{:S(2)}) %collective-permute-start.9) | collective-permute-done | bytes 106528 | tf_op jit(solution)/shard_map/ppermute | solution.py:346
  11.3 5.9 %collective-permute-done.8 = bf16[32,1664]{1,0:T(8,128)(2,1)S(1)} collective-permute-done((bf16[32,1664]{1,0:T(8,128)(2,1)}, bf16[32,1664]{1,0:T(8,128)(2,1)S(1)}, u32[]{:S(2)}, u32[]{:S(2)}) %collective-permute-start.8) | collective-permute-done | bytes 106528 | tf_op jit(solution)/shard_map/ppermute | solution.py:346
  17.1 0.1 fusion
  17.2 1.3 %collective-permute-start.11 = (bf16[3,32,1664]{2,1,0:T(8,128)(2,1)S(1)}, bf16[3,32,1664]{2,1,0:T(8,128)(2,1)S(1)}, u32[]{:S(2)}, u32[]{:S(2)}) collective-permute-start(bf16[3,32,1664]{2,1,0:T(8,128)(2,1)S(1)} %get-tuple-element.42), channel_id=1, source_target_pairs={{0,16},{4,20},{8,24},{12,28},{16,0},{20,4},{24,8},{28,12},{1,17},{... | collective-permute-start | bytes 958472 | tf_op jit(solution)/shard_map/ppermute | solution.py:343
  18.5 1.2 %collective-permute-start.10 = (bf16[3,32,1664]{2,1,0:T(8,128)(2,1)S(1)}, bf16[3,32,1664]{2,1,0:T(8,128)(2,1)S(1)}, u32[]{:S(2)}, u32[]{:S(2)}) collective-permute-start(bf16[3,32,1664]{2,1,0:T(8,128)(2,1)S(1)} %get-tuple-element.42), channel_id=1, source_target_pairs={{0,8},{4,12},{8,0},{12,4},{16,24},{20,28},{24,16},{28,20},{1,9},{5... | collective-permute-start | bytes 958472 | tf_op jit(solution)/shard_map/ppermute | solution.py:343
  19.7 0.2 collective-permute-start.12
  19.9 5.1 %collective-permute-done.11 = bf16[3,32,1664]{2,1,0:T(8,128)(2,1)S(1)} collective-permute-done((bf16[3,32,1664]{2,1,0:T(8,128)(2,1)S(1)}, bf16[3,32,1664]{2,1,0:T(8,128)(2,1)S(1)}, u32[]{:S(2)}, u32[]{:S(2)}) %collective-permute-start.11) | collective-permute-done | bytes 319520 | tf_op jit(solution)/shard_map/ppermute | solution.py:343
  25.0 1.0 %collective-permute-done.10 = bf16[3,32,1664]{2,1,0:T(8,128)(2,1)S(1)} collective-permute-done((bf16[3,32,1664]{2,1,0:T(8,128)(2,1)S(1)}, bf16[3,32,1664]{2,1,0:T(8,128)(2,1)S(1)}, u32[]{:S(2)}, u32[]{:S(2)}) %collective-permute-start.10) | collective-permute-done | bytes 319520 | tf_op jit(solution)/shard_map/ppermute | solution.py:343
  26.0 6.8 %collective-permute-done.12 = bf16[3,32,1664]{2,1,0:T(8,128)(2,1)S(1)} collective-permute-done((bf16[3,32,1664]{2,1,0:T(8,128)(2,1)S(1)}, bf16[3,32,1664]{2,1,0:T(8,128)(2,1)S(1)}, u32[]{:S(2)}, u32[]{:S(2)}) %collective-permute-start.12) | collective-permute-done | bytes 319520 | tf_op jit(solution)/shard_map/ppermute | solution.py:343
  32.7 0.2 pad_maximum_fusion.refs_6_
  32.9 2.5 %collective-permute-start.13 = (bf16[4,3,32,1664]{3,2,1,0:T(8,128)(2,1)S(1)}, bf16[4,3,32,1664]{3,2,1,0:T(8,128)(2,1)}, u32[]{:S(2)}, u32[]{:S(2)}) collective-permute-start(bf16[4,3,32,1664]{3,2,1,0:T(8,128)(2,1)S(1)} %pad_maximum_fusion.refs_6_), channel_id=1, source_target_pairs={{0,4},{4,0},{8,12},{12,8},{16,20},{20,16},{24,28},{28,24},{1,5},{5... | collective-permute-start | bytes 3833864 | tf_op jit(solution)/shard_map/ppermute | solution.py:343
  35.5 0.1 copy.11
  35.6 0.1 copy.12
  35.7 0.1 pad_maximum_fusion.3.refs_0_
  35.9 0.0 copy-start.1
  35.9 1.8 %collective-permute-start.2 = (bf16[256,128]{1,0:T(8,128)(2,1)S(1)}, bf16[256,128]{1,0:T(8,128)(2,1)S(1)}, u32[]{:S(2)}, u32[]{:S(2)}) collective-permute-start(bf16[256,128]{1,0:T(8,128)(2,1)S(1)} %pad_maximum_fusion.3.refs_0_), channel_id=1, source_target_pairs={{0,3},{1,2},{2,1},{3,0},{4,7},{5,6},{6,5},{7,4},{8,11},{9,10},{10,... | collective-permute-start | bytes 196616 | tf_op jit(solution)/shard_map/ppermute | solution.py:346
  37.7 1.8 %collective-permute-start = (bf16[256,128]{1,0:T(8,128)(2,1)S(1)}, bf16[256,128]{1,0:T(8,128)(2,1)S(1)}, u32[]{:S(2)}, u32[]{:S(2)}) collective-permute-start(bf16[256,128]{1,0:T(8,128)(2,1)S(1)} %pad_maximum_fusion.3.refs_0_), channel_id=1, source_target_pairs={{0,1},{1,0},{2,3},{3,2},{4,5},{5,4},{6,7},{7,6},{8,9},{9,8},{10,11... | collective-permute-start | bytes 196616 | tf_op jit(solution)/shard_map/ppermute | solution.py:346
  39.5 3.5 %fold_maps.1 = (bf16[256,128]{1,0:T(8,128)(2,1)}, bf16[128,1664]{1,0:T(8,128)(2,1)}, bf16[64,256]{1,0:T(8,128)(2,1)}) custom-call(bf16[64,1536]{1,0:T(8,128)(2,1)} %in_hbm.3, f32[1536]{0:T(1024)} %gain_hbm.3, bf16[3,1536,256]{2,1,0:T(8,128)(2,1)} %qkv_hbm.3, f32[1536]{0:T(1024)} %final_hbm.3, bf16[64,1536]{1,0:T(8,128)(2,1)} %bitcast.21), custom_call_target="tpu_custom_call" | custom-call | flops 235929600 | bytes 1966080 | tf_op jit(solution)/shard_map/fold_maps/pallas_call | solution.py:371
  43.0 1.8 %collective-permute-start.5 = (bf16[256,128]{1,0:T(8,128)(2,1)}, bf16[256,128]{1,0:T(8,128)(2,1)S(1)}, u32[]{:S(2)}, u32[]{:S(2)}) collective-permute-start(bf16[256,128]{1,0:T(8,128)(2,1)} %get-tuple-element.23.refs_4_), channel_id=1, source_target_pairs={{0,3},{1,2},{2,1},{3,0},{4,7},{5,6},{6,5},{7,4},{8,11},{9,10},{10,... | collective-permute-start | bytes 196616 | tf_op jit(solution)/shard_map/ppermute | solution.py:346
  44.8 0.0 collective-permute-done.2.refs_3_
  44.8 0.0 collective-permute-start.4
  44.8 0.0 collective-permute-done.1.refs_2_
  44.8 1.8 %collective-permute-start.3 = (bf16[256,128]{1,0:T(8,128)(2,1)}, bf16[256,128]{1,0:T(8,128)(2,1)S(1)}, u32[]{:S(2)}, u32[]{:S(2)}) collective-permute-start(bf16[256,128]{1,0:T(8,128)(2,1)} %get-tuple-element.23.refs_4_), channel_id=1, source_target_pairs={{0,1},{1,0},{2,3},{3,2},{4,5},{5,4},{6,7},{7,6},{8,9},{9,8},{10,11... | collective-permute-start | bytes 196616 | tf_op jit(solution)/shard_map/ppermute | solution.py:346
  46.6 0.1 pad_maximum_fusion.2
  46.7 4.4 %collective-permute-start.6 = (bf16[4,256,128]{2,1,0:T(8,128)(2,1)S(1)}, bf16[4,256,128]{2,1,0:T(8,128)(2,1)S(1)}, u32[]{:S(2)}, u32[]{:S(2)}) collective-permute-start(bf16[4,256,128]{2,1,0:T(8,128)(2,1)S(1)} %pad_maximum_fusion.2), channel_id=1, source_target_pairs={{4,0},{5,1},{6,2},{7,3},{8,4},{9,5},{10,6},{11,7},{12,8},{13,9},{1... | collective-permute-start | bytes 786440 | tf_op jit(solution)/shard_map/ppermute | solution.py:340
  51.1 0.0 copy-start.4
  51.1 0.8 copy-done.4
  52.0 0.8 copy-done.6
  52.7 3.2 %attend_own.2 = (bf16[512,384]{1,0:T(8,128)(2,1)S(1)}, bf16[1024,128]{1,0:T(8,128)(2,1)S(1)}, bf16[256,128]{1,0:T(8,128)(2,1)S(1)}, bf16[1024,256]{1,0:T(8,128)(2,1)S(1)}, f32[8,1024]{1,0:T(8,128)S(1)}) custom-call(s32[15]{0:T(128)S(1)} %copy-done.1, bf16[256,128]{1,0:T(8,128)(2,1)S(1)} %pad_maximum_fusion.3.refs_0_, ...), custom_call_target="tpu_custom_call" | custom-call | flops 1073741824 | bytes 262144 | tf_op jit(solution)/shard_map/attend_own/pallas_call | solution.py:406
  55.9 0.0 collective-permute-done.5.refs_2_
  55.9 0.0 collective-permute-done.4.refs_1_
  55.9 0.0 copy-start.5
  56.0 4.9 %attend_rest.2.refs_1_ = bf16[512,768]{1,0:T(8,128)(2,1)S(1)} custom-call(bf16[64,256]{1,0:T(8,128)(2,1)S(1)} %copy-done.7, bf16[1024,128]{1,0:T(8,128)(2,1)S(1)} %get-tuple-element.26.right_ref, bf16[256,128]{1,0:T(8,128)(2,1)S(1)} %get-tuple-element.27.mine_ref, bf16[1024,256]{1,0:T(8,128)(2,1)S(1)} %get-tuple-element.28.ext_ref, ...), custom_call_target="tpu_custom_call" | custom-call | flops 3221225472 | bytes 786432 | tf_op jit(solution)/shard_map/attend_rest/pallas_call | solution.py:429
  60.9 3.2 %attend_own.3 = (bf16[512,384]{1,0:T(8,128)(2,1)S(1)}, bf16[1024,128]{1,0:T(8,128)(2,1)S(1)}, bf16[256,128]{1,0:T(8,128)(2,1)S(1)}, bf16[1024,256]{1,0:T(8,128)(2,1)S(1)}, f32[8,1024]{1,0:T(8,128)S(1)}) custom-call(s32[15]{0:T(128)S(1)} %copy-done.1, bf16[256,128]{1,0:T(8,128)(2,1)S(1)} %pad_maximum_fusion.3.refs_0_, ...), custom_call_target="tpu_custom_call" | custom-call | flops 1073741824 | bytes 262144 | tf_op jit(solution)/shard_map/attend_own/pallas_call | solution.py:406
  64.1 5.1 %attend_rest.3.refs_3_ = bf16[512,768]{1,0:T(8,128)(2,1)S(1)} custom-call(bf16[64,256]{1,0:T(8,128)(2,1)S(1)} %copy-done.7, bf16[1024,128]{1,0:T(8,128)(2,1)S(1)} %get-tuple-element.31.right_ref, bf16[256,128]{1,0:T(8,128)(2,1)S(1)} %get-tuple-element.32.mine_ref, bf16[1024,256]{1,0:T(8,128)(2,1)S(1)} %get-tuple-element.33.ext_ref, ...), custom_call_target="tpu_custom_call" | custom-call | flops 3221225472 | bytes 786432 | tf_op jit(solution)/shard_map/attend_rest/pallas_call | solution.py:429
  69.2 6.6 %finish.1 = (f32[2,256,128]{2,1,0:T(8,128)S(1)}, bf16[128,128]{1,0:T(8,128)(2,1)S(1)}, bf16[128,128]{1,0:T(8,128)(2,1)S(1)}) custom-call(s32[15]{0:T(128)S(1)} %copy-done.1, bf16[512,384]{1,0:T(8,128)(2,1)S(1)} %get-tuple-element.25.refs_0_, bf16[512,768]{1,0:T(8,128)(2,1)S(1)} %attend_rest.2.refs_1_, bf16[512,384]{1,0:T(8,128)(2,1)S(1)} %get-tuple-element.30.refs_2_, ...), custom_call_target="tpu_custom_call" | custom-call | flops 3221225472 | bytes 3145728 | tf_op jit(solution)/shard_map/finish/pallas_call | solution.py:447
  75.8 1.3 %collective-permute-start.15 = (bf16[128,128]{1,0:T(8,128)(2,1)S(1)}, bf16[128,128]{1,0:T(8,128)(2,1)S(1)}, u32[]{:S(2)}, u32[]{:S(2)}) collective-permute-start(bf16[128,128]{1,0:T(8,128)(2,1)S(1)} %get-tuple-element.39), channel_id=1, source_target_pairs={{3,4},{7,8},{11,12},{15,16},{19,20},{23,24},{27,28}} | collective-permute-start | bytes 98312 | tf_op jit(solution)/shard_map/ppermute | solution.py:340
  77.1 1.3 %collective-permute-start.14 = (bf16[128,128]{1,0:T(8,128)(2,1)S(1)}, bf16[128,128]{1,0:T(8,128)(2,1)S(1)}, u32[]{:S(2)}, u32[]{:S(2)}) collective-permute-start(bf16[128,128]{1,0:T(8,128)(2,1)S(1)} %get-tuple-element.39), channel_id=1, source_target_pairs={{2,4},{3,5},{6,8},{7,9},{10,12},{11,13},{14,16},{15,17},{18,20},{1... | collective-permute-start | bytes 98312 | tf_op jit(solution)/shard_map/ppermute | solution.py:340
  78.4 1.3 %collective-permute-start.17 = (bf16[128,128]{1,0:T(8,128)(2,1)S(1)}, bf16[128,128]{1,0:T(8,128)(2,1)S(1)}, u32[]{:S(2)}, u32[]{:S(2)}) collective-permute-start(bf16[128,128]{1,0:T(8,128)(2,1)S(1)} %get-tuple-element.40), channel_id=1, source_target_pairs={{3,0},{7,4},{11,8},{15,12},{19,16},{23,20},{27,24},{31,28}} | collective-permute-start | bytes 98312 | tf_op jit(solution)/shard_map/ppermute | solution.py:340
  79.7 1.3 %collective-permute-start.16 = (bf16[128,128]{1,0:T(8,128)(2,1)S(1)}, bf16[128,128]{1,0:T(8,128)(2,1)S(1)}, u32[]{:S(2)}, u32[]{:S(2)}) collective-permute-start(bf16[128,128]{1,0:T(8,128)(2,1)S(1)} %get-tuple-element.40), channel_id=1, source_target_pairs={{2,0},{3,1},{6,4},{7,5},{10,8},{11,9},{14,12},{15,13},{18,16},{19,... | collective-permute-start | bytes 98312 | tf_op jit(solution)/shard_map/ppermute | solution.py:340
  81.0 1.9 %collective-permute-done.15.refs_1_ = bf16[128,128]{1,0:T(8,128)(2,1)S(1)} collective-permute-done((bf16[128,128]{1,0:T(8,128)(2,1)S(1)}, bf16[128,128]{1,0:T(8,128)(2,1)S(1)}, u32[]{:S(2)}, u32[]{:S(2)}) %collective-permute-start.15) | collective-permute-done | bytes 32800 | tf_op jit(solution)/shard_map/ppermute | solution.py:340
  82.9 1.0 %collective-permute-done.14.refs_0_ = bf16[128,128]{1,0:T(8,128)(2,1)S(1)} collective-permute-done((bf16[128,128]{1,0:T(8,128)(2,1)S(1)}, bf16[128,128]{1,0:T(8,128)(2,1)S(1)}, u32[]{:S(2)}, u32[]{:S(2)}) %collective-permute-start.14) | collective-permute-done | bytes 32800 | tf_op jit(solution)/shard_map/ppermute | solution.py:340
  83.9 2.0 %collective-permute-done.17.refs_3_ = bf16[128,128]{1,0:T(8,128)(2,1)S(1)} collective-permute-done((bf16[128,128]{1,0:T(8,128)(2,1)S(1)}, bf16[128,128]{1,0:T(8,128)(2,1)S(1)}, u32[]{:S(2)}, u32[]{:S(2)}) %collective-permute-start.17) | collective-permute-done | bytes 32800 | tf_op jit(solution)/shard_map/ppermute | solution.py:340
  85.9 0.4 collective-permute-done.16.refs_2_
  86.3 1.5 %combine.1 = f32[2,64,256]{2,1,0:T(8,128)} custom-call(s32[15]{0:T(128)S(1)} %copy-done.1, f32[2,64,256]{2,1,0:T(8,128)S(1)} %bitcast.16, f32[2,256,128]{2,1,0:T(8,128)S(1)} %get-tuple-element.38.rows_ref, bf16[128,128]{1,0:T(8,128)(2,1)S(1)} %collective-permute-done.14.refs_0_, bf16[128,128]{1,0:T(8,128)(2,1)S(1)} %collective-permute-done.15.refs_1_, ...), custom_call_target="tpu_custom_call" | custom-call | tf_op jit(solution)/shard_map/combine/pallas_call | solution.py:471
  (19 shorter events, 0.0 us)
Async XLA Ops:
  4.1 7.1 %collective-permute-start.9 = (bf16[32,1664]{1,0:T(8,128)(2,1)}, bf16[32,1664]{1,0:T(8,128)(2,1)S(1)}, u32[]{:S(2)}, u32[]{:S(2)}) collective-permute-start(bf16[32,1664]{1,0:T(8,128)(2,1)} %get-tuple-element.37), channel_id=1, source_target_pairs={{0,3},{1,2},{2,1},{3,0},{4,7},{5,6},{6,5},{7,4},{8,11},{9,10},{10,... | collective-permute-start | bytes 319496 | tf_op jit(solution)/shard_map/ppermute | solution.py:346
  8.3 8.8 %collective-permute-start.8 = (bf16[32,1664]{1,0:T(8,128)(2,1)}, bf16[32,1664]{1,0:T(8,128)(2,1)S(1)}, u32[]{:S(2)}, u32[]{:S(2)}) collective-permute-start(bf16[32,1664]{1,0:T(8,128)(2,1)} %get-tuple-element.37), channel_id=1, source_target_pairs={{0,2},{1,3},{2,0},{3,1},{4,6},{5,7},{6,4},{7,5},{8,10},{9,11},{10,... | collective-permute-start | bytes 319496 | tf_op jit(solution)/shard_map/ppermute | solution.py:346
  8.3 8.8 %collective-permute-start.7 = (bf16[32,1664]{1,0:T(8,128)(2,1)}, bf16[32,1664]{1,0:T(8,128)(2,1)S(1)}, u32[]{:S(2)}, u32[]{:S(2)}) collective-permute-start(bf16[32,1664]{1,0:T(8,128)(2,1)} %get-tuple-element.37), channel_id=1, source_target_pairs={{0,1},{1,0},{2,3},{3,2},{4,5},{5,4},{6,7},{7,6},{8,9},{9,8},{10,11... | collective-permute-start | bytes 319496 | tf_op jit(solution)/shard_map/ppermute | solution.py:346
  17.2 7.8 %collective-permute-start.11 = (bf16[3,32,1664]{2,1,0:T(8,128)(2,1)S(1)}, bf16[3,32,1664]{2,1,0:T(8,128)(2,1)S(1)}, u32[]{:S(2)}, u32[]{:S(2)}) collective-permute-start(bf16[3,32,1664]{2,1,0:T(8,128)(2,1)S(1)} %get-tuple-element.42), channel_id=1, source_target_pairs={{0,16},{4,20},{8,24},{12,28},{16,0},{20,4},{24,8},{28,12},{1,17},{... | collective-permute-start | bytes 958472 | tf_op jit(solution)/shard_map/ppermute | solution.py:343
  18.5 7.5 %collective-permute-start.10 = (bf16[3,32,1664]{2,1,0:T(8,128)(2,1)S(1)}, bf16[3,32,1664]{2,1,0:T(8,128)(2,1)S(1)}, u32[]{:S(2)}, u32[]{:S(2)}) collective-permute-start(bf16[3,32,1664]{2,1,0:T(8,128)(2,1)S(1)} %get-tuple-element.42), channel_id=1, source_target_pairs={{0,8},{4,12},{8,0},{12,4},{16,24},{20,28},{24,16},{28,20},{1,9},{5... | collective-permute-start | bytes 958472 | tf_op jit(solution)/shard_map/ppermute | solution.py:343
  19.7 13.0 %collective-permute-start.12 = (bf16[3,32,1664]{2,1,0:T(8,128)(2,1)S(1)}, bf16[3,32,1664]{2,1,0:T(8,128)(2,1)S(1)}, u32[]{:S(2)}, u32[]{:S(2)}) collective-permute-start(bf16[3,32,1664]{2,1,0:T(8,128)(2,1)S(1)} %get-tuple-element.42), channel_id=1, source_target_pairs={{0,24},{4,28},{8,16},{12,20},{16,8},{20,12},{24,0},{28,4},{1,25},{... | collective-permute-start | bytes 958472 | tf_op jit(solution)/shard_map/ppermute | solution.py:343
  32.7 2.7 %copy-start = (f32[2,256,64]{1,2,0:T(8,128)S(1)}, f32[2,256,64]{1,2,0:T(8,128)}, u32[]{:S(2)}) copy-start(f32[2,256,64]{1,2,0:T(8,128)} %param.8) | copy-start | bytes 393220
  32.9 36.3 %collective-permute-start.13 = (bf16[4,3,32,1664]{3,2,1,0:T(8,128)(2,1)S(1)}, bf16[4,3,32,1664]{3,2,1,0:T(8,128)(2,1)}, u32[]{:S(2)}, u32[]{:S(2)}) collective-permute-start(bf16[4,3,32,1664]{3,2,1,0:T(8,128)(2,1)S(1)} %pad_maximum_fusion.refs_6_), channel_id=1, source_target_pairs={{0,4},{4,0},{8,12},{12,8},{16,20},{20,16},{24,28},{28,24},{1,5},{5... | collective-permute-start | bytes 3833864 | tf_op jit(solution)/shard_map/ppermute | solution.py:343
  35.9 15.3 %copy-start.1 = (s32[15]{0:T(128)S(1)}, s32[15]{0:T(128)}, u32[]{:S(2)}) copy-start(s32[15]{0:T(128)} %margin_ref.7) | copy-start | bytes 184
  35.9 8.9 %collective-permute-start.2 = (bf16[256,128]{1,0:T(8,128)(2,1)S(1)}, bf16[256,128]{1,0:T(8,128)(2,1)S(1)}, u32[]{:S(2)}, u32[]{:S(2)}) collective-permute-start(bf16[256,128]{1,0:T(8,128)(2,1)S(1)} %pad_maximum_fusion.3.refs_0_), channel_id=1, source_target_pairs={{0,3},{1,2},{2,1},{3,0},{4,7},{5,6},{6,5},{7,4},{8,11},{9,10},{10,... | collective-permute-start | bytes 196616 | tf_op jit(solution)/shard_map/ppermute | solution.py:346
  37.7 7.1 %collective-permute-start.1 = (bf16[256,128]{1,0:T(8,128)(2,1)S(1)}, bf16[256,128]{1,0:T(8,128)(2,1)S(1)}, u32[]{:S(2)}, u32[]{:S(2)}) collective-permute-start(bf16[256,128]{1,0:T(8,128)(2,1)S(1)} %pad_maximum_fusion.3.refs_0_), channel_id=1, source_target_pairs={{0,2},{1,3},{2,0},{3,1},{4,6},{5,7},{6,4},{7,5},{8,10},{9,11},{10,... | collective-permute-start | bytes 196616 | tf_op jit(solution)/shard_map/ppermute | solution.py:346
  37.7 8.9 %collective-permute-start = (bf16[256,128]{1,0:T(8,128)(2,1)S(1)}, bf16[256,128]{1,0:T(8,128)(2,1)S(1)}, u32[]{:S(2)}, u32[]{:S(2)}) collective-permute-start(bf16[256,128]{1,0:T(8,128)(2,1)S(1)} %pad_maximum_fusion.3.refs_0_), channel_id=1, source_target_pairs={{0,1},{1,0},{2,3},{3,2},{4,5},{5,4},{6,7},{7,6},{8,9},{9,8},{10,11... | collective-permute-start | bytes 196616 | tf_op jit(solution)/shard_map/ppermute | solution.py:346
  43.0 12.9 %collective-permute-start.5 = (bf16[256,128]{1,0:T(8,128)(2,1)}, bf16[256,128]{1,0:T(8,128)(2,1)S(1)}, u32[]{:S(2)}, u32[]{:S(2)}) collective-permute-start(bf16[256,128]{1,0:T(8,128)(2,1)} %get-tuple-element.23.refs_4_), channel_id=1, source_target_pairs={{0,3},{1,2},{2,1},{3,0},{4,7},{5,6},{6,5},{7,4},{8,11},{9,10},{10,... | collective-permute-start | bytes 196616 | tf_op jit(solution)/shard_map/ppermute | solution.py:346
  44.8 11.1 %collective-permute-start.4 = (bf16[256,128]{1,0:T(8,128)(2,1)}, bf16[256,128]{1,0:T(8,128)(2,1)S(1)}, u32[]{:S(2)}, u32[]{:S(2)}) collective-permute-start(bf16[256,128]{1,0:T(8,128)(2,1)} %get-tuple-element.23.refs_4_), channel_id=1, source_target_pairs={{0,2},{1,3},{2,0},{3,1},{4,6},{5,7},{6,4},{7,5},{8,10},{9,11},{10,... | collective-permute-start | bytes 196616 | tf_op jit(solution)/shard_map/ppermute | solution.py:346
  44.8 11.1 %collective-permute-start.3 = (bf16[256,128]{1,0:T(8,128)(2,1)}, bf16[256,128]{1,0:T(8,128)(2,1)S(1)}, u32[]{:S(2)}, u32[]{:S(2)}) collective-permute-start(bf16[256,128]{1,0:T(8,128)(2,1)} %get-tuple-element.23.refs_4_), channel_id=1, source_target_pairs={{0,1},{1,0},{2,3},{3,2},{4,5},{5,4},{6,7},{7,6},{8,9},{9,8},{10,11... | collective-permute-start | bytes 196616 | tf_op jit(solution)/shard_map/ppermute | solution.py:346
  46.7 14.2 %collective-permute-start.6 = (bf16[4,256,128]{2,1,0:T(8,128)(2,1)S(1)}, bf16[4,256,128]{2,1,0:T(8,128)(2,1)S(1)}, u32[]{:S(2)}, u32[]{:S(2)}) collective-permute-start(bf16[4,256,128]{2,1,0:T(8,128)(2,1)S(1)} %pad_maximum_fusion.2), channel_id=1, source_target_pairs={{4,0},{5,1},{6,2},{7,3},{8,4},{9,5},{10,6},{11,7},{12,8},{13,9},{1... | collective-permute-start | bytes 786440 | tf_op jit(solution)/shard_map/ppermute | solution.py:340
  51.1 0.8 copy-start.4
  52.0 0.8 copy-start.6
  52.7 3.2 %copy-start.7 = (bf16[64,256]{1,0:T(8,128)(2,1)S(1)}, bf16[64,256]{1,0:T(8,128)(2,1)}, u32[]{:S(2)}) copy-start(bf16[64,256]{1,0:T(8,128)(2,1)} %get-tuple-element.24.refs_5_.gram_ref) | copy-start | bytes 98308
  55.9 4.9 %copy-start.5 = (bf16[256,128]{1,0:T(8,128)(2,1)S(1)}, bf16[256,128]{1,0:T(8,128)(2,1)}, u32[]{:S(2)}) copy-start(bf16[256,128]{1,0:T(8,128)(2,1)} %get-tuple-element.23.refs_4_) | copy-start | bytes 196612
  64.1 5.2 %copy-start.2 = (bf16[256,1664]{1,0:T(8,128)(2,1)S(1)}, bf16[256,1664]{1,0:T(8,128)(2,1)}, u32[]{:S(2)}) copy-start(bf16[256,1664]{1,0:T(8,128)(2,1)} %get-tuple-element.36.refs_5_) | copy-start | bytes 2555908
  64.1 5.2 %copy-start.3 = (bf16[128,1664]{1,0:T(8,128)(2,1)S(1)}, bf16[128,1664]{1,0:T(8,128)(2,1)}, u32[]{:S(2)}) copy-start(bf16[128,1664]{1,0:T(8,128)(2,1)} %get-tuple-element.35.refs_4_) | copy-start | bytes 1277956
  75.8 7.1 %collective-permute-start.15 = (bf16[128,128]{1,0:T(8,128)(2,1)S(1)}, bf16[128,128]{1,0:T(8,128)(2,1)S(1)}, u32[]{:S(2)}, u32[]{:S(2)}) collective-permute-start(bf16[128,128]{1,0:T(8,128)(2,1)S(1)} %get-tuple-element.39), channel_id=1, source_target_pairs={{3,4},{7,8},{11,12},{15,16},{19,20},{23,24},{27,28}} | collective-permute-start | bytes 98312 | tf_op jit(solution)/shard_map/ppermute | solution.py:340
  77.1 6.8 %collective-permute-start.14 = (bf16[128,128]{1,0:T(8,128)(2,1)S(1)}, bf16[128,128]{1,0:T(8,128)(2,1)S(1)}, u32[]{:S(2)}, u32[]{:S(2)}) collective-permute-start(bf16[128,128]{1,0:T(8,128)(2,1)S(1)} %get-tuple-element.39), channel_id=1, source_target_pairs={{2,4},{3,5},{6,8},{7,9},{10,12},{11,13},{14,16},{15,17},{18,20},{1... | collective-permute-start | bytes 98312 | tf_op jit(solution)/shard_map/ppermute | solution.py:340
  78.4 7.5 %collective-permute-start.17 = (bf16[128,128]{1,0:T(8,128)(2,1)S(1)}, bf16[128,128]{1,0:T(8,128)(2,1)S(1)}, u32[]{:S(2)}, u32[]{:S(2)}) collective-permute-start(bf16[128,128]{1,0:T(8,128)(2,1)S(1)} %get-tuple-element.40), channel_id=1, source_target_pairs={{3,0},{7,4},{11,8},{15,12},{19,16},{23,20},{27,24},{31,28}} | collective-permute-start | bytes 98312 | tf_op jit(solution)/shard_map/ppermute | solution.py:340
  79.7 6.6 %collective-permute-start.16 = (bf16[128,128]{1,0:T(8,128)(2,1)S(1)}, bf16[128,128]{1,0:T(8,128)(2,1)S(1)}, u32[]{:S(2)}, u32[]{:S(2)}) collective-permute-start(bf16[128,128]{1,0:T(8,128)(2,1)S(1)} %get-tuple-element.40), channel_id=1, source_target_pairs={{2,0},{3,1},{6,4},{7,5},{10,8},{11,9},{14,12},{15,13},{18,16},{19,... | collective-permute-start | bytes 98312 | tf_op jit(solution)/shard_map/ppermute | solution.py:340

commit v6 on v5

--- a/solution.py
+++ b/solution.py
@@ -71,42 +71,17 @@
     return weight - jnp.mean(weight, axis=-1, keepdims=True)
 
 
-def fold_back_kernel(shares, in_hbm, gain_hbm, qkv_hbm, out_hbm, final_hbm, head_hbm, *refs):
-    back_ref, part_ref, in_ref, gain_ref, value_ref, out_ref, final_ref, head_ref, sem = refs
-    pairs = [(in_hbm, in_ref), (gain_hbm, gain_ref), (qkv_hbm.at[2], value_ref), (out_hbm, out_ref)]
+def fold_kernel(shares, in_hbm, gain_hbm, qkv_hbm, out_hbm, final_hbm, head_hbm, *refs):
+    map_ref, back_ref, part_ref, direct_ref, gram_ref = refs[:5]
+    in_ref, gain_ref, qkv_ref, out_ref, final_ref, head_ref, sem = refs[5:]
+    pairs = [(in_hbm, in_ref), (gain_hbm, gain_ref), (qkv_hbm.at[2], qkv_ref.at[2]), (out_hbm, out_ref)]
+    pairs += [(qkv_hbm.at[0], qkv_ref.at[0]), (qkv_hbm.at[1], qkv_ref.at[1])]
     copies = started(pairs + [(final_hbm, final_ref), (head_hbm, head_ref)], sem)
     copies[0].wait()
     copies[1].wait()
     centered = centered_rows(in_ref)
     channels, depth = centered.shape
     width = out_ref.shape[0]
-    both = jnp.concatenate(split(centered * gain_ref[...][None, :]), axis=0)
-    copies[2].wait()
-    values = folded(both, value_ref[...], channels)
-    copies[3].wait()
-    tiled = jnp.concatenate([values] * (width // HDIM), axis=0)
-    same = iota((width, width), 0) // channels == iota((width, width), 1) // HDIM
-    high, low = split(jnp.where(same, tiled, 0.0))
-    back = matmul(high, out_ref[...]) + matmul(low, out_ref[...])
-    back = back - jnp.mean(back, axis=-1, keepdims=True)
-    back_ref[:, :depth] = back.astype(BF16)
-    copies[4].wait()
-    copies[5].wait()
-    scores = matmul_nt(jnp.concatenate(split(back * final_ref[...][None, :]), axis=0), head_ref[...])
-    back_ref[:, depth:] = halves(scores[:width] + scores[width:])
-    rows = width // shares
-    sub = lax.rem(lax.axis_index("group"), shares)
-    part_ref[...] = back_ref[pl.ds(pl.multiple_of(sub * rows, rows), rows), :]
-
-
-def fold_maps_kernel(in_hbm, gain_hbm, qkv_hbm, final_hbm, head_hbm, *refs):
-    map_ref, direct_ref, gram_ref, in_ref, gain_ref, query_ref, key_ref, final_ref, head_ref, sem = refs
-    pairs = [(in_hbm, in_ref), (gain_hbm, gain_ref), (qkv_hbm.at[0], query_ref), (qkv_hbm.at[1], key_ref)]
-    copies = started(pairs + [(final_hbm, final_ref), (head_hbm, head_ref)], sem)
-    copies[0].wait()
-    copies[1].wait()
-    centered = centered_rows(in_ref)
-    channels, depth = centered.shape
     both = jnp.concatenate(split(centered * gain_ref[...][None, :]), axis=0)
 
     high, low = split(centered)
@@ -122,16 +97,30 @@
     gram_ref[:, LANES:] = jnp.where(left, third.astype(F32), 0.0).astype(BF16)
 
     copies[2].wait()
-    queries = folded(both, query_ref[...], channels)
+    values = folded(both, qkv_ref[2], channels)
+    tiled = jnp.concatenate([values] * (width // HDIM), axis=0)
+    same = iota((width, width), 0) // channels == iota((width, width), 1) // HDIM
+    high, low = split(jnp.where(same, tiled, 0.0))
     copies[3].wait()
-    keys = folded(both, key_ref[...], channels)
+    back = matmul(high, out_ref[...]) + matmul(low, out_ref[...])
+    back = back - jnp.mean(back, axis=-1, keepdims=True)
+    back_ref[:, :depth] = back.astype(BF16)
+    copies[4].wait()
+    queries = folded(both, qkv_ref[0], channels)
+    copies[5].wait()
+    keys = folded(both, qkv_ref[1], channels)
     map_ref[...] = jnp.concatenate([queries, keys], axis=0).T.astype(BF16)
 
-    copies[4].wait()
-    copies[5].wait()
-    scores = matmul_nt(jnp.concatenate(split(centered * final_ref[...][None, :]), axis=0), head_ref[...])
-    direct_ref[:channels, depth:] = halves(scores[:channels] + scores[channels:])
+    copies[6].wait()
+    copies[7].wait()
+    pieces = split(back * final_ref[...][None, :]) + split(centered * final_ref[...][None, :])
+    scores = matmul_nt(jnp.concatenate(pieces, axis=0), head_ref[...])
+    back_ref[:, depth:] = halves(scores[:width] + scores[width : 2 * width])
+    direct_ref[:channels, depth:] = halves(scores[2 * width : 2 * width + channels] + scores[2 * width + channels :])
     direct_ref[channels:, depth:] = jnp.zeros((channels, LANES), BF16)
+    rows = width // shares
+    sub = lax.rem(lax.axis_index("group"), shares)
+    part_ref[...] = back_ref[pl.ds(pl.multiple_of(sub * rows, rows), rows), :]
 
 
 def twice(tokens):
@@ -350,38 +339,31 @@
     pieces = [packed] + gathered(packed)
     stacked = jnp.stack(pieces)
     following = across(stacked, -1, [(i, i) for i in range(count)])
-    hbm = pl.BlockSpec(memory_space=pltpu.HBM)
-    small = (pltpu.VMEM(final_gain.shape, F32), pltpu.VMEM(head_out.shape[::-1], BF16), pltpu.SemaphoreType.DMA((6,)))
-    fronts = (pltpu.VMEM(in_weight.shape, BF16), pltpu.VMEM(norm_gain.shape, F32))
-    matrix = pltpu.VMEM(qkv_weight.shape[1:], BF16)
-    back, part = pl.pallas_call(
-        functools.partial(fold_back_kernel, shares),
+    maps, back, part, direct, gram = pl.pallas_call(
+        functools.partial(fold_kernel, shares),
         out_shape=(
+            jax.ShapeDtypeStruct((width, LANES), BF16),
             jax.ShapeDtypeStruct((width, depth + LANES), BF16),
             jax.ShapeDtypeStruct((width // shares, depth + LANES), BF16),
-        ),
-        in_specs=[hbm] * 6,
-        compiler_params=limit(62),
-        out_specs=(VMEM,) * 2,
-        scratch_shapes=[*fronts, matrix, pltpu.VMEM(out_weight.shape, BF16), *small],
-        cost_estimate=pl.CostEstimate(flops=width * depth * 1000, bytes_accessed=5 * width * depth, transcendentals=0),
-        name="fold_back",
-    )(in_weight, norm_gain, qkv_weight, out_weight, final_gain, head_out.T)
-    own_part = jnp.stack(gathered(part))
-    maps, direct, gram = pl.pallas_call(
-        fold_maps_kernel,
-        out_shape=(
-            jax.ShapeDtypeStruct((width, LANES), BF16),
             jax.ShapeDtypeStruct((2 * channels, depth + LANES), BF16),
             jax.ShapeDtypeStruct((channels, 2 * LANES), BF16),
         ),
-        in_specs=[hbm] * 5,
+        in_specs=[pl.BlockSpec(memory_space=pltpu.HBM)] * 6,
         compiler_params=limit(62),
-        out_specs=(VMEM,) * 3,
-        scratch_shapes=[*fronts, matrix, matrix, *small],
-        cost_estimate=pl.CostEstimate(flops=width * depth * 600, bytes_accessed=5 * width * depth, transcendentals=0),
-        name="fold_maps",
-    )(in_weight, norm_gain, qkv_weight, final_gain, head_out.T)
+        out_specs=(VMEM,) * 5,
+        scratch_shapes=[
+            pltpu.VMEM(in_weight.shape, BF16),
+            pltpu.VMEM(norm_gain.shape, F32),
+            pltpu.VMEM(qkv_weight.shape, BF16),
+            pltpu.VMEM(out_weight.shape, BF16),
+            pltpu.VMEM(final_gain.shape, F32),
+            pltpu.VMEM(head_out.shape[::-1], BF16),
+            pltpu.SemaphoreType.DMA((8,)),
+        ],
+        cost_estimate=pl.CostEstimate(flops=width * depth * 1200, bytes_accessed=8 * width * depth, transcendentals=0),
+        name="fold",
+    )(in_weight, norm_gain, qkv_weight, out_weight, final_gain, head_out.T)
+    own_part = jnp.stack(gathered(part))
     far_maps = gathered(maps)
     own_width = width // QUAD * QUAD
     rest_maps = far_maps if own_width else [maps] + far_maps

time: 88.5 us -> 86.2 us (0.974)
  waiting for transfers between devices: 26.6 us -> 30.6 us
  Pallas kernels: 32 us -> 28.9 us
  local copies, waits for them, and re-layouts: 1.86 us -> 0.26 us
  starting transfers between devices: 26.6 us -> 25.2 us
    ppermute x9, waiting for transfers between devices: 8.44 us -> 12.4 us  [gathered(): lax.ppermute(value, 'seq', [(i, i ^ k) for i in range(count)])]
    pallas_call x2 -> x1, Pallas kernels: 7.6 us -> 5.22 us  [body(): pl.pallas_call(functools.partial(fold_kernel, shares), out_shape=(jax.Sha...]
    unnamed x18 -> x14, local copies, waits for them, and re-layouts: 1.85 us -> 0.25 us
    ppermute x9, starting transfers between devices: 11.8 us -> 10.2 us  [gathered(): lax.ppermute(value, 'seq', [(i, i ^ k) for i in range(count)])]
  transfers between devices with their start and end apart: 18 -> 18, of which waited for: 9 -> 10; matrix products, arithmetic and copies ran while one was open for 0% -> 1% of each run, Pallas kernels for 23% -> 19%
where the time goes in v6:
time: 86.2 us; the launch traced here: 85.6 us
  waiting for transfers between devices  30.6 us (35%)
  Pallas kernels  28.9 us (34%)
  starting transfers between devices  25.2 us (29%)
    ppermute x4, waiting for transfers between devices, swap(): return lax.ppermute(value, 'group', [(g, g ^ bits) for g in range(groups)])  12.8 us
    ppermute x9, waiting for transfers between devices, gathered(): lax.ppermute(value, 'seq', [(i, i ^ k) for i in range(count)])  12.4 us
    ppermute x9, starting transfers between devices, gathered(): lax.ppermute(value, 'seq', [(i, i ^ k) for i in range(count)])  10.2 us
    pallas_call x2, Pallas kernels, attend_rest(): pl.pallas_call(attend_rest_kernel, out_shape=jax.ShapeDtypeStruct((2 * sh...  10 us
    ppermute x5, starting transfers between devices, across(): return lax.ppermute(value, ('group', 'seq'), moves)  9.7 us
    pallas_call x2, Pallas kernels, attend_own(): pl.pallas_call(functools.partial(attend_own_kernel, count, window, own_wi...  6.36 us
    pallas_call x1, Pallas kernels, body(): pl.pallas_call(functools.partial(finish_kernel, count, shares, list(high)...  5.82 us
    ppermute x5, waiting for transfers between devices, across(): return lax.ppermute(value, ('group', 'seq'), moves)  5.3 us
  transfers between devices with their start and end apart: 18, of which 10 were waited for; matrix products, arithmetic and copies ran while one was open for 1% of the time, Pallas kernels for 19%

profile of v6, /device:TPU:1, one launch (start us, length us, event | category | flops | bytes accessed | tf_op | source)
XLA Modules:
  0.0 85.6 jit_solution(7886329674644895830)
XLA Ops:
  0.0 5.2 %fold.1 = (bf16[256,128]{1,0:T(8,128)(2,1)}, bf16[256,1664]{1,0:T(8,128)(2,1)}, bf16[32,1664]{1,0:T(8,128)(2,1)}, bf16[128,1664]{1,0:T(8,128)(2,1)}, bf16[64,256]{1,0:T(8,128)(2,1)}) custom-call(bf16[64,1536]{1,0:T(8,128)(2,1)} %in_hbm.1, f32[1536]{0:T(1024)} %gain_hbm.1, bf16[3,1536,256]{2,1,0:T(8,128)(2,1)} %qkv_hbm.1, bf16[256,1536]{1,0:T(8,128)(2,1)} %out_hbm.1, ...), custom_call_target="tpu_custom_call" | custom-call | flops 471859200 | bytes 3145728 | tf_op jit(solution)/shard_map/fold/pallas_call | solution.py:342
  5.2 4.2 %collective-permute-start.9 = (bf16[32,1664]{1,0:T(8,128)(2,1)}, bf16[32,1664]{1,0:T(8,128)(2,1)S(1)}, u32[]{:S(2)}, u32[]{:S(2)}) collective-permute-start(bf16[32,1664]{1,0:T(8,128)(2,1)} %get-tuple-element.37), channel_id=1, source_target_pairs={{0,3},{1,2},{2,1},{3,0},{4,7},{5,6},{6,5},{7,4},{8,11},{9,10},{10,... | collective-permute-start | bytes 319496 | tf_op jit(solution)/shard_map/ppermute | solution.py:335
  9.4 0.0 collective-permute-start.8
  9.4 0.4 collective-permute-start.7
  9.8 2.6 %collective-permute-done.9 = bf16[32,1664]{1,0:T(8,128)(2,1)S(1)} collective-permute-done((bf16[32,1664]{1,0:T(8,128)(2,1)}, bf16[32,1664]{1,0:T(8,128)(2,1)S(1)}, u32[]{:S(2)}, u32[]{:S(2)}) %collective-permute-start.9) | collective-permute-done | bytes 106528 | tf_op jit(solution)/shard_map/ppermute | solution.py:335
  12.4 5.8 %collective-permute-done.8 = bf16[32,1664]{1,0:T(8,128)(2,1)S(1)} collective-permute-done((bf16[32,1664]{1,0:T(8,128)(2,1)}, bf16[32,1664]{1,0:T(8,128)(2,1)S(1)}, u32[]{:S(2)}, u32[]{:S(2)}) %collective-permute-start.8) | collective-permute-done | bytes 106528 | tf_op jit(solution)/shard_map/ppermute | solution.py:335
  18.2 0.0 collective-permute-done.7
  18.2 0.1 fusion
  18.3 1.3 %collective-permute-start.11 = (bf16[3,32,1664]{2,1,0:T(8,128)(2,1)S(1)}, bf16[3,32,1664]{2,1,0:T(8,128)(2,1)S(1)}, u32[]{:S(2)}, u32[]{:S(2)}) collective-permute-start(bf16[3,32,1664]{2,1,0:T(8,128)(2,1)S(1)} %get-tuple-element.42), channel_id=1, source_target_pairs={{0,16},{4,20},{8,24},{12,28},{16,0},{20,4},{24,8},{28,12},{1,17},{... | collective-permute-start | bytes 958472 | tf_op jit(solution)/shard_map/ppermute | solution.py:332
  19.6 1.2 %collective-permute-start.10 = (bf16[3,32,1664]{2,1,0:T(8,128)(2,1)S(1)}, bf16[3,32,1664]{2,1,0:T(8,128)(2,1)S(1)}, u32[]{:S(2)}, u32[]{:S(2)}) collective-permute-start(bf16[3,32,1664]{2,1,0:T(8,128)(2,1)S(1)} %get-tuple-element.42), channel_id=1, source_target_pairs={{0,8},{4,12},{8,0},{12,4},{16,24},{20,28},{24,16},{28,20},{1,9},{5... | collective-permute-start | bytes 958472 | tf_op jit(solution)/shard_map/ppermute | solution.py:332
  20.8 0.2 collective-permute-start.12
  21.0 5.1 %collective-permute-done.11 = bf16[3,32,1664]{2,1,0:T(8,128)(2,1)S(1)} collective-permute-done((bf16[3,32,1664]{2,1,0:T(8,128)(2,1)S(1)}, bf16[3,32,1664]{2,1,0:T(8,128)(2,1)S(1)}, u32[]{:S(2)}, u32[]{:S(2)}) %collective-permute-start.11) | collective-permute-done | bytes 319520 | tf_op jit(solution)/shard_map/ppermute | solution.py:332
  26.1 1.0 %collective-permute-done.10 = bf16[3,32,1664]{2,1,0:T(8,128)(2,1)S(1)} collective-permute-done((bf16[3,32,1664]{2,1,0:T(8,128)(2,1)S(1)}, bf16[3,32,1664]{2,1,0:T(8,128)(2,1)S(1)}, u32[]{:S(2)}, u32[]{:S(2)}) %collective-permute-start.10) | collective-permute-done | bytes 319520 | tf_op jit(solution)/shard_map/ppermute | solution.py:332
  27.1 6.8 %collective-permute-done.12 = bf16[3,32,1664]{2,1,0:T(8,128)(2,1)S(1)} collective-permute-done((bf16[3,32,1664]{2,1,0:T(8,128)(2,1)S(1)}, bf16[3,32,1664]{2,1,0:T(8,128)(2,1)S(1)}, u32[]{:S(2)}, u32[]{:S(2)}) %collective-permute-start.12) | collective-permute-done | bytes 319520 | tf_op jit(solution)/shard_map/ppermute | solution.py:332
  33.9 0.2 pad_maximum_fusion.refs_6_
  34.1 2.5 %collective-permute-start.13 = (bf16[4,3,32,1664]{3,2,1,0:T(8,128)(2,1)S(1)}, bf16[4,3,32,1664]{3,2,1,0:T(8,128)(2,1)S(1)}, u32[]{:S(2)}, u32[]{:S(2)}) collective-permute-start(bf16[4,3,32,1664]{3,2,1,0:T(8,128)(2,1)S(1)} %pad_maximum_fusion.refs_6_), channel_id=1, source_target_pairs={{0,4},{4,0},{8,12},{12,8},{16,20},{20,16},{24,28},{28,24},{1,5},{5... | collective-permute-start | bytes 3833864 | tf_op jit(solution)/shard_map/ppermute | solution.py:332
  36.6 0.1 copy.11
  36.7 0.1 copy.12
  36.9 0.1 pad_maximum_fusion.3.refs_0_
  37.0 2.1 %collective-permute-start.2 = (bf16[256,128]{1,0:T(8,128)(2,1)S(1)}, bf16[256,128]{1,0:T(8,128)(2,1)S(1)}, u32[]{:S(2)}, u32[]{:S(2)}) collective-permute-start(bf16[256,128]{1,0:T(8,128)(2,1)S(1)} %pad_maximum_fusion.3.refs_0_), channel_id=1, source_target_pairs={{0,3},{1,2},{2,1},{3,0},{4,7},{5,6},{6,5},{7,4},{8,11},{9,10},{10,... | collective-permute-start | bytes 196616 | tf_op jit(solution)/shard_map/ppermute | solution.py:335
  39.1 0.0 collective-permute-start.1
  39.1 1.5 %collective-permute-start = (bf16[256,128]{1,0:T(8,128)(2,1)S(1)}, bf16[256,128]{1,0:T(8,128)(2,1)S(1)}, u32[]{:S(2)}, u32[]{:S(2)}) collective-permute-start(bf16[256,128]{1,0:T(8,128)(2,1)S(1)} %pad_maximum_fusion.3.refs_0_), channel_id=1, source_target_pairs={{0,1},{1,0},{2,3},{3,2},{4,5},{5,4},{6,7},{7,6},{8,9},{9,8},{10,11... | collective-permute-start | bytes 196616 | tf_op jit(solution)/shard_map/ppermute | solution.py:335
  40.6 2.0 %collective-permute-start.5 = (bf16[256,128]{1,0:T(8,128)(2,1)S(1)}, bf16[256,128]{1,0:T(8,128)(2,1)S(1)}, u32[]{:S(2)}, u32[]{:S(2)}) collective-permute-start(bf16[256,128]{1,0:T(8,128)(2,1)S(1)} %copy-done.4), channel_id=1, source_target_pairs={{0,3},{1,2},{2,1},{3,0},{4,7},{5,6},{6,5},{7,4},{8,11},{9,10},{10,... | collective-permute-start | bytes 196616 | tf_op jit(solution)/shard_map/ppermute | solution.py:335
  42.6 0.0 collective-permute-done.2.refs_3_
  42.6 0.0 collective-permute-start.4
  42.6 4.0 %collective-permute-done.1.refs_2_ = bf16[256,128]{1,0:T(8,128)(2,1)S(1)} collective-permute-done((bf16[256,128]{1,0:T(8,128)(2,1)S(1)}, bf16[256,128]{1,0:T(8,128)(2,1)S(1)}, u32[]{:S(2)}, u32[]{:S(2)}) %collective-permute-start.1) | collective-permute-done | bytes 65568 | tf_op jit(solution)/shard_map/ppermute | solution.py:335
  46.6 0.0 collective-permute-start.3
  46.6 0.0 collective-permute-done.refs_1_
  46.6 0.1 pad_maximum_fusion.2
  46.7 4.5 %collective-permute-start.6 = (bf16[4,256,128]{2,1,0:T(8,128)(2,1)S(1)}, bf16[4,256,128]{2,1,0:T(8,128)(2,1)S(1)}, u32[]{:S(2)}, u32[]{:S(2)}) collective-permute-start(bf16[4,256,128]{2,1,0:T(8,128)(2,1)S(1)} %pad_maximum_fusion.2), channel_id=1, source_target_pairs={{4,0},{5,1},{6,2},{7,3},{8,4},{9,5},{10,6},{11,7},{12,8},{13,9},{1... | collective-permute-start | bytes 786440 | tf_op jit(solution)/shard_map/ppermute | solution.py:329
  51.3 3.2 %attend_own.2 = (bf16[512,384]{1,0:T(8,128)(2,1)S(1)}, bf16[1024,128]{1,0:T(8,128)(2,1)S(1)}, bf16[256,128]{1,0:T(8,128)(2,1)S(1)}, bf16[1024,256]{1,0:T(8,128)(2,1)S(1)}, f32[8,1024]{1,0:T(8,128)S(1)}) custom-call(s32[15]{0:T(128)S(1)} %copy-done.1, bf16[256,128]{1,0:T(8,128)(2,1)S(1)} %pad_maximum_fusion.3.refs_0_, ...), custom_call_target="tpu_custom_call" | custom-call | flops 1073741824 | bytes 262144 | tf_op jit(solution)/shard_map/attend_own/pallas_call | solution.py:388
  54.5 0.0 collective-permute-done.4.refs_1_
  54.5 0.0 collective-permute-done.3.refs_0_
  54.5 4.9 %attend_rest.2.refs_1_ = bf16[512,768]{1,0:T(8,128)(2,1)S(1)} custom-call(bf16[64,256]{1,0:T(8,128)(2,1)S(1)} %copy-done.5, bf16[1024,128]{1,0:T(8,128)(2,1)S(1)} %get-tuple-element.26.right_ref, bf16[256,128]{1,0:T(8,128)(2,1)S(1)} %get-tuple-element.27.mine_ref, bf16[1024,256]{1,0:T(8,128)(2,1)S(1)} %get-tuple-element.28.ext_ref, ...), custom_call_target="tpu_custom_call" | custom-call | flops 3221225472 | bytes 786432 | tf_op jit(solution)/shard_map/attend_rest/pallas_call | solution.py:411
  59.4 0.0 collective-permute-done.6.refs_6_
  59.4 3.2 %attend_own.3 = (bf16[512,384]{1,0:T(8,128)(2,1)S(1)}, bf16[1024,128]{1,0:T(8,128)(2,1)S(1)}, bf16[256,128]{1,0:T(8,128)(2,1)S(1)}, bf16[1024,256]{1,0:T(8,128)(2,1)S(1)}, f32[8,1024]{1,0:T(8,128)S(1)}) custom-call(s32[15]{0:T(128)S(1)} %copy-done.1, bf16[256,128]{1,0:T(8,128)(2,1)S(1)} %pad_maximum_fusion.3.refs_0_, ...), custom_call_target="tpu_custom_call" | custom-call | flops 1073741824 | bytes 262144 | tf_op jit(solution)/shard_map/attend_own/pallas_call | solution.py:388
  62.6 5.1 %attend_rest.3.refs_3_ = bf16[512,768]{1,0:T(8,128)(2,1)S(1)} custom-call(bf16[64,256]{1,0:T(8,128)(2,1)S(1)} %copy-done.5, bf16[1024,128]{1,0:T(8,128)(2,1)S(1)} %get-tuple-element.31.right_ref, bf16[256,128]{1,0:T(8,128)(2,1)S(1)} %get-tuple-element.32.mine_ref, bf16[1024,256]{1,0:T(8,128)(2,1)S(1)} %get-tuple-element.33.ext_ref, ...), custom_call_target="tpu_custom_call" | custom-call | flops 3221225472 | bytes 786432 | tf_op jit(solution)/shard_map/attend_rest/pallas_call | solution.py:411
  67.7 0.0 collective-permute-done.13.refs_7_
  67.8 5.8 %finish.1 = (f32[2,256,128]{2,1,0:T(8,128)S(1)}, bf16[128,128]{1,0:T(8,128)(2,1)S(1)}, bf16[128,128]{1,0:T(8,128)(2,1)S(1)}) custom-call(s32[15]{0:T(128)S(1)} %copy-done.1, bf16[512,384]{1,0:T(8,128)(2,1)S(1)} %get-tuple-element.25.refs_0_, bf16[512,768]{1,0:T(8,128)(2,1)S(1)} %attend_rest.2.refs_1_, bf16[512,384]{1,0:T(8,128)(2,1)S(1)} %get-tuple-element.30.refs_2_, ...), custom_call_target="tpu_custom_call" | custom-call | flops 3221225472 | bytes 3145728 | tf_op jit(solution)/shard_map/finish/pallas_call | solution.py:429
  73.6 1.3 %collective-permute-start.15 = (bf16[128,128]{1,0:T(8,128)(2,1)S(1)}, bf16[128,128]{1,0:T(8,128)(2,1)S(1)}, u32[]{:S(2)}, u32[]{:S(2)}) collective-permute-start(bf16[128,128]{1,0:T(8,128)(2,1)S(1)} %get-tuple-element.39), channel_id=1, source_target_pairs={{3,4},{7,8},{11,12},{15,16},{19,20},{23,24},{27,28}} | collective-permute-start | bytes 98312 | tf_op jit(solution)/shard_map/ppermute | solution.py:329
  74.9 1.3 %collective-permute-start.14 = (bf16[128,128]{1,0:T(8,128)(2,1)S(1)}, bf16[128,128]{1,0:T(8,128)(2,1)S(1)}, u32[]{:S(2)}, u32[]{:S(2)}) collective-permute-start(bf16[128,128]{1,0:T(8,128)(2,1)S(1)} %get-tuple-element.39), channel_id=1, source_target_pairs={{2,4},{3,5},{6,8},{7,9},{10,12},{11,13},{14,16},{15,17},{18,20},{1... | collective-permute-start | bytes 98312 | tf_op jit(solution)/shard_map/ppermute | solution.py:329
  76.2 1.3 %collective-permute-start.17 = (bf16[128,128]{1,0:T(8,128)(2,1)S(1)}, bf16[128,128]{1,0:T(8,128)(2,1)S(1)}, u32[]{:S(2)}, u32[]{:S(2)}) collective-permute-start(bf16[128,128]{1,0:T(8,128)(2,1)S(1)} %get-tuple-element.40), channel_id=1, source_target_pairs={{3,0},{7,4},{11,8},{15,12},{19,16},{23,20},{27,24},{31,28}} | collective-permute-start | bytes 98312 | tf_op jit(solution)/shard_map/ppermute | solution.py:329
  77.5 1.3 %collective-permute-start.16 = (bf16[128,128]{1,0:T(8,128)(2,1)S(1)}, bf16[128,128]{1,0:T(8,128)(2,1)S(1)}, u32[]{:S(2)}, u32[]{:S(2)}) collective-permute-start(bf16[128,128]{1,0:T(8,128)(2,1)S(1)} %get-tuple-element.40), channel_id=1, source_target_pairs={{2,0},{3,1},{6,4},{7,5},{10,8},{11,9},{14,12},{15,13},{18,16},{19,... | collective-permute-start | bytes 98312 | tf_op jit(solution)/shard_map/ppermute | solution.py:329
  78.8 1.9 %collective-permute-done.15.refs_1_ = bf16[128,128]{1,0:T(8,128)(2,1)S(1)} collective-permute-done((bf16[128,128]{1,0:T(8,128)(2,1)S(1)}, bf16[128,128]{1,0:T(8,128)(2,1)S(1)}, u32[]{:S(2)}, u32[]{:S(2)}) %collective-permute-start.15) | collective-permute-done | bytes 32800 | tf_op jit(solution)/shard_map/ppermute | solution.py:329
  80.7 1.0 %collective-permute-done.14.refs_0_ = bf16[128,128]{1,0:T(8,128)(2,1)S(1)} collective-permute-done((bf16[128,128]{1,0:T(8,128)(2,1)S(1)}, bf16[128,128]{1,0:T(8,128)(2,1)S(1)}, u32[]{:S(2)}, u32[]{:S(2)}) %collective-permute-start.14) | collective-permute-done | bytes 32800 | tf_op jit(solution)/shard_map/ppermute | solution.py:329
  81.7 2.0 %collective-permute-done.17.refs_3_ = bf16[128,128]{1,0:T(8,128)(2,1)S(1)} collective-permute-done((bf16[128,128]{1,0:T(8,128)(2,1)S(1)}, bf16[128,128]{1,0:T(8,128)(2,1)S(1)}, u32[]{:S(2)}, u32[]{:S(2)}) %collective-permute-start.17) | collective-permute-done | bytes 32800 | tf_op jit(solution)/shard_map/ppermute | solution.py:329
  83.7 0.4 collective-permute-done.16.refs_2_
  84.1 1.5 %combine.1 = f32[2,64,256]{2,1,0:T(8,128)} custom-call(s32[15]{0:T(128)S(1)} %copy-done.1, f32[2,64,256]{2,1,0:T(8,128)S(1)} %bitcast.16, f32[2,256,128]{2,1,0:T(8,128)S(1)} %get-tuple-element.38.rows_ref, bf16[128,128]{1,0:T(8,128)(2,1)S(1)} %collective-permute-done.14.refs_0_, bf16[128,128]{1,0:T(8,128)(2,1)S(1)} %collective-permute-done.15.refs_1_, ...), custom_call_target="tpu_custom_call" | custom-call | tf_op jit(solution)/shard_map/combine/pallas_call | solution.py:453
  (14 shorter events, 0.0 us)
Async XLA Ops:
  5.2 7.1 %collective-permute-start.9 = (bf16[32,1664]{1,0:T(8,128)(2,1)}, bf16[32,1664]{1,0:T(8,128)(2,1)S(1)}, u32[]{:S(2)}, u32[]{:S(2)}) collective-permute-start(bf16[32,1664]{1,0:T(8,128)(2,1)} %get-tuple-element.37), channel_id=1, source_target_pairs={{0,3},{1,2},{2,1},{3,0},{4,7},{5,6},{6,5},{7,4},{8,11},{9,10},{10,... | collective-permute-start | bytes 319496 | tf_op jit(solution)/shard_map/ppermute | solution.py:335
  9.4 8.8 %collective-permute-start.8 = (bf16[32,1664]{1,0:T(8,128)(2,1)}, bf16[32,1664]{1,0:T(8,128)(2,1)S(1)}, u32[]{:S(2)}, u32[]{:S(2)}) collective-permute-start(bf16[32,1664]{1,0:T(8,128)(2,1)} %get-tuple-element.37), channel_id=1, source_target_pairs={{0,2},{1,3},{2,0},{3,1},{4,6},{5,7},{6,4},{7,5},{8,10},{9,11},{10,... | collective-permute-start | bytes 319496 | tf_op jit(solution)/shard_map/ppermute | solution.py:335
  9.4 8.8 %collective-permute-start.7 = (bf16[32,1664]{1,0:T(8,128)(2,1)}, bf16[32,1664]{1,0:T(8,128)(2,1)S(1)}, u32[]{:S(2)}, u32[]{:S(2)}) collective-permute-start(bf16[32,1664]{1,0:T(8,128)(2,1)} %get-tuple-element.37), channel_id=1, source_target_pairs={{0,1},{1,0},{2,3},{3,2},{4,5},{5,4},{6,7},{7,6},{8,9},{9,8},{10,11... | collective-permute-start | bytes 319496 | tf_op jit(solution)/shard_map/ppermute | solution.py:335
  18.3 7.8 %collective-permute-start.11 = (bf16[3,32,1664]{2,1,0:T(8,128)(2,1)S(1)}, bf16[3,32,1664]{2,1,0:T(8,128)(2,1)S(1)}, u32[]{:S(2)}, u32[]{:S(2)}) collective-permute-start(bf16[3,32,1664]{2,1,0:T(8,128)(2,1)S(1)} %get-tuple-element.42), channel_id=1, source_target_pairs={{0,16},{4,20},{8,24},{12,28},{16,0},{20,4},{24,8},{28,12},{1,17},{... | collective-permute-start | bytes 958472 | tf_op jit(solution)/shard_map/ppermute | solution.py:332
  19.6 7.5 %collective-permute-start.10 = (bf16[3,32,1664]{2,1,0:T(8,128)(2,1)S(1)}, bf16[3,32,1664]{2,1,0:T(8,128)(2,1)S(1)}, u32[]{:S(2)}, u32[]{:S(2)}) collective-permute-start(bf16[3,32,1664]{2,1,0:T(8,128)(2,1)S(1)} %get-tuple-element.42), channel_id=1, source_target_pairs={{0,8},{4,12},{8,0},{12,4},{16,24},{20,28},{24,16},{28,20},{1,9},{5... | collective-permute-start | bytes 958472 | tf_op jit(solution)/shard_map/ppermute | solution.py:332
  20.8 13.0 %collective-permute-start.12 = (bf16[3,32,1664]{2,1,0:T(8,128)(2,1)S(1)}, bf16[3,32,1664]{2,1,0:T(8,128)(2,1)S(1)}, u32[]{:S(2)}, u32[]{:S(2)}) collective-permute-start(bf16[3,32,1664]{2,1,0:T(8,128)(2,1)S(1)} %get-tuple-element.42), channel_id=1, source_target_pairs={{0,24},{4,28},{8,16},{12,20},{16,8},{20,12},{24,0},{28,4},{1,25},{... | collective-permute-start | bytes 958472 | tf_op jit(solution)/shard_map/ppermute | solution.py:332
  33.8 2.8 %copy-start = (f32[2,256,64]{1,2,0:T(8,128)S(1)}, f32[2,256,64]{1,2,0:T(8,128)}, u32[]{:S(2)}) copy-start(f32[2,256,64]{1,2,0:T(8,128)} %param.8) | copy-start | bytes 393220
  33.8 6.7 %copy-start.4 = (bf16[256,128]{1,0:T(8,128)(2,1)S(1)}, bf16[256,128]{1,0:T(8,128)(2,1)}, u32[]{:S(2)}) copy-start(bf16[256,128]{1,0:T(8,128)(2,1)} %get-tuple-element.23.refs_4_) | copy-start | bytes 196612
  33.8 17.4 %copy-start.1 = (s32[15]{0:T(128)S(1)}, s32[15]{0:T(128)}, u32[]{:S(2)}) copy-start(s32[15]{0:T(128)} %margin_ref.7) | copy-start | bytes 184
  33.9 17.4 %copy-start.5 = (bf16[64,256]{1,0:T(8,128)(2,1)S(1)}, bf16[64,256]{1,0:T(8,128)(2,1)}, u32[]{:S(2)}) copy-start(bf16[64,256]{1,0:T(8,128)(2,1)} %get-tuple-element.24.refs_5_.gram_ref) | copy-start | bytes 98308
  34.1 33.7 %collective-permute-start.13 = (bf16[4,3,32,1664]{3,2,1,0:T(8,128)(2,1)S(1)}, bf16[4,3,32,1664]{3,2,1,0:T(8,128)(2,1)S(1)}, u32[]{:S(2)}, u32[]{:S(2)}) collective-permute-start(bf16[4,3,32,1664]{3,2,1,0:T(8,128)(2,1)S(1)} %pad_maximum_fusion.refs_6_), channel_id=1, source_target_pairs={{0,4},{4,0},{8,12},{12,8},{16,20},{20,16},{24,28},{28,24},{1,5},{5... | collective-permute-start | bytes 3833864 | tf_op jit(solution)/shard_map/ppermute | solution.py:332
  37.0 5.6 %collective-permute-start.2 = (bf16[256,128]{1,0:T(8,128)(2,1)S(1)}, bf16[256,128]{1,0:T(8,128)(2,1)S(1)}, u32[]{:S(2)}, u32[]{:S(2)}) collective-permute-start(bf16[256,128]{1,0:T(8,128)(2,1)S(1)} %pad_maximum_fusion.3.refs_0_), channel_id=1, source_target_pairs={{0,3},{1,2},{2,1},{3,0},{4,7},{5,6},{6,5},{7,4},{8,11},{9,10},{10,... | collective-permute-start | bytes 196616 | tf_op jit(solution)/shard_map/ppermute | solution.py:335
  39.1 7.6 %collective-permute-start.1 = (bf16[256,128]{1,0:T(8,128)(2,1)S(1)}, bf16[256,128]{1,0:T(8,128)(2,1)S(1)}, u32[]{:S(2)}, u32[]{:S(2)}) collective-permute-start(bf16[256,128]{1,0:T(8,128)(2,1)S(1)} %pad_maximum_fusion.3.refs_0_), channel_id=1, source_target_pairs={{0,2},{1,3},{2,0},{3,1},{4,6},{5,7},{6,4},{7,5},{8,10},{9,11},{10,... | collective-permute-start | bytes 196616 | tf_op jit(solution)/shard_map/ppermute | solution.py:335
  39.1 7.6 %collective-permute-start = (bf16[256,128]{1,0:T(8,128)(2,1)S(1)}, bf16[256,128]{1,0:T(8,128)(2,1)S(1)}, u32[]{:S(2)}, u32[]{:S(2)}) collective-permute-start(bf16[256,128]{1,0:T(8,128)(2,1)S(1)} %pad_maximum_fusion.3.refs_0_), channel_id=1, source_target_pairs={{0,1},{1,0},{2,3},{3,2},{4,5},{5,4},{6,7},{7,6},{8,9},{9,8},{10,11... | collective-permute-start | bytes 196616 | tf_op jit(solution)/shard_map/ppermute | solution.py:335
  40.6 13.9 %collective-permute-start.5 = (bf16[256,128]{1,0:T(8,128)(2,1)S(1)}, bf16[256,128]{1,0:T(8,128)(2,1)S(1)}, u32[]{:S(2)}, u32[]{:S(2)}) collective-permute-start(bf16[256,128]{1,0:T(8,128)(2,1)S(1)} %copy-done.4), channel_id=1, source_target_pairs={{0,3},{1,2},{2,1},{3,0},{4,7},{5,6},{6,5},{7,4},{8,11},{9,10},{10,... | collective-permute-start | bytes 196616 | tf_op jit(solution)/shard_map/ppermute | solution.py:335
  42.6 11.9 %collective-permute-start.4 = (bf16[256,128]{1,0:T(8,128)(2,1)S(1)}, bf16[256,128]{1,0:T(8,128)(2,1)S(1)}, u32[]{:S(2)}, u32[]{:S(2)}) collective-permute-start(bf16[256,128]{1,0:T(8,128)(2,1)S(1)} %copy-done.4), channel_id=1, source_target_pairs={{0,2},{1,3},{2,0},{3,1},{4,6},{5,7},{6,4},{7,5},{8,10},{9,11},{10,... | collective-permute-start | bytes 196616 | tf_op jit(solution)/shard_map/ppermute | solution.py:335
  46.6 7.9 %collective-permute-start.3 = (bf16[256,128]{1,0:T(8,128)(2,1)S(1)}, bf16[256,128]{1,0:T(8,128)(2,1)S(1)}, u32[]{:S(2)}, u32[]{:S(2)}) collective-permute-start(bf16[256,128]{1,0:T(8,128)(2,1)S(1)} %copy-done.4), channel_id=1, source_target_pairs={{0,1},{1,0},{2,3},{3,2},{4,5},{5,4},{6,7},{7,6},{8,9},{9,8},{10,11... | collective-permute-start | bytes 196616 | tf_op jit(solution)/shard_map/ppermute | solution.py:335
  46.7 12.7 %collective-permute-start.6 = (bf16[4,256,128]{2,1,0:T(8,128)(2,1)S(1)}, bf16[4,256,128]{2,1,0:T(8,128)(2,1)S(1)}, u32[]{:S(2)}, u32[]{:S(2)}) collective-permute-start(bf16[4,256,128]{2,1,0:T(8,128)(2,1)S(1)} %pad_maximum_fusion.2), channel_id=1, source_target_pairs={{4,0},{5,1},{6,2},{7,3},{8,4},{9,5},{10,6},{11,7},{12,8},{13,9},{1... | collective-permute-start | bytes 786440 | tf_op jit(solution)/shard_map/ppermute | solution.py:329
  62.6 5.2 %copy-start.2 = (bf16[256,1664]{1,0:T(8,128)(2,1)S(1)}, bf16[256,1664]{1,0:T(8,128)(2,1)}, u32[]{:S(2)}) copy-start(bf16[256,1664]{1,0:T(8,128)(2,1)} %get-tuple-element.36.refs_5_) | copy-start | bytes 2555908
  62.6 5.2 %copy-start.3 = (bf16[128,1664]{1,0:T(8,128)(2,1)S(1)}, bf16[128,1664]{1,0:T(8,128)(2,1)}, u32[]{:S(2)}) copy-start(bf16[128,1664]{1,0:T(8,128)(2,1)} %get-tuple-element.35.refs_4_) | copy-start | bytes 1277956
  73.6 7.1 %collective-permute-start.15 = (bf16[128,128]{1,0:T(8,128)(2,1)S(1)}, bf16[128,128]{1,0:T(8,128)(2,1)S(1)}, u32[]{:S(2)}, u32[]{:S(2)}) collective-permute-start(bf16[128,128]{1,0:T(8,128)(2,1)S(1)} %get-tuple-element.39), channel_id=1, source_target_pairs={{3,4},{7,8},{11,12},{15,16},{19,20},{23,24},{27,28}} | collective-permute-start | bytes 98312 | tf_op jit(solution)/shard_map/ppermute | solution.py:329
  74.9 6.8 %collective-permute-start.14 = (bf16[128,128]{1,0:T(8,128)(2,1)S(1)}, bf16[128,128]{1,0:T(8,128)(2,1)S(1)}, u32[]{:S(2)}, u32[]{:S(2)}) collective-permute-start(bf16[128,128]{1,0:T(8,128)(2,1)S(1)} %get-tuple-element.39), channel_id=1, source_target_pairs={{2,4},{3,5},{6,8},{7,9},{10,12},{11,13},{14,16},{15,17},{18,20},{1... | collective-permute-start | bytes 98312 | tf_op jit(solution)/shard_map/ppermute | solution.py:329
  76.2 7.5 %collective-permute-start.17 = (bf16[128,128]{1,0:T(8,128)(2,1)S(1)}, bf16[128,128]{1,0:T(8,128)(2,1)S(1)}, u32[]{:S(2)}, u32[]{:S(2)}) collective-permute-start(bf16[128,128]{1,0:T(8,128)(2,1)S(1)} %get-tuple-element.40), channel_id=1, source_target_pairs={{3,0},{7,4},{11,8},{15,12},{19,16},{23,20},{27,24},{31,28}} | collective-permute-start | bytes 98312 | tf_op jit(solution)/shard_map/ppermute | solution.py:329
  77.5 6.6 %collective-permute-start.16 = (bf16[128,128]{1,0:T(8,128)(2,1)S(1)}, bf16[128,128]{1,0:T(8,128)(2,1)S(1)}, u32[]{:S(2)}, u32[]{:S(2)}) collective-permute-start(bf16[128,128]{1,0:T(8,128)(2,1)S(1)} %get-tuple-element.40), channel_id=1, source_target_pairs={{2,0},{3,1},{6,4},{7,5},{10,8},{11,9},{14,12},{15,13},{18,16},{19,... | collective-permute-start | bytes 98312 | tf_op jit(solution)/shard_map/ppermute | solution.py:329
